TPU v7x, 128 devices: a whole 4x4x4 slice. The times are simulated.
128 devices in a mesh: kv: 4 (over y), blk: 32 (over z, x, core).
Axes of the slice: x: 4, y: 4, z: 4, core: 2. Of those that a mesh axis runs over, the one named last changes fastest.
Arguments:
- queries: bfloat16 [128, 4096], P('blk', 'kv'), may hold values from -120 to 120
- cache_keys: bfloat16 [128, 4096, 4, 128], P('blk', None, 'kv'), may hold values from -5 to 5
- cache_values: bfloat16 [128, 4096, 4, 128], P('blk', None, 'kv'), may hold values from -6 to 6
- lengths: int32 [128], replicated, may hold values from 1 to 32768, as said below
- sinks: float32 [32], P('kv'), may hold values from 5 to 11
- out_proj: bfloat16 [4096, 2048], P('kv'), may hold values from -0.09375 to 0.09375
- decode_resid: bfloat16 [128, 2048], P(('blk', 'kv')), may hold values from -4 to 4
- prefill_hidden: bfloat16 [128, 111, 2048], P(('blk', 'kv')), may hold values from -6 to 6
- norm_gain: float32 [2048], replicated, may hold values from 0.1 to 1.9
- router: bfloat16 [2048, 128], replicated, may hold values from -80 to 80
- routes: int32 [128, 112, 8], P(('blk', 'kv')), may hold values from 0 to 127, all different within a row; in each aligned block of 112 rows (0 to 111, 112 to 223, ..., all dimensions but the last counted through in order) at most 14 rows name the same one
- expert_gate: bfloat16 [128, 2048, 768], P(('kv', 'blk')), may hold values from -0.125 to 0.125
- expert_up: bfloat16 [128, 2048, 768], P(('kv', 'blk')), may hold values from -0.125 to 0.125
- expert_down: bfloat16 [128, 768, 2048], P(('kv', 'blk')), may hold values from -0.21875 to 0.21875
Outputs:
- layer_out: bfloat16 [128, 112, 2048], P(('blk', 'kv'))
Inputs may be any that keep to these rules, and one draw needn't show every extreme that they name: `lengths`: at least one request has exactly 32768 cached positions. `routes`: within the rows of one device (112 rows, aligned blocks) no expert is named by more than 14 rows, and in every draw some expert reaches 14 in some block.
All inputs are finite; a program needn't handle non-finite values.
Results may differ from a plain program's by a relative error of at most 0.0094.
Values may be sent and summed in bfloat16 or wider, within the bound.
A program may use at most 128 MiB of HBM per device.

v0:
```python
import math

import jax
import jax.numpy as jnp
from jax import lax
from jax.experimental import pallas as pl
from jax.experimental.pallas import tpu as pltpu
from jax.sharding import PartitionSpec as P

NEG_FILL = -1e30
EPSILON = 1e-06
MESH = pl.DeviceIdType.MESH


def kv_reduce_kernel(n_kv, part_ref, out_ref, held, send_sem, recv_sem):
    me = lax.axis_index("kv")
    blk = lax.axis_index("blk")
    barrier = pltpu.get_barrier_semaphore()
    for step in range(1, n_kv):
        peer = lax.rem(me + step, n_kv)
        pl.semaphore_signal(barrier, inc=1, device_id=(peer, blk), device_id_type=MESH)
    pl.semaphore_wait(barrier, n_kv - 1)
    for step in range(1, n_kv):
        peer = lax.rem(me + step, n_kv)
        pltpu.make_async_remote_copy(
            src_ref=part_ref.at[peer],
            dst_ref=held.at[me],
            send_sem=send_sem.at[peer],
            recv_sem=recv_sem.at[me],
            device_id=(peer, blk),
            device_id_type=MESH,
        ).start()
    own = part_ref[me]
    for step in range(1, n_kv):
        peer = lax.rem(me + step, n_kv)
        arrival = pltpu.make_async_remote_copy(
            src_ref=part_ref.at[peer],
            dst_ref=held.at[peer],
            send_sem=send_sem.at[peer],
            recv_sem=recv_sem.at[peer],
            device_id=(peer, blk),
            device_id_type=MESH,
        )
        arrival.wait_send()
        arrival.wait_recv()
    total = own
    for step in range(1, n_kv):
        peer = lax.rem(me + step, n_kv)
        total = total + held[peer]
    out_ref[...] = total


def kv_reduce(partial, n_kv):
    rows, width = partial.shape
    return pl.pallas_call(
        lambda *refs: kv_reduce_kernel(n_kv, *refs),
        out_shape=jax.ShapeDtypeStruct((1, width), jnp.float32),
        in_specs=[pl.BlockSpec(memory_space=pltpu.VMEM)],
        out_specs=pl.BlockSpec(memory_space=pltpu.VMEM),
        scratch_shapes=[
            pltpu.VMEM((n_kv, 1, width), jnp.float32),
            pltpu.SemaphoreType.DMA((n_kv,)),
            pltpu.SemaphoreType.DMA((n_kv,)),
        ],
        compiler_params=pltpu.CompilerParams(collective_id=0, has_side_effects=True),
    )(partial.reshape(rows, 1, width))


def expert_block(slots, gate_weights, up_weights, down_weights):
    gate_act = jnp.dot(slots, gate_weights[0], preferred_element_type=jnp.float32)
    up_act = jnp.dot(slots, up_weights[0], preferred_element_type=jnp.float32)
    inner_act = (gate_act / (1.0 + jnp.exp(-gate_act)) * up_act).astype(jnp.bfloat16)
    result = jnp.dot(inner_act, down_weights[0], preferred_element_type=jnp.float32)
    return result.astype(jnp.bfloat16)


def body(
    queries,
    cache_keys,
    cache_values,
    lengths,
    sinks,
    out_proj,
    decode_resid,
    prefill_hidden,
    norm_gain,
    router,
    routes,
    expert_gate,
    expert_up,
    expert_down,
):
    n_kv = lax.axis_size("kv")
    my_block = lax.axis_index("blk")
    per_block = queries.shape[0]
    head_count = sinks.shape[0]
    head_dim = cache_keys.shape[3]
    window = cache_keys.shape[1]
    grouped_q = queries.reshape(per_block, head_count, head_dim)
    key_rows = cache_keys[:, :, 0, :]
    value_rows = cache_values[:, :, 0, :]
    my_lengths = lax.dynamic_slice_in_dim(lengths, my_block * per_block, per_block)
    scores = jnp.einsum("rgd,rjd->rgj", grouped_q, key_rows, preferred_element_type=jnp.float32) * (
        1.0 / math.sqrt(head_dim)
    )
    first_valid = window - jnp.minimum(my_lengths, window)
    is_valid = (jnp.arange(window, dtype=jnp.int32)[None, :] >= first_valid[:, None])[:, None, :]
    masked = jnp.where(is_valid, scores, NEG_FILL)
    top_limit = jnp.maximum(jnp.max(masked, axis=2), sinks[None, :])
    weights = jnp.where(is_valid, jnp.exp(masked - top_limit[..., None]), 0.0)
    denominator = jnp.sum(weights, axis=2) + jnp.exp(sinks[None, :] - top_limit)
    numerator = jnp.einsum(
        "rgj,rjd->rgd", weights.astype(jnp.bfloat16), value_rows, preferred_element_type=jnp.float32
    )
    attended = (
        (numerator / denominator[..., None])
        .astype(jnp.bfloat16)
        .reshape(per_block, head_count * head_dim)
    )
    partial_proj = jnp.dot(attended, out_proj, preferred_element_type=jnp.float32)
    projected = kv_reduce(partial_proj, n_kv)
    decoded = (decode_resid.astype(jnp.float32) + projected).astype(jnp.bfloat16)
    hidden = jnp.concatenate([decoded, prefill_hidden[0]], axis=0)
    hidden_f = hidden.astype(jnp.float32)
    mean_sq = jnp.mean(hidden_f * hidden_f, axis=1, keepdims=True)
    normed = (hidden_f * lax.rsqrt(mean_sq + EPSILON) * norm_gain).astype(jnp.bfloat16)

    experts = router.shape[1]
    chosen_ids = routes[0]
    tokens, top_k = chosen_ids.shape
    model_width = hidden.shape[1]
    capacity = 16
    logits = jnp.dot(normed, router, preferred_element_type=jnp.float32)
    one_hot = chosen_ids[..., None] == jnp.arange(experts, dtype=jnp.int32)
    chosen = jnp.sum(jnp.where(one_hot, logits[:, None, :], 0.0), axis=2)
    gate_probs = jax.nn.softmax(chosen, axis=1)
    row_hot = jnp.any(one_hot, axis=1).astype(jnp.int32)
    earlier = jnp.cumsum(row_hot, axis=0) - row_hot
    slot_rank = jnp.sum(jnp.where(one_hot, earlier[:, None, :], 0), axis=2)
    rank_hot = slot_rank[..., None] == jnp.arange(capacity, dtype=jnp.int32)
    fills = one_hot[..., None] & rank_hot[:, :, None, :]
    place = jnp.any(fills, axis=1).reshape(tokens, experts * capacity).astype(jnp.bfloat16)
    outgoing = jnp.einsum("ts,td->sd", place, normed, preferred_element_type=jnp.float32)
    outgoing = outgoing.astype(jnp.bfloat16).reshape(experts, capacity, model_width)
    arrived = lax.all_to_all(outgoing, ("kv", "blk"), split_axis=0, concat_axis=0, tiled=True)
    processed = expert_block(
        arrived.reshape(experts * capacity, model_width), expert_gate, expert_up, expert_down
    )
    returned = lax.all_to_all(
        processed.reshape(experts, capacity, model_width),
        ("kv", "blk"),
        split_axis=0,
        concat_axis=0,
        tiled=True,
    ).reshape(experts * capacity, model_width)
    mix = jnp.sum(jnp.where(fills, gate_probs[..., None, None], 0.0), axis=1)
    mix = mix.reshape(tokens, experts * capacity)
    mix_hi = mix.astype(jnp.bfloat16)
    mix_lo = (mix - mix_hi.astype(jnp.float32)).astype(jnp.bfloat16)
    both = jnp.dot(
        jnp.concatenate([mix_hi, mix_lo], axis=0), returned, preferred_element_type=jnp.float32
    )
    combined = both[:tokens] + both[tokens:]
    layer_sum = (hidden_f + combined).astype(jnp.bfloat16)
    return layer_sum[None]


def solution(mesh):
    return jax.shard_map(
        body,
        mesh=mesh,
        in_specs=(
            P("blk", "kv"),
            P("blk", None, "kv", None),
            P("blk", None, "kv", None),
            P(),
            P("kv"),
            P("kv", None),
            P(("blk", "kv"), None),
            P(("blk", "kv"), None, None),
            P(),
            P(),
            P(("blk", "kv"), None, None),
            P(("kv", "blk"), None, None),
            P(("kv", "blk"), None, None),
            P(("kv", "blk"), None, None),
        ),
        out_specs=P(("blk", "kv"), None, None),
        check_vma=False,
    )
```

profile of v0, /device:TPU:2, one launch (start us, length us, event | category | flops | bytes accessed | tf_op | source)
XLA Modules:
  0.0 287.0 jit_solution(15364005516779067585)
XLA Ops:
  0.0 0.0 copy-start
  0.0 0.9 minimum_subtract_fusion
  0.9 0.1 iota_compare_fusion.2
  1.0 0.0 copy-start.4
  1.0 3.9 %fusion.50 = (f32[4,8]{1,0:T(4,128)S(1)}, f32[4,8,4096]{2,1,0:T(8,128)S(1)}) fusion(bf16[4,4096,1,128]{3,1,2,0:T(8,128)(2,1)} %param.15, bf16[1,4,8,128]{3,1,2,0:T(4,128)(2,1)} %bitcast.65, pred[4,4096]{1,0:T(4,128)(4,1)S(1)} %iota_compare_fusion.2), kind=kOutput, calls=%fused_computation.66 | convolution fusion | flops 33947616 | bytes 4743296 | tf_op jit(solution)/shard_map/rgd,rjd->rgj/dot_general | solution.py:103
  4.9 0.0 copy-done.14
  4.9 0.3 fusion.30
  5.2 0.0 copy-done.3
  5.2 0.0 copy-start.11
  5.2 0.0 copy-start.13
  5.3 0.7 fusion.17
  6.0 0.0 copy-done.4
  6.0 0.0 copy-start.12
  6.0 0.7 fusion.40
  6.7 0.6 reshape.150.refs_0_
  7.3 7.6 %shard_map.136 = f32[1,2048]{1,0:T(1,128)} custom-call(f32[4,1,2048]{2,1,0:T(1,128)} %reshape.150.refs_0_), custom_call_target="tpu_custom_call" | custom-call | tf_op jit(solution)/shard_map/pallas_call | solution.py:55
  14.9 0.0 copy-done.11
  14.9 0.7 add_convert_fusion
  15.6 1.3 fusion.25
  16.9 0.0 copy-done.13
  16.9 0.1 copy.24
  17.1 0.3 iota_compare_fusion.1
  17.3 0.2 reduce_window_sum.11
  17.5 2.1 select_reduce_fusion.1
  19.6 0.2 iota_compare_fusion
  19.8 0.6 copy-done.7
  20.4 3.4 %and_reduce_fusion = pred[112,128,16]{1,2,0:T(8,128)(4,1)} fusion(pred[112,8,16]{2,1,0:T(8,128)(4,1)S(1)} %iota_compare_fusion, pred[112,8,128]{2,1,0:T(8,128)(4,1)S(1)} %get-tuple-element.7), kind=kLoop, calls=%fused_computation | loop fusion | flops 3440640 | bytes 358400 | tf_op jit(solution)/shard_map/reduce_or | solution.py:142
  23.9 1.6 copy.29
  25.5 3.4 %convolution_convert_fusion.1 = bf16[2048,2048]{1,0:T(8,128)(2,1)S(1)} fusion(pred[112,2048]{0,1:T(8,128)(4,1)S(1)} %bitcast.64, f32[2048]{0:T(1024)S(1)} %copy-done.12, f32[112]{0:T(128)S(1)} %add_rsqrt_fusion, bf16[111,2048]{1,0:T(8,128)(2,1)} %bitcast.61, bf16[1,2048]{1,0:T(2,128)(2,1)S(1)} %add_convert_fusion), kind=kOutput, calls=%fused_computation.3 | convolution fusion | flops 945324032 | bytes 9085376 | tf_op jit(solution)/shard_map/ts,td->sd/dot_general | solution.py:143
  29.0 0.0 copy-start.15
  29.0 107.0 %all_to_all.10 = bf16[128,16,2048]{2,1,0:T(8,128)(2,1)S(1)} all-to-all(bf16[128,16,2048]{2,1,0:T(8,128)(2,1)S(1)} %bitcast.56), channel_id=1, replica_groups=mesh['kv'=4,'blk'=32] {'kv','blk'}, dimensions={0} | all-to-all | bytes 16777216 | tf_op jit(solution)/shard_map/all_to_all | solution.py:145
  136.0 3.2 %copy-done.2 = bf16[128,16,2048]{2,1,0:T(8,128)(2,1)} copy-done((bf16[128,16,2048]{2,1,0:T(8,128)(2,1)}, bf16[128,16,2048]{2,1,0:T(8,128)(2,1)S(1)}, u32[]{:S(2)}) %copy-start.2) | copy-done | bytes 8388632
  139.2 8.6 %fusion.8 = f32[2048,768]{1,0:T(8,128)} fusion(bf16[2048,2048]{1,0:T(8,128)(2,1)S(1)} %bitcast.58, bf16[1,2048,768]{2,1,0:T(8,128)(2,1)S(1)} %copy-done.15), kind=kOutput, calls=%fused_computation.13 | convolution fusion | flops 6442450944 | bytes 17825792 | tf_op jit(solution)/shard_map/dot_general | solution.py:70
  147.7 21.3 %convolution_convert_fusion = bf16[2048,2048]{1,0:T(8,128)(2,1)} fusion(f32[2048,768]{1,0:T(8,128)} %fusion.8, bf16[2048,2048]{1,0:T(8,128)(2,1)} %bitcast.59, bf16[1,768,2048]{2,1,0:T(8,128)(2,1)S(1)} %copy-done, bf16[1,2048,768]{2,1,0:T(8,128)(2,1)} %param.26), kind=kOutput, calls=%fused_computation.2 | convolution fusion | flops 12896960512 | bytes 29360128 | tf_op jit(solution)/shard_map/dot_general | solution.py:73
  169.0 7.5 %all-to-all-start.1 = ((bf16[128,16,2048]{2,1,0:T(8,128)(2,1)}), bf16[128,16,2048]{2,1,0:T(8,128)(2,1)}, u32[]{:S(2)}, u32[]{:S(2)}) async-start(bf16[128,16,2048]{2,1,0:T(8,128)(2,1)} %bitcast.57), calls=%async_computation.1 | async-start | bytes 16777216 | tf_op jit(solution)/shard_map/all_to_all | solution.py:149
  176.5 0.0 copy-done.5
  176.6 0.0 copy-done.16
  176.6 0.4 fusion.38
  177.0 0.3 select_reduce_fusion
  177.3 0.1 copy.26
  177.3 0.1 reduce_max.19
  177.5 0.1 copy.27
  177.6 4.1 %fusion = f32[112,128,16]{1,2,0:T(8,128)S(1)} fusion(f32[112,8]{1,0:T(8,128)S(1)} %copy.27, pred[112,8,16]{2,1,0:T(8,128)(4,1)S(1)} %copy-done.8, pred[112,8,128]{2,1,0:T(8,128)(4,1)S(1)} %get-tuple-element.7), kind=kLoop, calls=%fused_computation.4 | loop fusion | flops 5275648 | bytes 1050112 | tf_op jit(solution)/shard_map/reduce_sum | solution.py:156
  181.8 0.7 copy.28
  182.5 1.1 fusion.24
  183.6 96.5 %all-to-all-done.1 = bf16[128,16,2048]{2,1,0:T(8,128)(2,1)} async-done(((bf16[128,16,2048]{2,1,0:T(8,128)(2,1)}), bf16[128,16,2048]{2,1,0:T(8,128)(2,1)}, u32[]{:S(2)}, u32[]{:S(2)}) %all-to-all-start.1) | async-done | bytes 8388640 | tf_op jit(solution)/shard_map/all_to_all | solution.py:149
  280.1 6.0 %fusion.20 = f32[224,2048]{1,0:T(8,128)S(1)} fusion(bf16[2048,2048]{1,0:T(8,128)(2,1)} %bitcast.12, bf16[112,2048]{0,1:T(8,128)(2,1)} %get-tuple-element.5, bf16[112,2048]{0,1:T(8,128)(2,1)} %get-tuple-element.6), kind=kOutput, calls=%fused_computation.22 | convolution fusion | flops 1880883200 | bytes 11141120 | tf_op jit(solution)/shard_map/dot_general | solution.py:160
  286.1 1.0 fusion.29
  (26 shorter events, 0.1 us)
Async XLA Ops:
  0.0 147.7 %copy-start = (bf16[1,768,2048]{2,1,0:T(8,128)(2,1)S(1)}, bf16[1,768,2048]{2,1,0:T(8,128)(2,1)}, u32[]{:S(2)}) copy-start(bf16[1,768,2048]{2,1,0:T(8,128)(2,1)} %param.27) | copy-start | bytes 9437188
  0.0 4.9 %copy-start.14 = (f32[8]{0:T(128)S(1)}, f32[8]{0:T(128)}, u32[]{:S(2)}) copy-start(f32[8]{0:T(128)} %param.18) | copy-start | bytes 100
  0.0 5.2 %copy-start.3 = (bf16[4,4096,1,128]{3,1,2,0:T(8,128)(2,1)S(1)}, bf16[4,4096,1,128]{3,1,2,0:T(8,128)(2,1)}, u32[]{:S(2)}) copy-start(bf16[4,4096,1,128]{3,1,2,0:T(8,128)(2,1)} %param.16) | copy-start | bytes 12582916
  1.0 5.0 %copy-start.4 = (bf16[1024,2048]{1,0:T(8,128)(2,1)S(1)}, bf16[1024,2048]{1,0:T(8,128)(2,1)}, u32[]{:S(2)}) copy-start(bf16[1024,2048]{1,0:T(8,128)(2,1)} %param.19) | copy-start | bytes 12582916
  5.2 9.7 %copy-start.11 = (bf16[1,2048]{1,0:T(2,128)(2,1)S(1)}, bf16[1,2048]{1,0:T(2,128)(2,1)}, u32[]{:S(2)}) copy-start(bf16[1,2048]{1,0:T(2,128)(2,1)} %param.20) | copy-start | bytes 12292
  5.2 11.7 %copy-start.13 = (s32[1,112,8]{1,2,0:T(8,128)S(1)}, s32[1,112,8]{1,2,0:T(8,128)}, u32[]{:S(2)}) copy-start(s32[1,112,8]{1,2,0:T(8,128)} %param.24) | copy-start | bytes 10756
  6.0 19.5 %copy-start.12 = (f32[2048]{0:T(1024)S(1)}, f32[2048]{0:T(1024)}, u32[]{:S(2)}) copy-start(f32[2048]{0:T(1024)} %param.22) | copy-start | bytes 24580
  17.0 2.8 copy-start.9
  19.8 0.6 copy-start.7
  29.0 110.2 %copy-start.15 = (bf16[1,2048,768]{2,1,0:T(8,128)(2,1)S(1)}, bf16[1,2048,768]{2,1,0:T(8,128)(2,1)}, u32[]{:S(2)}) copy-start(bf16[1,2048,768]{2,1,0:T(8,128)(2,1)} %param.25) | copy-start | bytes 9437188
  136.0 3.2 %copy-start.2 = (bf16[128,16,2048]{2,1,0:T(8,128)(2,1)}, bf16[128,16,2048]{2,1,0:T(8,128)(2,1)S(1)}, u32[]{:S(2)}) copy-start(bf16[128,16,2048]{2,1,0:T(8,128)(2,1)S(1)} %all_to_all.10) | copy-start | bytes 25165828
  169.0 7.5 %copy-start.5 = (bf16[1,111,2048]{2,1,0:T(8,128)(2,1)S(1)}, bf16[1,111,2048]{2,1,0:T(8,128)(2,1)}, u32[]{:S(2)}) copy-start(bf16[1,111,2048]{2,1,0:T(8,128)(2,1)} %param.21) | copy-start | bytes 1363972
  169.0 7.5 %copy-start.16 = (bf16[2048,128]{1,0:T(8,128)(2,1)S(1)}, bf16[2048,128]{1,0:T(8,128)(2,1)}, u32[]{:S(2)}) copy-start(bf16[2048,128]{1,0:T(8,128)(2,1)} %param.23) | copy-start | bytes 1572868
  169.0 7.9 %copy-start.10 = (s32[112,8]{1,0:T(8,128)S(1)}, s32[112,8]{1,0:T(8,128)}, u32[]{:S(2)}) copy-start(s32[112,8]{1,0:T(8,128)} %copy-done.9) | copy-start | bytes 10756
  169.0 8.6 %copy-start.8 = (pred[112,8,16]{2,1,0:T(8,128)(4,1)S(1)}, pred[112,8,16]{2,1,0:T(8,128)(4,1)}, u32[]{:S(2)}) copy-start(pred[112,8,16]{2,1,0:T(8,128)(4,1)} %copy-done.7) | copy-start | bytes 43012
  169.0 111.0 %all-to-all-start.1 = ((bf16[128,16,2048]{2,1,0:T(8,128)(2,1)}), bf16[128,16,2048]{2,1,0:T(8,128)(2,1)}, u32[]{:S(2)}, u32[]{:S(2)}) async-start(bf16[128,16,2048]{2,1,0:T(8,128)(2,1)} %bitcast.57), calls=%async_computation.1 | async-start | bytes 16777216 | tf_op jit(solution)/shard_map/all_to_all | solution.py:149
  280.1 6.0 %copy-start.6 = (bf16[1,111,2048]{2,1,0:T(8,128)(2,1)S(1)}, bf16[1,111,2048]{2,1,0:T(8,128)(2,1)}, u32[]{:S(2)}) copy-start(bf16[1,111,2048]{2,1,0:T(8,128)(2,1)} %param.21) | copy-start | bytes 1363972
  280.1 7.0 %copy-start.1 = (bf16[1,768,2048]{2,1,0:T(8,128)(2,1)S(1)}, bf16[1,768,2048]{2,1,0:T(8,128)(2,1)}, u32[]{:S(2)}) copy-start(bf16[1,768,2048]{2,1,0:T(8,128)(2,1)} %param.27) | copy-start | bytes 9437188
where the time goes:
time: 290 us; the launch traced here: 287 us
  blocking collectives  107 us (37%)
  waiting for transfers between devices  96.5 us (33%)
  matrix products  45 us (16%)
  other arithmetic  16.1 us (6%)
  Pallas kernels  7.62 us (3%)
  starting transfers between devices  7.51 us (3%)
  local copies, waits for them, and re-layouts  7.08 us (2%)
    all_to_all x1, blocking collectives, body(): lax.all_to_all(outgoing, ('kv', 'blk'), split_axis=0, concat_axis=0, tile...  107 us
    all_to_all x1, waiting for transfers between devices, body(): lax.all_to_all(processed.reshape(experts, capacity, model_width), ('kv',...  96.5 us
    dot_general x1, matrix products, expert_block(): jnp.dot(inner_act, down_weights[0], preferred_element_type=jnp.float32)  21.3 us
    dot_general x1, matrix products, expert_block(): jnp.dot(slots, gate_weights[0], preferred_element_type=jnp.float32)  8.57 us
    pallas_call x1, Pallas kernels, kv_reduce(): pl.pallas_call(lambda *refs: kv_reduce_kernel(n_kv, *refs), out_shape=jax...  7.62 us
    all_to_all x1, starting transfers between devices, body(): lax.all_to_all(processed.reshape(experts, capacity, model_width), ('kv',...  7.51 us
    dot_general x1, matrix products, body(): jnp.dot(jnp.concatenate([mix_hi, mix_lo], axis=0), returned, preferred_el...  6.01 us
  transfers between devices with their start and end apart: 1, of which 1 were waited for; matrix products, arithmetic and copies ran while one was open for 2% of the time, Pallas kernels for 0%

commit v1 on v0

--- a/solution.py
+++ b/solution.py
@@ -140,27 +140,55 @@
     rank_hot = slot_rank[..., None] == jnp.arange(capacity, dtype=jnp.int32)
     fills = one_hot[..., None] & rank_hot[:, :, None, :]
     place = jnp.any(fills, axis=1).reshape(tokens, experts * capacity).astype(jnp.bfloat16)
-    outgoing = jnp.einsum("ts,td->sd", place, normed, preferred_element_type=jnp.float32)
-    outgoing = outgoing.astype(jnp.bfloat16).reshape(experts, capacity, model_width)
-    arrived = lax.all_to_all(outgoing, ("kv", "blk"), split_axis=0, concat_axis=0, tiled=True)
-    processed = expert_block(
-        arrived.reshape(experts * capacity, model_width), expert_gate, expert_up, expert_down
-    )
-    returned = lax.all_to_all(
-        processed.reshape(experts, capacity, model_width),
-        ("kv", "blk"),
-        split_axis=0,
-        concat_axis=0,
-        tiled=True,
-    ).reshape(experts * capacity, model_width)
+    pieces = 2
+    piece = model_width // pieces
+    arrived = []
+    for i in range(pieces):
+        sent = jnp.einsum(
+            "ts,td->sd",
+            place,
+            normed[:, i * piece : (i + 1) * piece],
+            preferred_element_type=jnp.float32,
+        ).astype(jnp.bfloat16)
+        arrived.append(
+            lax.all_to_all(
+                sent.reshape(experts, capacity, piece),
+                ("kv", "blk"),
+                split_axis=0,
+                concat_axis=0,
+                tiled=True,
+            ).reshape(experts * capacity, piece)
+        )
+    gate_w, up_w, down_w = expert_gate[0], expert_up[0], expert_down[0]
+    gate_act = sum(
+        jnp.dot(arrived[i], gate_w[i * piece : (i + 1) * piece], preferred_element_type=jnp.float32)
+        for i in range(pieces)
+    )
+    up_act = sum(
+        jnp.dot(arrived[i], up_w[i * piece : (i + 1) * piece], preferred_element_type=jnp.float32)
+        for i in range(pieces)
+    )
+    inner_act = (gate_act / (1.0 + jnp.exp(-gate_act)) * up_act).astype(jnp.bfloat16)
     mix = jnp.sum(jnp.where(fills, gate_probs[..., None, None], 0.0), axis=1)
     mix = mix.reshape(tokens, experts * capacity)
     mix_hi = mix.astype(jnp.bfloat16)
     mix_lo = (mix - mix_hi.astype(jnp.float32)).astype(jnp.bfloat16)
-    both = jnp.dot(
-        jnp.concatenate([mix_hi, mix_lo], axis=0), returned, preferred_element_type=jnp.float32
-    )
-    combined = both[:tokens] + both[tokens:]
+    mix_both = jnp.concatenate([mix_hi, mix_lo], axis=0)
+    combined_parts = []
+    for i in range(pieces):
+        processed = jnp.dot(
+            inner_act, down_w[:, i * piece : (i + 1) * piece], preferred_element_type=jnp.float32
+        ).astype(jnp.bfloat16)
+        returned = lax.all_to_all(
+            processed.reshape(experts, capacity, piece),
+            ("kv", "blk"),
+            split_axis=0,
+            concat_axis=0,
+            tiled=True,
+        ).reshape(experts * capacity, piece)
+        both = jnp.dot(mix_both, returned, preferred_element_type=jnp.float32)
+        combined_parts.append(both[:tokens] + both[tokens:])
+    combined = jnp.concatenate(combined_parts, axis=1)
     layer_sum = (hidden_f + combined).astype(jnp.bfloat16)
     return layer_sum[None]
 

time: 290 us -> 295 us (1.017)
  blocking collectives: 107 us -> 0 us
  waiting for transfers between devices: 96.5 us -> 172 us
  matrix products: 45 us -> 68.5 us
  starting transfers between devices: 7.51 us -> 27.9 us
  local copies, waits for them, and re-layouts: 7.08 us -> 3.21 us
    all_to_all x1 -> x0, blocking collectives: 107 us -> none  [body(): lax.all_to_all(outgoing, ('kv', 'blk'), split_axis=0, concat_axis=0, tile...]
    all_to_all x1 -> x4, waiting for transfers between devices: 96.5 us -> 172 us  [the longest x2 87.5 us: body(): lax.all_to_all(processed.reshape(experts, capacity, piece), ('kv', 'blk')...]
    dot_general x4 -> x10, matrix products: 39.3 us -> 63 us  [the longest x2 19.8 us: body(): jnp.dot(arrived[i], up_w[i * piece:(i + 1) * piece], preferred_element_ty...]
    all_to_all x1 -> x4, starting transfers between devices: 7.51 us -> 27.9 us  [the longest x2 16.1 us: body(): lax.all_to_all(sent.reshape(experts, capacity, piece), ('kv', 'blk'), spl...]
    unnamed x34 -> x24, local copies, waits for them, and re-layouts: 3.9 us -> 0.06 us
  transfers between devices with their start and end apart: 1 -> 4, of which waited for: 1 -> 4; matrix products, arithmetic and copies ran while one was open for 2% -> 13% of each run, Pallas kernels for 0% -> 0%
where the time goes in v1:
time: 295 us; the launch traced here: 293 us
  waiting for transfers between devices  172 us (58%)
  matrix products  68.5 us (23%)
  starting transfers between devices  27.9 us (9%)
  other arithmetic  13.7 us (5%)
  Pallas kernels  7.62 us (3%)
  local copies, waits for them, and re-layouts  3.21 us (1%)
    all_to_all x2, waiting for transfers between devices, body(): lax.all_to_all(processed.reshape(experts, capacity, piece), ('kv', 'blk')...  87.5 us
    all_to_all x2, waiting for transfers between devices, body(): lax.all_to_all(sent.reshape(experts, capacity, piece), ('kv', 'blk'), spl...  84 us
    dot_general x2, matrix products, body(): jnp.dot(arrived[i], up_w[i * piece:(i + 1) * piece], preferred_element_ty...  19.8 us
    dot_general x2, matrix products, body(): jnp.dot(arrived[i], gate_w[i * piece:(i + 1) * piece], preferred_element_...  17.1 us
    all_to_all x2, starting transfers between devices, body(): lax.all_to_all(sent.reshape(experts, capacity, piece), ('kv', 'blk'), spl...  16.1 us
    dot_general x2, matrix products, body(): jnp.dot(inner_act, down_w[:, i * piece:(i + 1) * piece], preferred_elemen...  12.9 us
    all_to_all x2, starting transfers between devices, body(): lax.all_to_all(processed.reshape(experts, capacity, piece), ('kv', 'blk')...  11.8 us
    pallas_call x1, Pallas kernels, kv_reduce(): pl.pallas_call(lambda *refs: kv_reduce_kernel(n_kv, *refs), out_shape=jax...  7.62 us
  transfers between devices with their start and end apart: 4, of which 4 were waited for; matrix products, arithmetic and copies ran while one was open for 13% of the time, Pallas kernels for 0%

profile of v1, /device:TPU:2, one launch (start us, length us, event | category | flops | bytes accessed | tf_op | source)
XLA Modules:
  0.0 292.8 jit_solution(5485067483578042799)
XLA Ops:
  0.0 0.9 copy.24
  0.9 0.3 iota_compare_fusion.1
  1.1 0.2 reduce_window_sum.11
  1.3 2.1 select_reduce_fusion.1
  3.4 0.2 iota_compare_fusion
  3.6 2.8 and_reduce_fusion
  6.4 0.8 copy.29
  7.2 0.9 minimum_subtract_fusion
  8.1 0.1 iota_compare_fusion.2
  8.2 3.8 %fusion.55 = (f32[4,8]{1,0:T(4,128)S(1)}, f32[4,8,4096]{2,1,0:T(8,128)S(1)}) fusion(bf16[4,4096,1,128]{3,1,2,0:T(8,128)(2,1)} %param.15, bf16[1,4,8,128]{3,1,2,0:T(4,128)(2,1)} %bitcast.83, pred[4,4096]{1,0:T(4,128)(4,1)S(1)} %iota_compare_fusion.2), kind=kOutput, calls=%fused_computation.78 | convolution fusion | flops 33947616 | bytes 4743296 | tf_op jit(solution)/shard_map/rgd,rjd->rgj/dot_general | solution.py:103
  12.0 0.3 fusion.36
  12.3 0.7 fusion.24
  13.1 0.7 fusion.45
  13.7 0.6 reshape.225.refs_0_
  14.4 7.6 %shard_map.136 = f32[1,2048]{1,0:T(1,128)} custom-call(f32[4,1,2048]{2,1,0:T(1,128)} %reshape.225.refs_0_), custom_call_target="tpu_custom_call" | custom-call | tf_op jit(solution)/shard_map/pallas_call | solution.py:55
  22.0 0.7 add_convert_fusion
  22.7 0.2 fusion.28
  23.0 0.3 fusion.30
  23.2 3.2 %convolution_convert_fusion.3 = bf16[2048,1024]{1,0:T(8,128)(2,1)} fusion(pred[112,2048]{0,1:T(8,128)(4,1)S(1)} %bitcast.80, bf16[112,2048]{1,0:T(8,128)(2,1)S(1)} %fusion.30), kind=kOutput, calls=%fused_computation.12 | convolution fusion | flops 471859200 | bytes 4685824 | tf_op jit(solution)/shard_map/ts,td->sd/dot_general | solution.py:147
  26.4 10.0 %all-to-all-start = ((bf16[128,16,1024]{2,1,0:T(8,128)(2,1)}), bf16[128,16,1024]{2,1,0:T(8,128)(2,1)}, u32[]{:S(2)}, u32[]{:S(2)}) async-start(bf16[128,16,1024]{2,1,0:T(8,128)(2,1)} %bitcast.75), calls=%async_computation | async-start | bytes 8388608 | tf_op jit(solution)/shard_map/all_to_all | solution.py:154
  36.5 3.2 %convolution_convert_fusion.2 = bf16[2048,1024]{1,0:T(8,128)(2,1)} fusion(pred[112,2048]{0,1:T(8,128)(4,1)S(1)} %bitcast.81, bf16[112,2048]{1,0:T(8,128)(2,1)S(1)} %fusion.30), kind=kOutput, calls=%fused_computation.11 | convolution fusion | flops 471859200 | bytes 4685824 | tf_op jit(solution)/shard_map/ts,td->sd/dot_general | solution.py:147
  39.7 49.0 %all-to-all-done = bf16[128,16,1024]{2,1,0:T(8,128)(2,1)} async-done(((bf16[128,16,1024]{2,1,0:T(8,128)(2,1)}), bf16[128,16,1024]{2,1,0:T(8,128)(2,1)}, u32[]{:S(2)}, u32[]{:S(2)}) %all-to-all-start) | async-done | bytes 4194336 | tf_op jit(solution)/shard_map/all_to_all | solution.py:154
  88.7 6.1 %all-to-all-start.1 = ((bf16[128,16,1024]{2,1,0:T(8,128)(2,1)}), bf16[128,16,1024]{2,1,0:T(8,128)(2,1)}, u32[]{:S(2)}, u32[]{:S(2)}) async-start(bf16[128,16,1024]{2,1,0:T(8,128)(2,1)} %bitcast.74), calls=%async_computation.1 | async-start | bytes 8388608 | tf_op jit(solution)/shard_map/all_to_all | solution.py:154
  94.8 8.9 %fusion.8 = f32[2048,768]{1,0:T(8,128)} fusion(bf16[2048,1024]{1,0:T(8,128)(2,1)} %bitcast.8, bf16[1,2048,768]{2,1,0:T(8,128)(2,1)} %param.26), kind=kOutput, calls=%fused_computation.16 | convolution fusion | flops 3221225472 | bytes 12058624 | tf_op jit(solution)/shard_map/dot_general | solution.py:168
  103.6 8.3 %fusion.12 = f32[2048,768]{1,0:T(8,128)} fusion(bf16[2048,1024]{1,0:T(8,128)(2,1)} %bitcast.8, bf16[1,2048,768]{2,1,0:T(8,128)(2,1)S(1)} %copy-done.7), kind=kOutput, calls=%fused_computation.20 | convolution fusion | flops 3221225472 | bytes 12058624 | tf_op jit(solution)/shard_map/dot_general | solution.py:164
  111.9 35.0 %all-to-all-done.1 = bf16[128,16,1024]{2,1,0:T(8,128)(2,1)} async-done(((bf16[128,16,1024]{2,1,0:T(8,128)(2,1)}), bf16[128,16,1024]{2,1,0:T(8,128)(2,1)}, u32[]{:S(2)}, u32[]{:S(2)}) %all-to-all-start.1) | async-done | bytes 4194336 | tf_op jit(solution)/shard_map/all_to_all | solution.py:154
  146.9 8.8 %fusion.10 = f32[2048,768]{1,0:T(8,128)} fusion(bf16[2048,1024]{1,0:T(8,128)(2,1)} %bitcast.11, bf16[1,2048,768]{2,1,0:T(8,128)(2,1)} %param.25), kind=kOutput, calls=%fused_computation.18 | convolution fusion | flops 3221225472 | bytes 12058624 | tf_op jit(solution)/shard_map/dot_general | solution.py:164
  155.8 11.0 %multiply_convert_fusion = bf16[2048,768]{1,0:T(8,128)(2,1)S(1)} fusion(f32[2048,768]{1,0:T(8,128)S(1)} %copy-done.10, f32[2048,768]{1,0:T(8,128)} %fusion.12, f32[2048,768]{1,0:T(8,128)} %fusion.10, bf16[2048,1024]{1,0:T(8,128)(2,1)} %bitcast.11, bf16[1,2048,768]{2,1,0:T(8,128)(2,1)S(1)} %copy-done.8), kind=kOutput, calls=%fused_computation.3 | convolution fusion | flops 3232235520 | bytes 27787264 | tf_op jit(solution)/shard_map/dot_general | solution.py:168
  166.8 5.1 %convolution_convert_fusion = bf16[2048,1024]{1,0:T(8,128)(2,1)} fusion(bf16[2048,768]{1,0:T(8,128)(2,1)S(1)} %multiply_convert_fusion, bf16[768,2048]{1,0:T(8,128)(2,1)S(1)} %bitcast.86), kind=kOutput, calls=%fused_computation.9 | convolution fusion | flops 3223322624 | bytes 8912896 | tf_op jit(solution)/shard_map/dot_general | solution.py:179
  171.9 5.9 %all-to-all-start.3 = ((bf16[128,16,1024]{2,1,0:T(8,128)(2,1)}), bf16[128,16,1024]{2,1,0:T(8,128)(2,1)}, u32[]{:S(2)}, u32[]{:S(2)}) async-start(bf16[128,16,1024]{2,1,0:T(8,128)(2,1)} %bitcast.77), calls=%async_computation.3 | async-start | bytes 8388608 | tf_op jit(solution)/shard_map/all_to_all | solution.py:182
  177.8 7.8 %convolution_convert_fusion.1 = bf16[2048,1024]{1,0:T(8,128)(2,1)} fusion(bf16[2048,768]{1,0:T(8,128)(2,1)} %copy-done.11, bf16[768,2048]{1,0:T(8,128)(2,1)} %bitcast.85), kind=kOutput, calls=%fused_computation.10 | convolution fusion | flops 3223322624 | bytes 8912896 | tf_op jit(solution)/shard_map/dot_general | solution.py:179
  185.6 44.6 %all-to-all-done.3 = bf16[128,16,1024]{2,1,0:T(8,128)(2,1)} async-done(((bf16[128,16,1024]{2,1,0:T(8,128)(2,1)}), bf16[128,16,1024]{2,1,0:T(8,128)(2,1)}, u32[]{:S(2)}, u32[]{:S(2)}) %all-to-all-start.3) | async-done | bytes 4194336 | tf_op jit(solution)/shard_map/all_to_all | solution.py:182
  230.2 5.9 %all-to-all-start.2 = ((bf16[128,16,1024]{2,1,0:T(8,128)(2,1)}), bf16[128,16,1024]{2,1,0:T(8,128)(2,1)}, u32[]{:S(2)}, u32[]{:S(2)}) async-start(bf16[128,16,1024]{2,1,0:T(8,128)(2,1)} %bitcast.76), calls=%async_computation.2 | async-start | bytes 8388608 | tf_op jit(solution)/shard_map/all_to_all | solution.py:182
  236.1 0.3 fusion.56
  236.4 0.3 select_reduce_fusion
  236.7 0.1 copy.26
  236.7 0.1 reduce_max.19
  236.9 0.1 copy.27
  237.0 4.1 %fusion = f32[112,128,16]{1,2,0:T(8,128)S(1)} fusion(f32[112,8]{1,0:T(8,128)S(1)} %copy.27, pred[112,8,16]{2,1,0:T(8,128)(4,1)S(1)} %iota_compare_fusion, pred[112,8,128]{2,1,0:T(8,128)(4,1)S(1)} %get-tuple-element.5), kind=kLoop, calls=%fused_computation.2 | loop fusion | flops 5275648 | bytes 1050112 | tf_op jit(solution)/shard_map/reduce_sum | solution.py:172
  241.2 0.7 copy.28
  241.9 0.1 fusion.27
  241.9 0.1 bitcast_convert_fusion
  242.0 3.4 %fusion.32 = f32[224,1024]{1,0:T(8,128)S(1)} fusion(bf16[2048,1024]{1,0:T(8,128)(2,1)} %bitcast.20, bf16[112,2048]{0,1:T(8,128)(2,1)S(1)} %fusion.27, bf16[112,2048]{0,1:T(8,128)(2,1)S(1)} %bitcast_convert_fusion), kind=kOutput, calls=%fused_computation.40 | convolution fusion | flops 941359104 | bytes 6029312 | tf_op jit(solution)/shard_map/dot_general | solution.py:189
  245.4 0.1 fusion.34
  245.5 43.0 %all-to-all-done.2 = bf16[128,16,1024]{2,1,0:T(8,128)(2,1)} async-done(((bf16[128,16,1024]{2,1,0:T(8,128)(2,1)}), bf16[128,16,1024]{2,1,0:T(8,128)(2,1)}, u32[]{:S(2)}, u32[]{:S(2)}) %all-to-all-start.2) | async-done | bytes 4194336 | tf_op jit(solution)/shard_map/all_to_all | solution.py:182
  288.4 3.4 %fusion.33 = f32[224,1024]{1,0:T(8,128)S(1)} fusion(bf16[2048,1024]{1,0:T(8,128)(2,1)} %bitcast.17, bf16[112,2048]{0,1:T(8,128)(2,1)S(1)} %fusion.27, bf16[112,2048]{0,1:T(8,128)(2,1)S(1)} %bitcast_convert_fusion), kind=kOutput, calls=%fused_computation.41 | convolution fusion | flops 941359104 | bytes 6029312 | tf_op jit(solution)/shard_map/dot_general | solution.py:189
  291.8 0.1 fusion.35
  291.9 0.9 fusion.31
  (31 shorter events, 0.1 us)
Async XLA Ops:
  0.0 236.1 %copy-start = (bf16[2048,128]{1,0:T(8,128)(2,1)S(1)}, bf16[2048,128]{1,0:T(8,128)(2,1)}, u32[]{:S(2)}) copy-start(bf16[2048,128]{1,0:T(8,128)(2,1)} %param.23) | copy-start | bytes 1572868
  0.0 12.0 %copy-start.6 = (f32[8]{0:T(128)S(1)}, f32[8]{0:T(128)}, u32[]{:S(2)}) copy-start(f32[8]{0:T(128)} %param.18) | copy-start | bytes 100
  7.2 5.1 %copy-start.1 = (bf16[4,4096,1,128]{3,1,2,0:T(8,128)(2,1)S(1)}, bf16[4,4096,1,128]{3,1,2,0:T(8,128)(2,1)}, u32[]{:S(2)}) copy-start(bf16[4,4096,1,128]{3,1,2,0:T(8,128)(2,1)} %param.16) | copy-start | bytes 12582916
  8.2 4.9 %copy-start.2 = (bf16[1024,2048]{1,0:T(8,128)(2,1)S(1)}, bf16[1024,2048]{1,0:T(8,128)(2,1)}, u32[]{:S(2)}) copy-start(bf16[1024,2048]{1,0:T(8,128)(2,1)} %param.19) | copy-start | bytes 12582916
  12.3 9.7 %copy-start.5 = (bf16[1,2048]{1,0:T(2,128)(2,1)S(1)}, bf16[1,2048]{1,0:T(2,128)(2,1)}, u32[]{:S(2)}) copy-start(bf16[1,2048]{1,0:T(2,128)(2,1)} %param.20) | copy-start | bytes 12292
  12.3 10.4 %copy-start.3 = (bf16[1,111,2048]{2,1,0:T(8,128)(2,1)S(1)}, bf16[1,111,2048]{2,1,0:T(8,128)(2,1)}, u32[]{:S(2)}) copy-start(bf16[1,111,2048]{2,1,0:T(8,128)(2,1)} %param.21) | copy-start | bytes 1363972
  12.3 10.7 %copy-start.4 = (f32[2048]{0:T(1024)S(1)}, f32[2048]{0:T(1024)}, u32[]{:S(2)}) copy-start(f32[2048]{0:T(1024)} %param.22) | copy-start | bytes 24580
  26.4 62.3 %all-to-all-start = ((bf16[128,16,1024]{2,1,0:T(8,128)(2,1)}), bf16[128,16,1024]{2,1,0:T(8,128)(2,1)}, u32[]{:S(2)}, u32[]{:S(2)}) async-start(bf16[128,16,1024]{2,1,0:T(8,128)(2,1)} %bitcast.75), calls=%async_computation | async-start | bytes 8388608 | tf_op jit(solution)/shard_map/all_to_all | solution.py:154
  88.7 58.3 %all-to-all-start.1 = ((bf16[128,16,1024]{2,1,0:T(8,128)(2,1)}), bf16[128,16,1024]{2,1,0:T(8,128)(2,1)}, u32[]{:S(2)}, u32[]{:S(2)}) async-start(bf16[128,16,1024]{2,1,0:T(8,128)(2,1)} %bitcast.74), calls=%async_computation.1 | async-start | bytes 8388608 | tf_op jit(solution)/shard_map/all_to_all | solution.py:154
  94.8 8.9 %copy-start.7 = (bf16[1,2048,768]{2,1,0:T(8,128)(2,1)S(1)}, bf16[1,2048,768]{2,1,0:T(8,128)(2,1)}, u32[]{:S(2)}) copy-start(bf16[1,2048,768]{2,1,0:T(8,128)(2,1)} %param.25) | copy-start | bytes 9437188
  146.9 8.9 %copy-start.8 = (bf16[1,2048,768]{2,1,0:T(8,128)(2,1)S(1)}, bf16[1,2048,768]{2,1,0:T(8,128)(2,1)}, u32[]{:S(2)}) copy-start(bf16[1,2048,768]{2,1,0:T(8,128)(2,1)} %param.26) | copy-start | bytes 9437188
  146.9 8.9 %copy-start.10 = (f32[2048,768]{1,0:T(8,128)S(1)}, f32[2048,768]{1,0:T(8,128)}, u32[]{:S(2)}) copy-start(f32[2048,768]{1,0:T(8,128)} %fusion.8) | copy-start | bytes 18874372
  155.8 11.0 %copy-start.9 = (bf16[1,768,2048]{2,1,0:T(8,128)(2,1)S(1)}, bf16[1,768,2048]{2,1,0:T(8,128)(2,1)}, u32[]{:S(2)}) copy-start(bf16[1,768,2048]{2,1,0:T(8,128)(2,1)} %param.27) | copy-start | bytes 9437188
  166.8 5.1 %copy-start.11 = (bf16[2048,768]{1,0:T(8,128)(2,1)}, bf16[2048,768]{1,0:T(8,128)(2,1)S(1)}, u32[]{:S(2)}) copy-start(bf16[2048,768]{1,0:T(8,128)(2,1)S(1)} %multiply_convert_fusion) | copy-start | bytes 9437188
  171.9 58.2 %all-to-all-start.3 = ((bf16[128,16,1024]{2,1,0:T(8,128)(2,1)}), bf16[128,16,1024]{2,1,0:T(8,128)(2,1)}, u32[]{:S(2)}, u32[]{:S(2)}) async-start(bf16[128,16,1024]{2,1,0:T(8,128)(2,1)} %bitcast.77), calls=%async_computation.3 | async-start | bytes 8388608 | tf_op jit(solution)/shard_map/all_to_all | solution.py:182
  230.2 58.3 %all-to-all-start.2 = ((bf16[128,16,1024]{2,1,0:T(8,128)(2,1)}), bf16[128,16,1024]{2,1,0:T(8,128)(2,1)}, u32[]{:S(2)}, u32[]{:S(2)}) async-start(bf16[128,16,1024]{2,1,0:T(8,128)(2,1)} %bitcast.76), calls=%async_computation.2 | async-start | bytes 8388608 | tf_op jit(solution)/shard_map/all_to_all | solution.py:182

commit v2 on v0

--- a/solution.py
+++ b/solution.py
@@ -137,10 +137,12 @@
     row_hot = jnp.any(one_hot, axis=1).astype(jnp.int32)
     earlier = jnp.cumsum(row_hot, axis=0) - row_hot
     slot_rank = jnp.sum(jnp.where(one_hot, earlier[:, None, :], 0), axis=2)
-    rank_hot = slot_rank[..., None] == jnp.arange(capacity, dtype=jnp.int32)
-    fills = one_hot[..., None] & rank_hot[:, :, None, :]
-    place = jnp.any(fills, axis=1).reshape(tokens, experts * capacity).astype(jnp.bfloat16)
-    outgoing = jnp.einsum("ts,td->sd", place, normed, preferred_element_type=jnp.float32)
+    slot_id = chosen_ids * capacity + slot_rank
+    slot_iota = jnp.arange(experts * capacity, dtype=jnp.int32)
+    place_t = jnp.any(
+        slot_id[None, :, :] == slot_iota[:, None, None], axis=2
+    ).astype(jnp.bfloat16)
+    outgoing = jnp.dot(place_t, normed, preferred_element_type=jnp.float32)
     outgoing = outgoing.astype(jnp.bfloat16).reshape(experts, capacity, model_width)
     arrived = lax.all_to_all(outgoing, ("kv", "blk"), split_axis=0, concat_axis=0, tiled=True)
     processed = expert_block(
@@ -153,8 +155,10 @@
         concat_axis=0,
         tiled=True,
     ).reshape(experts * capacity, model_width)
-    mix = jnp.sum(jnp.where(fills, gate_probs[..., None, None], 0.0), axis=1)
-    mix = mix.reshape(tokens, experts * capacity)
+    mix = jnp.sum(
+        jnp.where(slot_id[:, :, None] == slot_iota[None, None, :], gate_probs[..., None], 0.0),
+        axis=1,
+    )
     mix_hi = mix.astype(jnp.bfloat16)
     mix_lo = (mix - mix_hi.astype(jnp.float32)).astype(jnp.bfloat16)
     both = jnp.dot(

time: 290 us -> 291 us (level)
  no operation moved by 1% of the time
where the time goes in v2:
time: 291 us; the launch traced here: 288 us
  blocking collectives  107 us (37%)
  waiting for transfers between devices  99 us (34%)
  matrix products  47 us (16%)
  other arithmetic  15.7 us (5%)
  Pallas kernels  7.62 us (3%)
  starting transfers between devices  7.5 us (3%)
  local copies, waits for them, and re-layouts  4.3 us (1%)
    all_to_all x1, blocking collectives, body(): lax.all_to_all(outgoing, ('kv', 'blk'), split_axis=0, concat_axis=0, tile...  107 us
    all_to_all x1, waiting for transfers between devices, body(): lax.all_to_all(processed.reshape(experts, capacity, model_width), ('kv',...  99 us
    dot_general x1, matrix products, expert_block(): jnp.dot(inner_act, down_weights[0], preferred_element_type=jnp.float32)  21.3 us
    dot_general x1, matrix products, expert_block(): jnp.dot(slots, gate_weights[0], preferred_element_type=jnp.float32)  8.57 us
    pallas_call x1, Pallas kernels, kv_reduce(): pl.pallas_call(lambda *refs: kv_reduce_kernel(n_kv, *refs), out_shape=jax...  7.62 us
    all_to_all x1, starting transfers between devices, body(): lax.all_to_all(processed.reshape(experts, capacity, model_width), ('kv',...  7.5 us
    dot_general x1, matrix products, body(): jnp.dot(jnp.concatenate([mix_hi, mix_lo], axis=0), returned, preferred_el...  5.86 us
  transfers between devices with their start and end apart: 1, of which 1 were waited for; matrix products, arithmetic and copies ran while one was open for 2% of the time, Pallas kernels for 0%

profile of v2, /device:TPU:2, one launch (start us, length us, event | category | flops | bytes accessed | tf_op | source)
XLA Modules:
  0.0 288.3 jit_solution(4235108891116080526)
XLA Ops:
  0.0 0.0 copy-start
  0.0 0.9 minimum_subtract_fusion
  0.9 0.1 iota_compare_fusion.3
  1.0 0.0 copy-start.7
  1.0 0.0 copy-start.6
  1.0 3.9 %fusion.50 = (f32[4,8]{1,0:T(4,128)S(1)}, f32[4,8,4096]{2,1,0:T(8,128)S(1)}) fusion(bf16[4,4096,1,128]{3,1,2,0:T(8,128)(2,1)} %param.15, bf16[1,4,8,128]{3,1,2,0:T(4,128)(2,1)} %bitcast.67, pred[4,4096]{1,0:T(4,128)(4,1)S(1)} %iota_compare_fusion.3), kind=kOutput, calls=%fused_computation.67 | convolution fusion | flops 33947616 | bytes 4743296 | tf_op jit(solution)/shard_map/rgd,rjd->rgj/dot_general | solution.py:103
  4.9 0.7 broadcast_maximum_fusion
  5.6 0.3 fusion.30
  5.9 0.7 exponential_add_fusion
  6.6 2.9 %fusion.17 = bf16[1,4,8,128]{3,2,1,0:T(8,128)(2,1)S(1)} fusion(bf16[4,4096,1,128]{3,1,2,0:T(8,128)(2,1)} %param.16, f32[4,8,4096]{2,1,0:T(8,128)S(1)} %get-tuple-element.8, f32[4,8]{1,0:T(4,128)S(1)} %broadcast_maximum_fusion, pred[4,4096]{1,0:T(4,128)(4,1)S(1)} %iota_compare_fusion.3, f32[4,8]{1,0:T(4,128)S(1)} %exponential_add_fusion), kind=kOutput, calls=%fused_computation.22 | convolution fusion | flops 33955840 | bytes 4743424 | tf_op jit(solution)/shard_map/rgj,rjd->rgd/dot_general | solution.py:112
  9.5 0.0 copy-done.3
  9.5 0.7 fusion.39
  10.2 0.6 reshape.146.refs_0_
  10.8 7.6 %shard_map.136 = f32[1,2048]{1,0:T(1,128)} custom-call(f32[4,1,2048]{2,1,0:T(1,128)} %reshape.146.refs_0_), custom_call_target="tpu_custom_call" | custom-call | tf_op jit(solution)/shard_map/pallas_call | solution.py:55
  18.4 0.0 copy-done.7
  18.4 0.7 add_convert_fusion
  19.2 1.3 fusion.20
  20.4 0.0 copy-done.6
  20.5 0.1 copy.25
  20.6 0.2 fusion.29
  20.8 0.2 reduce_window_sum.11
  21.0 2.1 select_reduce_fusion.2
  23.1 0.1 copy.29
  23.1 0.1 copy.30
  23.2 3.7 %fusion = pred[2048,112]{0,1:T(8,128)(4,1)S(1)} fusion(s32[112,8]{1,0:T(8,128)S(1)} %copy.30), kind=kLoop, calls=%fused_computation.5 | loop fusion | flops 3440640 | bytes 232960 | tf_op jit(solution)/shard_map/reduce_or | solution.py:142
  26.9 0.0 copy-done.8
  27.0 3.5 %convolution_convert_fusion.1 = bf16[2048,2048]{1,0:T(8,128)(2,1)S(1)} fusion(pred[2048,112]{0,1:T(8,128)(4,1)S(1)} %fusion, f32[2048]{0:T(1024)S(1)} %copy-done.8, f32[112]{0:T(128)S(1)} %add_rsqrt_fusion, bf16[111,2048]{1,0:T(8,128)(2,1)} %bitcast.61, bf16[1,2048]{1,0:T(2,128)(2,1)S(1)} %add_convert_fusion), kind=kOutput, calls=%fused_computation.1 | convolution fusion | flops 945324032 | bytes 9085376 | tf_op jit(solution)/shard_map/dot_general | solution.py:145
  30.4 0.0 copy-start.9
  30.4 107.0 %all_to_all.10 = bf16[128,16,2048]{2,1,0:T(8,128)(2,1)S(1)} all-to-all(bf16[128,16,2048]{2,1,0:T(8,128)(2,1)S(1)} %bitcast.56), channel_id=1, replica_groups=mesh['kv'=4,'blk'=32] {'kv','blk'}, dimensions={0} | all-to-all | bytes 16777216 | tf_op jit(solution)/shard_map/all_to_all | solution.py:147
  137.4 3.2 %copy-done.2 = bf16[128,16,2048]{2,1,0:T(8,128)(2,1)} copy-done((bf16[128,16,2048]{2,1,0:T(8,128)(2,1)}, bf16[128,16,2048]{2,1,0:T(8,128)(2,1)S(1)}, u32[]{:S(2)}) %copy-start.2) | copy-done | bytes 8388632
  140.6 0.0 copy-done.9
  140.6 8.6 %fusion.8 = f32[2048,768]{1,0:T(8,128)} fusion(bf16[2048,2048]{1,0:T(8,128)(2,1)S(1)} %bitcast.58, bf16[1,2048,768]{2,1,0:T(8,128)(2,1)S(1)} %copy-done.9), kind=kOutput, calls=%fused_computation.14 | convolution fusion | flops 6442450944 | bytes 17825792 | tf_op jit(solution)/shard_map/dot_general | solution.py:70
  149.2 0.0 copy-done
  149.2 21.3 %convolution_convert_fusion = bf16[2048,2048]{1,0:T(8,128)(2,1)} fusion(f32[2048,768]{1,0:T(8,128)} %fusion.8, bf16[2048,2048]{1,0:T(8,128)(2,1)} %bitcast.59, bf16[1,768,2048]{2,1,0:T(8,128)(2,1)S(1)} %copy-done, bf16[1,2048,768]{2,1,0:T(8,128)(2,1)} %param.26), kind=kOutput, calls=%fused_computation | convolution fusion | flops 12896960512 | bytes 29360128 | tf_op jit(solution)/shard_map/dot_general | solution.py:73
  170.5 7.5 %all-to-all-start.1 = ((bf16[128,16,2048]{2,1,0:T(8,128)(2,1)}), bf16[128,16,2048]{2,1,0:T(8,128)(2,1)}, u32[]{:S(2)}, u32[]{:S(2)}) async-start(bf16[128,16,2048]{2,1,0:T(8,128)(2,1)} %bitcast.57), calls=%async_computation.1 | async-start | bytes 16777216 | tf_op jit(solution)/shard_map/all_to_all | solution.py:151
  178.0 0.0 copy-done.4
  178.0 0.0 copy-done.10
  178.0 0.4 fusion.37
  178.4 0.3 select_reduce_fusion.1
  178.7 0.1 copy.27
  178.7 0.1 reduce_max.19
  178.9 0.1 copy.28
  179.0 2.4 select_reduce_fusion
  181.5 1.0 subtract_convert_fusion
  182.5 99.0 %all-to-all-done.1 = bf16[128,16,2048]{2,1,0:T(8,128)(2,1)} async-done(((bf16[128,16,2048]{2,1,0:T(8,128)(2,1)}), bf16[128,16,2048]{2,1,0:T(8,128)(2,1)}, u32[]{:S(2)}, u32[]{:S(2)}) %all-to-all-start.1) | async-done | bytes 8388640 | tf_op jit(solution)/shard_map/all_to_all | solution.py:151
  281.5 5.9 %fusion.24 = f32[224,2048]{1,0:T(8,128)S(1)} fusion(bf16[2048,2048]{1,0:T(8,128)(2,1)} %bitcast.12, bf16[112,2048]{1,0:T(8,128)(2,1)} %get-tuple-element.5, bf16[112,2048]{1,0:T(8,128)(2,1)} %get-tuple-element.6), kind=kOutput, calls=%fused_computation.28 | convolution fusion | flops 1880883200 | bytes 11141120 | tf_op jit(solution)/shard_map/dot_general | solution.py:164
  287.4 0.0 copy-done.5
  287.4 1.0 fusion.28
  (15 shorter events, 0.1 us)
Async XLA Ops:
  0.0 149.2 %copy-start = (bf16[1,768,2048]{2,1,0:T(8,128)(2,1)S(1)}, bf16[1,768,2048]{2,1,0:T(8,128)(2,1)}, u32[]{:S(2)}) copy-start(bf16[1,768,2048]{2,1,0:T(8,128)(2,1)} %param.27) | copy-start | bytes 9437188
  0.0 9.5 %copy-start.3 = (bf16[1024,2048]{1,0:T(8,128)(2,1)S(1)}, bf16[1024,2048]{1,0:T(8,128)(2,1)}, u32[]{:S(2)}) copy-start(bf16[1024,2048]{1,0:T(8,128)(2,1)} %param.19) | copy-start | bytes 12582916
  1.0 17.4 %copy-start.7 = (bf16[1,2048]{1,0:T(2,128)(2,1)S(1)}, bf16[1,2048]{1,0:T(2,128)(2,1)}, u32[]{:S(2)}) copy-start(bf16[1,2048]{1,0:T(2,128)(2,1)} %param.20) | copy-start | bytes 12292
  1.0 19.5 %copy-start.6 = (s32[1,112,8]{1,2,0:T(8,128)S(1)}, s32[1,112,8]{1,2,0:T(8,128)}, u32[]{:S(2)}) copy-start(s32[1,112,8]{1,2,0:T(8,128)} %param.24) | copy-start | bytes 10756
  4.9 22.0 %copy-start.8 = (f32[2048]{0:T(1024)S(1)}, f32[2048]{0:T(1024)}, u32[]{:S(2)}) copy-start(f32[2048]{0:T(1024)} %param.22) | copy-start | bytes 24580
  30.4 110.2 %copy-start.9 = (bf16[1,2048,768]{2,1,0:T(8,128)(2,1)S(1)}, bf16[1,2048,768]{2,1,0:T(8,128)(2,1)}, u32[]{:S(2)}) copy-start(bf16[1,2048,768]{2,1,0:T(8,128)(2,1)} %param.25) | copy-start | bytes 9437188
  137.4 3.2 %copy-start.2 = (bf16[128,16,2048]{2,1,0:T(8,128)(2,1)}, bf16[128,16,2048]{2,1,0:T(8,128)(2,1)S(1)}, u32[]{:S(2)}) copy-start(bf16[128,16,2048]{2,1,0:T(8,128)(2,1)S(1)} %all_to_all.10) | copy-start | bytes 25165828
  170.5 7.5 %copy-start.4 = (bf16[1,111,2048]{2,1,0:T(8,128)(2,1)S(1)}, bf16[1,111,2048]{2,1,0:T(8,128)(2,1)}, u32[]{:S(2)}) copy-start(bf16[1,111,2048]{2,1,0:T(8,128)(2,1)} %param.21) | copy-start | bytes 1363972
  170.5 7.5 %copy-start.10 = (bf16[2048,128]{1,0:T(8,128)(2,1)S(1)}, bf16[2048,128]{1,0:T(8,128)(2,1)}, u32[]{:S(2)}) copy-start(bf16[2048,128]{1,0:T(8,128)(2,1)} %param.23) | copy-start | bytes 1572868
  170.5 111.0 %all-to-all-start.1 = ((bf16[128,16,2048]{2,1,0:T(8,128)(2,1)}), bf16[128,16,2048]{2,1,0:T(8,128)(2,1)}, u32[]{:S(2)}, u32[]{:S(2)}) async-start(bf16[128,16,2048]{2,1,0:T(8,128)(2,1)} %bitcast.57), calls=%async_computation.1 | async-start | bytes 16777216 | tf_op jit(solution)/shard_map/all_to_all | solution.py:151
  281.5 5.9 %copy-start.5 = (bf16[1,111,2048]{2,1,0:T(8,128)(2,1)S(1)}, bf16[1,111,2048]{2,1,0:T(8,128)(2,1)}, u32[]{:S(2)}) copy-start(bf16[1,111,2048]{2,1,0:T(8,128)(2,1)} %param.21) | copy-start | bytes 1363972
  281.5 6.9 %copy-start.1 = (bf16[1,768,2048]{2,1,0:T(8,128)(2,1)S(1)}, bf16[1,768,2048]{2,1,0:T(8,128)(2,1)}, u32[]{:S(2)}) copy-start(bf16[1,768,2048]{2,1,0:T(8,128)(2,1)} %param.27) | copy-start | bytes 9437188

commit v3 on v0

--- a/solution.py
+++ b/solution.py
@@ -12,29 +12,59 @@
 MESH = pl.DeviceIdType.MESH
 
 
-def kv_reduce_kernel(n_kv, part_ref, out_ref, held, send_sem, recv_sem):
+def attend_reduce_kernel(
+    n_kv, q_ref, k_ref, v_ref, first_ref, sink_ref, proj_ref, out_ref, att, part, held, send_sem, recv_sem
+):
     me = lax.axis_index("kv")
     blk = lax.axis_index("blk")
     barrier = pltpu.get_barrier_semaphore()
     for step in range(1, n_kv):
         peer = lax.rem(me + step, n_kv)
         pl.semaphore_signal(barrier, inc=1, device_id=(peer, blk), device_id_type=MESH)
+    requests, heads, head_dim = q_ref.shape
+    window = k_ref.shape[1]
+    scale = 1.0 / math.sqrt(head_dim)
+    sink = sink_ref[...]
+    positions = lax.broadcasted_iota(jnp.int32, (heads, window), 1)
+    for r in range(requests):
+        scores = lax.dot_general(
+            q_ref[r], k_ref[r], (((1,), (1,)), ((), ())), preferred_element_type=jnp.float32
+        ) * scale
+        valid = positions >= first_ref[pl.ds(r, 1), :]
+        masked = jnp.where(valid, scores, NEG_FILL)
+        top = jnp.maximum(jnp.max(masked, axis=1, keepdims=True), sink)
+        weights = jnp.where(valid, jnp.exp(masked - top), 0.0)
+        denominator = jnp.sum(weights, axis=1, keepdims=True) + jnp.exp(sink - top)
+        numerator = jnp.dot(
+            weights.astype(jnp.bfloat16), v_ref[r], preferred_element_type=jnp.float32
+        )
+        att[:, pl.ds(r, 1), :] = (numerator / denominator).astype(jnp.bfloat16).astype(
+            jnp.float32
+        )[:, None, :]
+    total = jnp.zeros((requests, proj_ref.shape[1]), jnp.float32)
+    for h in range(heads):
+        total = total + jnp.dot(
+            att[h].astype(jnp.bfloat16),
+            proj_ref[pl.ds(h * head_dim, head_dim), :],
+            preferred_element_type=jnp.float32,
+        )
+    part[...] = total[:, None, :]
     pl.semaphore_wait(barrier, n_kv - 1)
     for step in range(1, n_kv):
         peer = lax.rem(me + step, n_kv)
         pltpu.make_async_remote_copy(
-            src_ref=part_ref.at[peer],
+            src_ref=part.at[peer],
             dst_ref=held.at[me],
             send_sem=send_sem.at[peer],
             recv_sem=recv_sem.at[me],
             device_id=(peer, blk),
             device_id_type=MESH,
         ).start()
-    own = part_ref[me]
+    own = part[me]
     for step in range(1, n_kv):
         peer = lax.rem(me + step, n_kv)
         arrival = pltpu.make_async_remote_copy(
-            src_ref=part_ref.at[peer],
+            src_ref=part.at[peer],
             dst_ref=held.at[peer],
             send_sem=send_sem.at[peer],
             recv_sem=recv_sem.at[peer],
@@ -43,27 +73,40 @@
         )
         arrival.wait_send()
         arrival.wait_recv()
-    total = own
-    for step in range(1, n_kv):
-        peer = lax.rem(me + step, n_kv)
-        total = total + held[peer]
-    out_ref[...] = total
-
-
-def kv_reduce(partial, n_kv):
-    rows, width = partial.shape
+    for step in range(1, n_kv):
+        peer = lax.rem(me + step, n_kv)
+        own = own + held[peer]
+    out_ref[...] = own
+
+
+def attend_reduce(queries, keys, values, first_valid, sinks, out_proj, n_kv):
+    requests = queries.shape[0]
+    heads = sinks.shape[0]
+    head_dim = keys.shape[2]
+    width = out_proj.shape[1]
     return pl.pallas_call(
-        lambda *refs: kv_reduce_kernel(n_kv, *refs),
+        lambda *refs: attend_reduce_kernel(n_kv, *refs),
         out_shape=jax.ShapeDtypeStruct((1, width), jnp.float32),
-        in_specs=[pl.BlockSpec(memory_space=pltpu.VMEM)],
+        in_specs=[pl.BlockSpec(memory_space=pltpu.VMEM)] * 6,
         out_specs=pl.BlockSpec(memory_space=pltpu.VMEM),
         scratch_shapes=[
+            pltpu.VMEM((heads, requests, head_dim), jnp.float32),
+            pltpu.VMEM((requests, 1, width), jnp.float32),
             pltpu.VMEM((n_kv, 1, width), jnp.float32),
             pltpu.SemaphoreType.DMA((n_kv,)),
             pltpu.SemaphoreType.DMA((n_kv,)),
         ],
-        compiler_params=pltpu.CompilerParams(collective_id=0, has_side_effects=True),
-    )(partial.reshape(rows, 1, width))
+        compiler_params=pltpu.CompilerParams(
+            collective_id=0, has_side_effects=True, vmem_limit_bytes=48 * 1024 * 1024
+        ),
+    )(
+        queries.reshape(requests, heads, head_dim),
+        keys,
+        values,
+        first_valid.reshape(requests, 1),
+        sinks.reshape(heads, 1),
+        out_proj,
+    )
 
 
 def expert_block(slots, gate_weights, up_weights, down_weights):
@@ -96,29 +139,17 @@
     head_count = sinks.shape[0]
     head_dim = cache_keys.shape[3]
     window = cache_keys.shape[1]
-    grouped_q = queries.reshape(per_block, head_count, head_dim)
-    key_rows = cache_keys[:, :, 0, :]
-    value_rows = cache_values[:, :, 0, :]
     my_lengths = lax.dynamic_slice_in_dim(lengths, my_block * per_block, per_block)
-    scores = jnp.einsum("rgd,rjd->rgj", grouped_q, key_rows, preferred_element_type=jnp.float32) * (
-        1.0 / math.sqrt(head_dim)
-    )
     first_valid = window - jnp.minimum(my_lengths, window)
-    is_valid = (jnp.arange(window, dtype=jnp.int32)[None, :] >= first_valid[:, None])[:, None, :]
-    masked = jnp.where(is_valid, scores, NEG_FILL)
-    top_limit = jnp.maximum(jnp.max(masked, axis=2), sinks[None, :])
-    weights = jnp.where(is_valid, jnp.exp(masked - top_limit[..., None]), 0.0)
-    denominator = jnp.sum(weights, axis=2) + jnp.exp(sinks[None, :] - top_limit)
-    numerator = jnp.einsum(
-        "rgj,rjd->rgd", weights.astype(jnp.bfloat16), value_rows, preferred_element_type=jnp.float32
-    )
-    attended = (
-        (numerator / denominator[..., None])
-        .astype(jnp.bfloat16)
-        .reshape(per_block, head_count * head_dim)
-    )
-    partial_proj = jnp.dot(attended, out_proj, preferred_element_type=jnp.float32)
-    projected = kv_reduce(partial_proj, n_kv)
+    projected = attend_reduce(
+        queries,
+        cache_keys[:, :, 0, :],
+        cache_values[:, :, 0, :],
+        first_valid,
+        sinks,
+        out_proj,
+        n_kv,
+    )
     decoded = (decode_resid.astype(jnp.float32) + projected).astype(jnp.bfloat16)
     hidden = jnp.concatenate([decoded, prefill_hidden[0]], axis=0)
     hidden_f = hidden.astype(jnp.float32)

time: 290 us -> 288 us (level)
  matrix products: 45 us -> 38.6 us
  Pallas kernels: 7.62 us -> 12 us
  local copies, waits for them, and re-layouts: 7.08 us -> 11 us
    dot_general x3 -> x0, matrix products: 5.3 us -> none  [the longest x1 3.93 us: body(): jnp.einsum('rgd,rjd->rgj', grouped_q, key_rows, preferred_element_type=jn...]
    pallas_call x1, Pallas kernels: 7.62 us -> 12 us  [attend_reduce(): pl.pallas_call(lambda *refs: attend_reduce_kernel(n_kv, *refs), out_shape...]
    unnamed x34 -> x35, local copies, waits for them, and re-layouts: 3.9 us -> 6.77 us
where the time goes in v3:
time: 288 us; the launch traced here: 286 us
  blocking collectives  106 us (37%)
  waiting for transfers between devices  96.5 us (34%)
  matrix products  38.6 us (13%)
  other arithmetic  13.9 us (5%)
  Pallas kernels  12 us (4%)
  local copies, waits for them, and re-layouts  11 us (4%)
  starting transfers between devices  7.51 us (3%)
    all_to_all x1, blocking collectives, body(): lax.all_to_all(outgoing, ('kv', 'blk'), split_axis=0, concat_axis=0, tile...  106 us
    all_to_all x1, waiting for transfers between devices, body(): lax.all_to_all(processed.reshape(experts, capacity, model_width), ('kv',...  96.5 us
    dot_general x1, matrix products, expert_block(): jnp.dot(inner_act, down_weights[0], preferred_element_type=jnp.float32)  21.3 us
    pallas_call x1, Pallas kernels, attend_reduce(): pl.pallas_call(lambda *refs: attend_reduce_kernel(n_kv, *refs), out_shape...  12 us
    dot_general x1, matrix products, expert_block(): jnp.dot(slots, gate_weights[0], preferred_element_type=jnp.float32)  8.57 us
    all_to_all x1, starting transfers between devices, body(): lax.all_to_all(processed.reshape(experts, capacity, model_width), ('kv',...  7.51 us
    unnamed x35, local copies, waits for them, and re-layouts  6.77 us
    dot_general x1, matrix products, body(): jnp.dot(jnp.concatenate([mix_hi, mix_lo], axis=0), returned, preferred_el...  6.01 us
  transfers between devices with their start and end apart: 1, of which 1 were waited for; matrix products, arithmetic and copies ran while one was open for 2% of the time, Pallas kernels for 0%

profile of v3, /device:TPU:2, one launch (start us, length us, event | category | flops | bytes accessed | tf_op | source)
XLA Modules:
  0.0 285.7 jit_solution(1871673636469068038)
XLA Ops:
  0.0 0.0 copy-start
  0.0 0.9 copy.32
  0.9 0.3 iota_compare_fusion.1
  1.2 0.2 reduce_window_sum.11
  1.4 2.1 select_reduce_fusion.1
  3.5 0.2 iota_compare_fusion
  3.7 0.0 copy-start.7
  3.7 0.0 copy-done.9
  3.7 0.6 copy-done.7
  4.3 3.4 %and_reduce_fusion = pred[112,128,16]{1,2,0:T(8,128)(4,1)} fusion(pred[112,8,16]{2,1,0:T(8,128)(4,1)S(1)} %iota_compare_fusion, pred[112,8,128]{2,1,0:T(8,128)(4,1)S(1)} %get-tuple-element.7), kind=kLoop, calls=%fused_computation | loop fusion | flops 3440640 | bytes 358400 | tf_op jit(solution)/shard_map/reduce_or | solution.py:173
  7.8 1.6 copy.37
  9.4 0.7 subtract_bitcast_fusion
  10.1 0.1 copy.30.refs_3_
  10.2 0.7 copy.41
  10.9 0.7 copy.31.refs_4_
  11.7 2.2 copy-done.2
  13.9 12.0 %shard_map.136 = f32[1,2048]{1,0:T(1,128)S(1)} custom-call(bf16[4,8,128]{2,1,0:T(8,128)(2,1)S(1)} %bitcast.40, bf16[4,4096,128]{2,1,0:T(8,128)(2,1)S(1)} %bitcast.39, bf16[4,4096,128]{2,1,0:T(8,128)(2,1)} %bitcast.45, s32[4,1]{1,0:T(4,128)S(1)} %copy.30.refs_3_, f32[8,1]{1,0:T(8,128)S(1)} %copy.31.refs_4_, bf16[1024,2048]{1,0:T(8,128)(2,1)} %refs_5_.1), custom_call_target="tpu_custom_call" | custom-call | tf_op jit(solution)/shard_map/pallas_call | solution.py:87
  25.8 0.0 copy-done.11
  25.9 0.0 copy-done.4
  25.9 0.2 fusion.12
  26.1 0.0 copy-done.12
  26.1 2.4 convolution_convert_fusion.1
  28.6 0.0 copy-done.13
  28.6 0.0 copy-start.15
  28.6 106.0 %all_to_all.10 = bf16[128,16,2048]{2,1,0:T(8,128)(2,1)S(1)} all-to-all(bf16[128,16,2048]{2,1,0:T(8,128)(2,1)S(1)} %bitcast.41), channel_id=1, replica_groups=mesh['kv'=4,'blk'=32] {'kv','blk'}, dimensions={0} | all-to-all | bytes 16777216 | tf_op jit(solution)/shard_map/all_to_all | solution.py:176
  134.6 3.2 %copy-done.3 = bf16[128,16,2048]{2,1,0:T(8,128)(2,1)} copy-done((bf16[128,16,2048]{2,1,0:T(8,128)(2,1)}, bf16[128,16,2048]{2,1,0:T(8,128)(2,1)S(1)}, u32[]{:S(2)}) %copy-start.3) | copy-done | bytes 8388632
  137.8 0.0 copy-done.15
  137.8 8.6 %fusion.4 = f32[2048,768]{1,0:T(8,128)} fusion(bf16[2048,2048]{1,0:T(8,128)(2,1)S(1)} %bitcast.43, bf16[1,2048,768]{2,1,0:T(8,128)(2,1)S(1)} %copy-done.15), kind=kOutput, calls=%fused_computation.8 | convolution fusion | flops 6442450944 | bytes 17825792 | tf_op jit(solution)/shard_map/dot_general | solution.py:113
  146.4 0.0 copy-done
  146.4 21.3 %convolution_convert_fusion = bf16[2048,2048]{1,0:T(8,128)(2,1)} fusion(f32[2048,768]{1,0:T(8,128)} %fusion.4, bf16[2048,2048]{1,0:T(8,128)(2,1)} %bitcast.44, bf16[1,768,2048]{2,1,0:T(8,128)(2,1)S(1)} %copy-done, bf16[1,2048,768]{2,1,0:T(8,128)(2,1)} %param.26), kind=kOutput, calls=%fused_computation.2 | convolution fusion | flops 12896960512 | bytes 29360128 | tf_op jit(solution)/shard_map/dot_general | solution.py:116
  167.7 0.0 copy-start.10
  167.7 0.0 copy-start.8
  167.7 7.5 %all-to-all-start.1 = ((bf16[128,16,2048]{2,1,0:T(8,128)(2,1)}), bf16[128,16,2048]{2,1,0:T(8,128)(2,1)}, u32[]{:S(2)}, u32[]{:S(2)}) async-start(bf16[128,16,2048]{2,1,0:T(8,128)(2,1)} %bitcast.42), calls=%async_computation.1 | async-start | bytes 16777216 | tf_op jit(solution)/shard_map/all_to_all | solution.py:180
  175.2 0.0 copy-done.5
  175.2 0.0 copy-done.14
  175.2 0.0 copy-done.16
  175.2 0.4 fusion.19
  175.6 0.3 select_reduce_fusion
  176.0 0.1 copy.34
  176.0 0.1 reduce_max.9
  176.2 0.1 copy.35
  176.3 4.1 %fusion = f32[112,128,16]{1,2,0:T(8,128)S(1)} fusion(f32[112,8]{1,0:T(8,128)S(1)} %copy.35, pred[112,8,16]{2,1,0:T(8,128)(4,1)S(1)} %copy-done.8, pred[112,8,128]{2,1,0:T(8,128)(4,1)S(1)} %get-tuple-element.7), kind=kLoop, calls=%fused_computation.4 | loop fusion | flops 5275648 | bytes 1050112 | tf_op jit(solution)/shard_map/reduce_sum | solution.py:187
  180.4 0.7 copy.36
  181.1 1.1 fusion.11
  182.3 96.5 %all-to-all-done.1 = bf16[128,16,2048]{2,1,0:T(8,128)(2,1)} async-done(((bf16[128,16,2048]{2,1,0:T(8,128)(2,1)}), bf16[128,16,2048]{2,1,0:T(8,128)(2,1)}, u32[]{:S(2)}, u32[]{:S(2)}) %all-to-all-start.1) | async-done | bytes 8388640 | tf_op jit(solution)/shard_map/all_to_all | solution.py:180
  278.7 6.0 %fusion.7 = f32[224,2048]{1,0:T(8,128)S(1)} fusion(bf16[2048,2048]{1,0:T(8,128)(2,1)} %bitcast.14, bf16[112,2048]{0,1:T(8,128)(2,1)} %get-tuple-element.5, bf16[112,2048]{0,1:T(8,128)(2,1)} %get-tuple-element.6), kind=kOutput, calls=%fused_computation.14 | convolution fusion | flops 1880883200 | bytes 11141120 | tf_op jit(solution)/shard_map/dot_general | solution.py:191
  284.7 0.0 copy-done.6
  284.7 1.0 fusion.16
  (21 shorter events, 0.1 us)
Async XLA Ops:
  0.0 146.4 %copy-start = (bf16[1,768,2048]{2,1,0:T(8,128)(2,1)S(1)}, bf16[1,768,2048]{2,1,0:T(8,128)(2,1)}, u32[]{:S(2)}) copy-start(bf16[1,768,2048]{2,1,0:T(8,128)(2,1)} %param.27) | copy-start | bytes 9437188
  0.9 2.8 copy-start.9
  3.7 0.6 copy-start.7
  11.7 2.2 copy-start.2
  13.9 12.0 %copy-start.11 = (bf16[1,2048]{1,0:T(2,128)(2,1)S(1)}, bf16[1,2048]{1,0:T(2,128)(2,1)}, u32[]{:S(2)}) copy-start(bf16[1,2048]{1,0:T(2,128)(2,1)} %param.20) | copy-start | bytes 12292
  13.9 12.0 %copy-start.4 = (bf16[1,111,2048]{2,1,0:T(8,128)(2,1)S(1)}, bf16[1,111,2048]{2,1,0:T(8,128)(2,1)}, u32[]{:S(2)}) copy-start(bf16[1,111,2048]{2,1,0:T(8,128)(2,1)} %param.21) | copy-start | bytes 1363972
  13.9 12.3 %copy-start.12 = (f32[2048]{0:T(1024)S(1)}, f32[2048]{0:T(1024)}, u32[]{:S(2)}) copy-start(f32[2048]{0:T(1024)} %param.22) | copy-start | bytes 24580
  26.1 2.4 copy-start.13
  28.6 109.3 %copy-start.15 = (bf16[1,2048,768]{2,1,0:T(8,128)(2,1)S(1)}, bf16[1,2048,768]{2,1,0:T(8,128)(2,1)}, u32[]{:S(2)}) copy-start(bf16[1,2048,768]{2,1,0:T(8,128)(2,1)} %param.25) | copy-start | bytes 9437188
  134.6 3.2 %copy-start.3 = (bf16[128,16,2048]{2,1,0:T(8,128)(2,1)}, bf16[128,16,2048]{2,1,0:T(8,128)(2,1)S(1)}, u32[]{:S(2)}) copy-start(bf16[128,16,2048]{2,1,0:T(8,128)(2,1)S(1)} %all_to_all.10) | copy-start | bytes 25165828
  167.7 7.6 %copy-start.5 = (bf16[1,111,2048]{2,1,0:T(8,128)(2,1)S(1)}, bf16[1,111,2048]{2,1,0:T(8,128)(2,1)}, u32[]{:S(2)}) copy-start(bf16[1,111,2048]{2,1,0:T(8,128)(2,1)} %param.21) | copy-start | bytes 1363972
  167.7 7.6 %copy-start.14 = (f32[112]{0:T(128)S(1)}, f32[112]{0:T(128)}, u32[]{:S(2)}) copy-start(f32[112]{0:T(128)} %copy-done.13) | copy-start | bytes 1348
  167.7 7.6 %copy-start.16 = (bf16[2048,128]{1,0:T(8,128)(2,1)S(1)}, bf16[2048,128]{1,0:T(8,128)(2,1)}, u32[]{:S(2)}) copy-start(bf16[2048,128]{1,0:T(8,128)(2,1)} %param.23) | copy-start | bytes 1572868
  167.7 8.0 %copy-start.10 = (s32[112,8]{1,0:T(8,128)S(1)}, s32[112,8]{1,0:T(8,128)}, u32[]{:S(2)}) copy-start(s32[112,8]{1,0:T(8,128)} %copy-done.9) | copy-start | bytes 10756
  167.7 8.6 %copy-start.8 = (pred[112,8,16]{2,1,0:T(8,128)(4,1)S(1)}, pred[112,8,16]{2,1,0:T(8,128)(4,1)}, u32[]{:S(2)}) copy-start(pred[112,8,16]{2,1,0:T(8,128)(4,1)} %copy-done.7) | copy-start | bytes 43012
  167.7 111.0 %all-to-all-start.1 = ((bf16[128,16,2048]{2,1,0:T(8,128)(2,1)}), bf16[128,16,2048]{2,1,0:T(8,128)(2,1)}, u32[]{:S(2)}, u32[]{:S(2)}) async-start(bf16[128,16,2048]{2,1,0:T(8,128)(2,1)} %bitcast.42), calls=%async_computation.1 | async-start | bytes 16777216 | tf_op jit(solution)/shard_map/all_to_all | solution.py:180
  278.7 7.0 %copy-start.1 = (bf16[1,768,2048]{2,1,0:T(8,128)(2,1)S(1)}, bf16[1,768,2048]{2,1,0:T(8,128)(2,1)}, u32[]{:S(2)}) copy-start(bf16[1,768,2048]{2,1,0:T(8,128)(2,1)} %param.27) | copy-start | bytes 9437188
  278.7 6.0 %copy-start.6 = (bf16[1,111,2048]{2,1,0:T(8,128)(2,1)S(1)}, bf16[1,111,2048]{2,1,0:T(8,128)(2,1)}, u32[]{:S(2)}) copy-start(bf16[1,111,2048]{2,1,0:T(8,128)(2,1)} %param.21) | copy-start | bytes 1363972

commit v4 on v3

--- a/solution.py
+++ b/solution.py
@@ -109,12 +109,127 @@
     )
 
 
-def expert_block(slots, gate_weights, up_weights, down_weights):
-    gate_act = jnp.dot(slots, gate_weights[0], preferred_element_type=jnp.float32)
-    up_act = jnp.dot(slots, up_weights[0], preferred_element_type=jnp.float32)
-    inner_act = (gate_act / (1.0 + jnp.exp(-gate_act)) * up_act).astype(jnp.bfloat16)
-    result = jnp.dot(inner_act, down_weights[0], preferred_element_type=jnp.float32)
-    return result.astype(jnp.bfloat16)
+LANE = 256
+TILE = 256
+SLOT_STRIDE = 16
+
+
+def _wire_shape(width, used):
+    return ((width // LANE) * used, LANE)
+
+
+def dispatch_kernel(used, place_ref, rows_ref, out_ref, staged):
+    chunks = out_ref.shape[0]
+    pieces = rows_ref.shape[1] // LANE
+    for q in range(pieces):
+        staged[...] = jnp.dot(
+            place_ref[...], rows_ref[:, pl.ds(q * LANE, LANE)], preferred_element_type=jnp.float32
+        )
+
+        def put(e, carry, q=q):
+            start = pl.multiple_of(e * SLOT_STRIDE, SLOT_STRIDE)
+            out_ref[e, pl.ds(q * used, used), :] = staged[pl.ds(start, used), :].astype(
+                out_ref.dtype
+            )
+            return carry
+
+        lax.fori_loop(0, chunks, put, 0)
+
+
+def dispatch(place_t, rows, used):
+    slots = place_t.shape[0]
+    width = rows.shape[1]
+    chunks = slots // SLOT_STRIDE
+    return pl.pallas_call(
+        lambda *refs: dispatch_kernel(used, *refs),
+        out_shape=jax.ShapeDtypeStruct((chunks,) + _wire_shape(width, used), jnp.bfloat16),
+        in_specs=[pl.BlockSpec(memory_space=pltpu.VMEM)] * 2,
+        out_specs=pl.BlockSpec(memory_space=pltpu.VMEM),
+        scratch_shapes=[pltpu.VMEM((slots, LANE), jnp.float32)],
+        compiler_params=pltpu.CompilerParams(vmem_limit_bytes=48 * 1024 * 1024),
+    )(place_t, rows)
+
+
+def expert_kernel(x_ref, gate_ref, up_ref, down_ref, out_ref, rows_in, rows_out):
+    chunks, wire_rows, _ = x_ref.shape
+    width = gate_ref.shape[0]
+    pieces = width // LANE
+    used = wire_rows // pieces
+    group = TILE // SLOT_STRIDE
+    rows_in[...] = jnp.zeros(rows_in.shape, rows_in.dtype)
+
+    def tile(i, carry):
+        for jl in range(group):
+            j = i * group + jl
+            for q in range(pieces):
+                rows_in[pl.ds(jl * SLOT_STRIDE, used), pl.ds(q * LANE, LANE)] = x_ref[
+                    j, pl.ds(q * used, used), :
+                ]
+        rows = rows_in[...]
+        gate_act = jnp.dot(rows, gate_ref[...], preferred_element_type=jnp.float32)
+        up_act = jnp.dot(rows, up_ref[...], preferred_element_type=jnp.float32)
+        inner_act = (gate_act / (1.0 + jnp.exp(-gate_act)) * up_act).astype(jnp.bfloat16)
+        rows_out[...] = jnp.dot(
+            inner_act, down_ref[...], preferred_element_type=jnp.float32
+        ).astype(rows_out.dtype)
+        for jl in range(group):
+            j = i * group + jl
+            for q in range(pieces):
+                out_ref[j, pl.ds(q * used, used), :] = rows_out[
+                    pl.ds(jl * SLOT_STRIDE, used), pl.ds(q * LANE, LANE)
+                ]
+        return carry
+
+    lax.fori_loop(0, chunks // group, tile, 0)
+
+
+def expert_block(arrived, gate_weights, up_weights, down_weights):
+    width = gate_weights.shape[1]
+    return pl.pallas_call(
+        expert_kernel,
+        out_shape=jax.ShapeDtypeStruct(arrived.shape, jnp.bfloat16),
+        in_specs=[pl.BlockSpec(memory_space=pltpu.VMEM)] * 4,
+        out_specs=pl.BlockSpec(memory_space=pltpu.VMEM),
+        scratch_shapes=[
+            pltpu.VMEM((TILE, width), jnp.bfloat16),
+            pltpu.VMEM((TILE, width), jnp.bfloat16),
+        ],
+        compiler_params=pltpu.CompilerParams(vmem_limit_bytes=60 * 1024 * 1024),
+    )(arrived, gate_weights[0], up_weights[0], down_weights[0])
+
+
+def combine_kernel(ret_ref, mix_ref, hidden_ref, out_ref, rows):
+    chunks, wire_rows, _ = ret_ref.shape
+    width = rows.shape[1]
+    pieces = width // LANE
+    used = wire_rows // pieces
+    tokens = hidden_ref.shape[0]
+    rows[...] = jnp.zeros(rows.shape, rows.dtype)
+
+    def fill(e, carry):
+        start = pl.multiple_of(e * SLOT_STRIDE, SLOT_STRIDE)
+        for q in range(pieces):
+            rows[pl.ds(start, used), pl.ds(q * LANE, LANE)] = ret_ref[e, pl.ds(q * used, used), :]
+        return carry
+
+    lax.fori_loop(0, chunks, fill, 0)
+    both = jnp.dot(mix_ref[...], rows[...], preferred_element_type=jnp.float32)
+    out_ref[...] = (
+        hidden_ref[...].astype(jnp.float32) + both[:tokens] + both[tokens:]
+    ).astype(out_ref.dtype)
+
+
+def combine(returned, mix_both, hidden):
+    chunks = returned.shape[0]
+    width = hidden.shape[1]
+    return pl.pallas_call(
+        combine_kernel,
+        out_shape=jax.ShapeDtypeStruct(hidden.shape, jnp.bfloat16),
+        in_specs=[pl.BlockSpec(memory_space=pltpu.VMEM)] * 3,
+        out_specs=pl.BlockSpec(memory_space=pltpu.VMEM),
+        scratch_shapes=[pltpu.VMEM((chunks * SLOT_STRIDE, width), jnp.bfloat16)],
+        compiler_params=pltpu.CompilerParams(vmem_limit_bytes=48 * 1024 * 1024),
+    )(returned, mix_both, hidden)
 
 
 def body(
@@ -171,28 +286,15 @@
     rank_hot = slot_rank[..., None] == jnp.arange(capacity, dtype=jnp.int32)
     fills = one_hot[..., None] & rank_hot[:, :, None, :]
     place = jnp.any(fills, axis=1).reshape(tokens, experts * capacity).astype(jnp.bfloat16)
-    outgoing = jnp.einsum("ts,td->sd", place, normed, preferred_element_type=jnp.float32)
-    outgoing = outgoing.astype(jnp.bfloat16).reshape(experts, capacity, model_width)
+    outgoing = dispatch(place.T, normed, 14)
     arrived = lax.all_to_all(outgoing, ("kv", "blk"), split_axis=0, concat_axis=0, tiled=True)
-    processed = expert_block(
-        arrived.reshape(experts * capacity, model_width), expert_gate, expert_up, expert_down
-    )
-    returned = lax.all_to_all(
-        processed.reshape(experts, capacity, model_width),
-        ("kv", "blk"),
-        split_axis=0,
-        concat_axis=0,
-        tiled=True,
-    ).reshape(experts * capacity, model_width)
+    processed = expert_block(arrived, expert_gate, expert_up, expert_down)
+    returned = lax.all_to_all(processed, ("kv", "blk"), split_axis=0, concat_axis=0, tiled=True)
     mix = jnp.sum(jnp.where(fills, gate_probs[..., None, None], 0.0), axis=1)
     mix = mix.reshape(tokens, experts * capacity)
     mix_hi = mix.astype(jnp.bfloat16)
     mix_lo = (mix - mix_hi.astype(jnp.float32)).astype(jnp.bfloat16)
-    both = jnp.dot(
-        jnp.concatenate([mix_hi, mix_lo], axis=0), returned, preferred_element_type=jnp.float32
-    )
-    combined = both[:tokens] + both[tokens:]
-    layer_sum = (hidden_f + combined).astype(jnp.bfloat16)
+    layer_sum = combine(returned, jnp.concatenate([mix_hi, mix_lo], axis=0), hidden)
     return layer_sum[None]
 
 

time: 288 us -> 272 us (0.944)
  Pallas kernels: 12 us -> 67.5 us
  matrix products: 38.6 us -> 0.27 us
  waiting for transfers between devices: 96.5 us -> 84.5 us
  blocking collectives: 106 us -> 95 us
  local copies, waits for them, and re-layouts: 11 us -> 6.4 us
    pallas_call x0 -> x3, Pallas kernels: none -> 55.6 us  [the longest x1 30.8 us: expert_block(): pl.pallas_call(expert_kernel, out_shape=jax.ShapeDtypeStruct(arrived.shap...]
    dot_general x4 -> x0, matrix products: 38.3 us -> none  [the longest x1 21.3 us: expert_block(): jnp.dot(inner_act, down_weights[0], preferred_element_type=jnp.float32)]
    all_to_all x1, waiting for transfers between devices: 96.5 us -> 84.5 us  [body(): lax.all_to_all(processed, ('kv', 'blk'), split_axis=0, concat_axis=0, til...]
    all_to_all x1, blocking collectives: 106 us -> 95 us  [body(): lax.all_to_all(outgoing, ('kv', 'blk'), split_axis=0, concat_axis=0, tile...]
    unnamed x35 -> x11, local copies, waits for them, and re-layouts: 6.77 us -> 2.91 us
where the time goes in v4:
time: 272 us; the launch traced here: 271 us
  blocking collectives  95 us (35%)
  waiting for transfers between devices  84.5 us (31%)
  Pallas kernels  67.5 us (25%)
  other arithmetic  11.6 us (4%)
  local copies, waits for them, and re-layouts  6.4 us (2%)
  starting transfers between devices  6 us (2%)
    all_to_all x1, blocking collectives, body(): lax.all_to_all(outgoing, ('kv', 'blk'), split_axis=0, concat_axis=0, tile...  95 us
    all_to_all x1, waiting for transfers between devices, body(): lax.all_to_all(processed, ('kv', 'blk'), split_axis=0, concat_axis=0, til...  84.5 us
    pallas_call x1, Pallas kernels, expert_block(): pl.pallas_call(expert_kernel, out_shape=jax.ShapeDtypeStruct(arrived.shap...  30.8 us
    pallas_call x1, Pallas kernels, dispatch(): pl.pallas_call(lambda *refs: dispatch_kernel(used, *refs), out_shape=jax....  16.9 us
    pallas_call x1, Pallas kernels, attend_reduce(): pl.pallas_call(lambda *refs: attend_reduce_kernel(n_kv, *refs), out_shape...  12 us
    pallas_call x1, Pallas kernels, combine(): pl.pallas_call(combine_kernel, out_shape=jax.ShapeDtypeStruct(hidden.shap...  7.87 us
    all_to_all x1, starting transfers between devices, body(): lax.all_to_all(processed, ('kv', 'blk'), split_axis=0, concat_axis=0, til...  6 us
  transfers between devices with their start and end apart: 1, of which 1 were waited for; matrix products, arithmetic and copies ran while one was open for 2% of the time, Pallas kernels for 0%

profile of v4, /device:TPU:2, one launch (start us, length us, event | category | flops | bytes accessed | tf_op | source)
XLA Modules:
  0.0 271.5 jit_solution(14112277482961986602)
XLA Ops:
  0.0 0.0 copy-start
  0.0 0.8 copy.34
  0.8 0.3 iota_compare_fusion.1
  1.1 0.2 reduce_window_sum.11
  1.3 2.1 select_reduce_fusion.1
  3.4 0.2 iota_compare_fusion
  3.6 2.8 %and_reduce_fusion = pred[112,128,16]{1,2,0:T(8,128)(4,1)S(1)} fusion(pred[112,8,16]{2,1,0:T(8,128)(4,1)S(1)} %iota_compare_fusion, pred[112,8,128]{2,1,0:T(8,128)(4,1)S(1)} %get-tuple-element.9), kind=kLoop, calls=%fused_computation.1 | loop fusion | flops 3440640 | bytes 358400 | tf_op jit(solution)/shard_map/reduce_or | solution.py:288
  6.4 0.1 transpose.24
  6.5 0.7 copy.35
  7.1 0.7 copy.47
  7.8 0.7 subtract_bitcast_fusion
  8.6 0.1 copy.36.refs_3_
  8.7 0.7 copy.37.refs_4_
  9.4 0.0 copy-start.1
  9.4 2.2 copy-done.1
  11.6 0.0 copy-start.4
  11.6 0.0 copy-start.2
  11.6 0.0 copy-start.3
  11.6 12.0 %shard_map.136 = f32[1,2048]{1,0:T(1,128)S(1)} custom-call(bf16[4,8,128]{2,1,0:T(8,128)(2,1)S(1)} %bitcast.23, bf16[4,4096,128]{2,1,0:T(8,128)(2,1)S(1)} %bitcast.21, bf16[4,4096,128]{2,1,0:T(8,128)(2,1)} %bitcast.24, s32[4,1]{1,0:T(4,128)S(1)} %copy.36.refs_3_, f32[8,1]{1,0:T(8,128)S(1)} %copy.37.refs_4_, bf16[1024,2048]{1,0:T(8,128)(2,1)} %refs_5_.1), custom_call_target="tpu_custom_call" | custom-call | tf_op jit(solution)/shard_map/pallas_call | solution.py:87
  23.6 0.0 copy-done.4
  23.6 0.0 copy-done.2
  23.6 0.3 fusion.1
  23.9 0.0 copy-done.3
  23.9 0.2 fusion.3.refs_1_
  24.1 16.9 %shard_map.137 = bf16[128,112,256]{2,1,0:T(8,128)(2,1)} custom-call(bf16[2048,112]{1,0:T(8,128)(2,1)S(1)} %bitcast.22, bf16[112,2048]{1,0:T(8,128)(2,1)S(1)} %fusion.3.refs_1_), custom_call_target="tpu_custom_call" | custom-call | tf_op jit(solution)/shard_map/pallas_call | solution.py:143
  41.0 95.0 %all_to_all.10.x_ref = bf16[128,112,256]{2,1,0:T(8,128)(2,1)} all-to-all(bf16[128,112,256]{2,1,0:T(8,128)(2,1)} %shard_map.137), channel_id=1, replica_groups=mesh['kv'=4,'blk'=32] {'kv','blk'}, dimensions={0} | all-to-all | bytes 14680064 | tf_op jit(solution)/shard_map/all_to_all | solution.py:290
  136.0 30.8 %shard_map.138 = bf16[128,112,256]{2,1,0:T(8,128)(2,1)} custom-call(bf16[128,112,256]{2,1,0:T(8,128)(2,1)} %all_to_all.10.x_ref, bf16[2048,768]{1,0:T(8,128)(2,1)} %bitcast.26, bf16[2048,768]{1,0:T(8,128)(2,1)} %bitcast.27, bf16[768,2048]{1,0:T(8,128)(2,1)} %bitcast.28), custom_call_target="tpu_custom_call" | custom-call | tf_op jit(solution)/shard_map/pallas_call | solution.py:188
  166.8 6.0 %all-to-all-start.1 = ((bf16[128,112,256]{2,1,0:T(8,128)(2,1)}), bf16[128,112,256]{2,1,0:T(8,128)(2,1)}, u32[]{:S(2)}, u32[]{:S(2)}) async-start(bf16[128,112,256]{2,1,0:T(8,128)(2,1)} %shard_map.138), calls=%async_computation.1 | async-start | bytes 14680064 | tf_op jit(solution)/shard_map/all_to_all | solution.py:292
  172.8 0.0 copy-done
  172.8 0.3 fusion.7
  173.1 0.3 select_reduce_fusion
  173.4 0.1 copy.39
  173.5 0.1 reduce_max.9
  173.6 0.1 copy.40
  173.7 4.1 %fusion = f32[112,128,16]{1,2,0:T(8,128)S(1)} fusion(f32[112,8]{1,0:T(8,128)S(1)} %copy.40, pred[112,8,16]{2,1,0:T(8,128)(4,1)S(1)} %iota_compare_fusion, pred[112,8,128]{2,1,0:T(8,128)(4,1)S(1)} %get-tuple-element.9), kind=kLoop, calls=%fused_computation.2 | loop fusion | flops 5275648 | bytes 1050112 | tf_op jit(solution)/shard_map/reduce_sum | solution.py:293
  177.9 0.7 copy.41
  178.6 0.3 copy.42
  178.9 0.1 subtract_convert_fusion
  179.0 0.1 pad_maximum_fusion.mix_ref
  179.1 84.5 %all-to-all-done.1.ret_ref = bf16[128,112,256]{2,1,0:T(8,128)(2,1)} async-done(((bf16[128,112,256]{2,1,0:T(8,128)(2,1)}), bf16[128,112,256]{2,1,0:T(8,128)(2,1)}, u32[]{:S(2)}, u32[]{:S(2)}) %all-to-all-start.1) | async-done | bytes 7340064 | tf_op jit(solution)/shard_map/all_to_all | solution.py:292
  263.6 7.9 %shard_map.139 = bf16[112,2048]{1,0:T(8,128)(2,1)} custom-call(bf16[128,112,256]{2,1,0:T(8,128)(2,1)} %all-to-all-done.1.ret_ref, bf16[224,2048]{1,0:T(8,128)(2,1)S(1)} %pad_maximum_fusion.mix_ref, bf16[112,2048]{1,0:T(8,128)(2,1)S(1)} %get-tuple-element.8.hidden_ref), custom_call_target="tpu_custom_call" | custom-call | tf_op jit(solution)/shard_map/pallas_call | solution.py:225
  (6 shorter events, 0.1 us)
Async XLA Ops:
  0.0 172.8 %copy-start = (bf16[2048,128]{1,0:T(8,128)(2,1)S(1)}, bf16[2048,128]{1,0:T(8,128)(2,1)}, u32[]{:S(2)}) copy-start(bf16[2048,128]{1,0:T(8,128)(2,1)} %param.23) | copy-start | bytes 1572868
  9.4 2.2 copy-start.1
  11.6 12.0 %copy-start.4 = (bf16[1,2048]{1,0:T(2,128)(2,1)S(1)}, bf16[1,2048]{1,0:T(2,128)(2,1)}, u32[]{:S(2)}) copy-start(bf16[1,2048]{1,0:T(2,128)(2,1)} %param.20) | copy-start | bytes 12292
  11.6 12.0 %copy-start.2 = (bf16[1,111,2048]{2,1,0:T(8,128)(2,1)S(1)}, bf16[1,111,2048]{2,1,0:T(8,128)(2,1)}, u32[]{:S(2)}) copy-start(bf16[1,111,2048]{2,1,0:T(8,128)(2,1)} %param.21) | copy-start | bytes 1363972
  11.6 12.3 %copy-start.3 = (f32[2048]{0:T(1024)S(1)}, f32[2048]{0:T(1024)}, u32[]{:S(2)}) copy-start(f32[2048]{0:T(1024)} %param.22) | copy-start | bytes 24580
  166.8 96.8 %all-to-all-start.1 = ((bf16[128,112,256]{2,1,0:T(8,128)(2,1)}), bf16[128,112,256]{2,1,0:T(8,128)(2,1)}, u32[]{:S(2)}, u32[]{:S(2)}) async-start(bf16[128,112,256]{2,1,0:T(8,128)(2,1)} %shard_map.138), calls=%async_computation.1 | async-start | bytes 14680064 | tf_op jit(solution)/shard_map/all_to_all | solution.py:292

commit v5 on v4

--- a/solution.py
+++ b/solution.py
@@ -121,19 +121,22 @@
 def dispatch_kernel(used, place_ref, rows_ref, out_ref, staged):
     chunks = out_ref.shape[0]
     pieces = rows_ref.shape[1] // LANE
-    for q in range(pieces):
+    group = TILE // SLOT_STRIDE
+
+    def tile(i, carry):
+        start = pl.multiple_of(i * TILE, TILE)
         staged[...] = jnp.dot(
-            place_ref[...], rows_ref[:, pl.ds(q * LANE, LANE)], preferred_element_type=jnp.float32
-        )
-
-        def put(e, carry, q=q):
-            start = pl.multiple_of(e * SLOT_STRIDE, SLOT_STRIDE)
-            out_ref[e, pl.ds(q * used, used), :] = staged[pl.ds(start, used), :].astype(
-                out_ref.dtype
-            )
-            return carry
-
-        lax.fori_loop(0, chunks, put, 0)
+            place_ref[pl.ds(start, TILE), :], rows_ref[...], preferred_element_type=jnp.float32
+        ).astype(staged.dtype)
+        for jl in range(group):
+            j = i * group + jl
+            for q in range(pieces):
+                out_ref[j, pl.ds(q * used, used), :] = staged[
+                    pl.ds(jl * SLOT_STRIDE, used), pl.ds(q * LANE, LANE)
+                ]
+        return carry
+
+    lax.fori_loop(0, chunks // group, tile, 0)
 
 
 def dispatch(place_t, rows, used):
@@ -145,7 +148,7 @@
         out_shape=jax.ShapeDtypeStruct((chunks,) + _wire_shape(width, used), jnp.bfloat16),
         in_specs=[pl.BlockSpec(memory_space=pltpu.VMEM)] * 2,
         out_specs=pl.BlockSpec(memory_space=pltpu.VMEM),
-        scratch_shapes=[pltpu.VMEM((slots, LANE), jnp.float32)],
+        scratch_shapes=[pltpu.VMEM((TILE, width), jnp.bfloat16)],
         compiler_params=pltpu.CompilerParams(vmem_limit_bytes=48 * 1024 * 1024),
     )(place_t, rows)
 

time: 272 us -> 262 us (0.963)
  Pallas kernels: 67.5 us -> 57.9 us
    pallas_call x1, Pallas kernels: 16.9 us -> 7.3 us  [dispatch(): pl.pallas_call(lambda *refs: dispatch_kernel(used, *refs), out_shape=jax....]
where the time goes in v5:
time: 262 us
  blocking collectives  95 us (36%)
  waiting for transfers between devices  84.5 us (32%)
  Pallas kernels  57.9 us (22%)
  other arithmetic  11.6 us (4%)
  local copies, waits for them, and re-layouts  6.4 us (2%)
  starting transfers between devices  6.01 us (2%)
    all_to_all x1, blocking collectives, body(): lax.all_to_all(outgoing, ('kv', 'blk'), split_axis=0, concat_axis=0, tile...  95 us
    all_to_all x1, waiting for transfers between devices, body(): lax.all_to_all(processed, ('kv', 'blk'), split_axis=0, concat_axis=0, til...  84.5 us
    pallas_call x1, Pallas kernels, expert_block(): pl.pallas_call(expert_kernel, out_shape=jax.ShapeDtypeStruct(arrived.shap...  30.8 us
    pallas_call x1, Pallas kernels, attend_reduce(): pl.pallas_call(lambda *refs: attend_reduce_kernel(n_kv, *refs), out_shape...  12 us
    pallas_call x1, Pallas kernels, combine(): pl.pallas_call(combine_kernel, out_shape=jax.ShapeDtypeStruct(hidden.shap...  7.87 us
    pallas_call x1, Pallas kernels, dispatch(): pl.pallas_call(lambda *refs: dispatch_kernel(used, *refs), out_shape=jax....  7.3 us
    all_to_all x1, starting transfers between devices, body(): lax.all_to_all(processed, ('kv', 'blk'), split_axis=0, concat_axis=0, til...  6.01 us
  transfers between devices with their start and end apart: 1, of which 1 were waited for; matrix products, arithmetic and copies ran while one was open for 2% of the time, Pallas kernels for 0%

profile of v5, /device:TPU:2, one launch (start us, length us, event | category | flops | bytes accessed | tf_op | source)
XLA Modules:
  0.0 261.8 jit_solution(14025703644207061676)
XLA Ops:
  0.0 0.0 copy-start
  0.0 0.8 copy.34
  0.8 0.3 iota_compare_fusion.1
  1.1 0.2 reduce_window_sum.11
  1.3 2.1 select_reduce_fusion.1
  3.4 0.2 iota_compare_fusion
  3.6 2.8 %and_reduce_fusion = pred[112,128,16]{1,2,0:T(8,128)(4,1)S(1)} fusion(pred[112,8,16]{2,1,0:T(8,128)(4,1)S(1)} %iota_compare_fusion, pred[112,8,128]{2,1,0:T(8,128)(4,1)S(1)} %get-tuple-element.9), kind=kLoop, calls=%fused_computation.1 | loop fusion | flops 3440640 | bytes 358400 | tf_op jit(solution)/shard_map/reduce_or | solution.py:291
  6.4 0.1 transpose.24
  6.5 0.7 copy.35
  7.1 0.7 copy.47
  7.8 0.7 subtract_bitcast_fusion
  8.6 0.1 copy.36.refs_3_
  8.7 0.7 copy.37.refs_4_
  9.4 0.0 copy-start.1
  9.4 2.2 copy-done.1
  11.6 0.0 copy-start.4
  11.6 0.0 copy-start.2
  11.6 0.0 copy-start.3
  11.6 12.0 %shard_map.136 = f32[1,2048]{1,0:T(1,128)S(1)} custom-call(bf16[4,8,128]{2,1,0:T(8,128)(2,1)S(1)} %bitcast.23, bf16[4,4096,128]{2,1,0:T(8,128)(2,1)S(1)} %bitcast.21, bf16[4,4096,128]{2,1,0:T(8,128)(2,1)} %bitcast.24, s32[4,1]{1,0:T(4,128)S(1)} %copy.36.refs_3_, f32[8,1]{1,0:T(8,128)S(1)} %copy.37.refs_4_, bf16[1024,2048]{1,0:T(8,128)(2,1)} %refs_5_.1), custom_call_target="tpu_custom_call" | custom-call | tf_op jit(solution)/shard_map/pallas_call | solution.py:87
  23.6 0.0 copy-done.4
  23.6 0.0 copy-done.2
  23.6 0.3 fusion.1
  23.9 0.0 copy-done.3
  23.9 0.2 fusion.3.refs_1_
  24.1 7.3 %shard_map.137 = bf16[128,112,256]{2,1,0:T(8,128)(2,1)} custom-call(bf16[2048,112]{1,0:T(8,128)(2,1)S(1)} %bitcast.22, bf16[112,2048]{1,0:T(8,128)(2,1)S(1)} %fusion.3.refs_1_), custom_call_target="tpu_custom_call" | custom-call | tf_op jit(solution)/shard_map/pallas_call | solution.py:146
  31.4 95.0 %all_to_all.10.x_ref = bf16[128,112,256]{2,1,0:T(8,128)(2,1)} all-to-all(bf16[128,112,256]{2,1,0:T(8,128)(2,1)} %shard_map.137), channel_id=1, replica_groups=mesh['kv'=4,'blk'=32] {'kv','blk'}, dimensions={0} | all-to-all | bytes 14680064 | tf_op jit(solution)/shard_map/all_to_all | solution.py:293
  126.4 30.8 %shard_map.138 = bf16[128,112,256]{2,1,0:T(8,128)(2,1)} custom-call(bf16[128,112,256]{2,1,0:T(8,128)(2,1)} %all_to_all.10.x_ref, bf16[2048,768]{1,0:T(8,128)(2,1)} %bitcast.26, bf16[2048,768]{1,0:T(8,128)(2,1)} %bitcast.27, bf16[768,2048]{1,0:T(8,128)(2,1)} %bitcast.28), custom_call_target="tpu_custom_call" | custom-call | tf_op jit(solution)/shard_map/pallas_call | solution.py:191
  157.1 6.0 %all-to-all-start.1 = ((bf16[128,112,256]{2,1,0:T(8,128)(2,1)}), bf16[128,112,256]{2,1,0:T(8,128)(2,1)}, u32[]{:S(2)}, u32[]{:S(2)}) async-start(bf16[128,112,256]{2,1,0:T(8,128)(2,1)} %shard_map.138), calls=%async_computation.1 | async-start | bytes 14680064 | tf_op jit(solution)/shard_map/all_to_all | solution.py:295
  163.1 0.0 copy-done
  163.2 0.3 fusion.7
  163.4 0.3 select_reduce_fusion
  163.8 0.1 copy.39
  163.8 0.1 reduce_max.9
  164.0 0.1 copy.40
  164.1 4.1 %fusion = f32[112,128,16]{1,2,0:T(8,128)S(1)} fusion(f32[112,8]{1,0:T(8,128)S(1)} %copy.40, pred[112,8,16]{2,1,0:T(8,128)(4,1)S(1)} %iota_compare_fusion, pred[112,8,128]{2,1,0:T(8,128)(4,1)S(1)} %get-tuple-element.9), kind=kLoop, calls=%fused_computation.2 | loop fusion | flops 5275648 | bytes 1050112 | tf_op jit(solution)/shard_map/reduce_sum | solution.py:296
  168.2 0.7 copy.41
  168.9 0.3 copy.42
  169.3 0.1 subtract_convert_fusion
  169.4 0.1 pad_maximum_fusion.mix_ref
  169.5 84.5 %all-to-all-done.1.ret_ref = bf16[128,112,256]{2,1,0:T(8,128)(2,1)} async-done(((bf16[128,112,256]{2,1,0:T(8,128)(2,1)}), bf16[128,112,256]{2,1,0:T(8,128)(2,1)}, u32[]{:S(2)}, u32[]{:S(2)}) %all-to-all-start.1) | async-done | bytes 7340064 | tf_op jit(solution)/shard_map/all_to_all | solution.py:295
  254.0 7.9 %shard_map.139 = bf16[112,2048]{1,0:T(8,128)(2,1)} custom-call(bf16[128,112,256]{2,1,0:T(8,128)(2,1)} %all-to-all-done.1.ret_ref, bf16[224,2048]{1,0:T(8,128)(2,1)S(1)} %pad_maximum_fusion.mix_ref, bf16[112,2048]{1,0:T(8,128)(2,1)S(1)} %get-tuple-element.8.hidden_ref), custom_call_target="tpu_custom_call" | custom-call | tf_op jit(solution)/shard_map/pallas_call | solution.py:228
  (6 shorter events, 0.1 us)
Async XLA Ops:
  0.0 163.2 %copy-start = (bf16[2048,128]{1,0:T(8,128)(2,1)S(1)}, bf16[2048,128]{1,0:T(8,128)(2,1)}, u32[]{:S(2)}) copy-start(bf16[2048,128]{1,0:T(8,128)(2,1)} %param.23) | copy-start | bytes 1572868
  9.4 2.2 copy-start.1
  11.6 12.0 %copy-start.4 = (bf16[1,2048]{1,0:T(2,128)(2,1)S(1)}, bf16[1,2048]{1,0:T(2,128)(2,1)}, u32[]{:S(2)}) copy-start(bf16[1,2048]{1,0:T(2,128)(2,1)} %param.20) | copy-start | bytes 12292
  11.6 12.0 %copy-start.2 = (bf16[1,111,2048]{2,1,0:T(8,128)(2,1)S(1)}, bf16[1,111,2048]{2,1,0:T(8,128)(2,1)}, u32[]{:S(2)}) copy-start(bf16[1,111,2048]{2,1,0:T(8,128)(2,1)} %param.21) | copy-start | bytes 1363972
  11.6 12.3 %copy-start.3 = (f32[2048]{0:T(1024)S(1)}, f32[2048]{0:T(1024)}, u32[]{:S(2)}) copy-start(f32[2048]{0:T(1024)} %param.22) | copy-start | bytes 24580
  157.1 96.8 %all-to-all-start.1 = ((bf16[128,112,256]{2,1,0:T(8,128)(2,1)}), bf16[128,112,256]{2,1,0:T(8,128)(2,1)}, u32[]{:S(2)}, u32[]{:S(2)}) async-start(bf16[128,112,256]{2,1,0:T(8,128)(2,1)} %shard_map.138), calls=%async_computation.1 | async-start | bytes 14680064 | tf_op jit(solution)/shard_map/all_to_all | solution.py:295

commit v6 on v5

--- a/solution.py
+++ b/solution.py
@@ -110,8 +110,7 @@
 
 
 LANE = 256
-TILE = 256
-SLOT_STRIDE = 16
+GROUP = 16
 
 
 def _wire_shape(width, used):
@@ -121,36 +120,43 @@
 def dispatch_kernel(used, place_ref, rows_ref, out_ref, staged):
     chunks = out_ref.shape[0]
     pieces = rows_ref.shape[1] // LANE
-    group = TILE // SLOT_STRIDE
+    tile_rows = GROUP * used
 
     def tile(i, carry):
-        start = pl.multiple_of(i * TILE, TILE)
         staged[...] = jnp.dot(
-            place_ref[pl.ds(start, TILE), :], rows_ref[...], preferred_element_type=jnp.float32
+            place_ref[i], rows_ref[...], preferred_element_type=jnp.float32
         ).astype(staged.dtype)
-        for jl in range(group):
-            j = i * group + jl
+        for jl in range(GROUP):
+            j = i * GROUP + jl
             for q in range(pieces):
                 out_ref[j, pl.ds(q * used, used), :] = staged[
-                    pl.ds(jl * SLOT_STRIDE, used), pl.ds(q * LANE, LANE)
+                    pl.ds(jl * used, used), pl.ds(q * LANE, LANE)
                 ]
         return carry
 
-    lax.fori_loop(0, chunks // group, tile, 0)
+    lax.fori_loop(0, chunks // GROUP, tile, 0)
 
 
 def dispatch(place_t, rows, used):
-    slots = place_t.shape[0]
+    tiles, tile_rows, _ = place_t.shape
     width = rows.shape[1]
-    chunks = slots // SLOT_STRIDE
+    chunks = tiles * GROUP
     return pl.pallas_call(
         lambda *refs: dispatch_kernel(used, *refs),
         out_shape=jax.ShapeDtypeStruct((chunks,) + _wire_shape(width, used), jnp.bfloat16),
         in_specs=[pl.BlockSpec(memory_space=pltpu.VMEM)] * 2,
         out_specs=pl.BlockSpec(memory_space=pltpu.VMEM),
-        scratch_shapes=[pltpu.VMEM((TILE, width), jnp.bfloat16)],
+        scratch_shapes=[pltpu.VMEM((tile_rows, width), jnp.bfloat16)],
         compiler_params=pltpu.CompilerParams(vmem_limit_bytes=48 * 1024 * 1024),
     )(place_t, rows)
+
+
+def _gather_tile(i, used, src_ref, dst):
+    pieces = dst.shape[1] // LANE
+    for jl in range(GROUP):
+        j = i * GROUP + jl
+        for q in range(pieces):
+            dst[pl.ds(jl * used, used), pl.ds(q * LANE, LANE)] = src_ref[j, pl.ds(q * used, used), :]
 
 
 def expert_kernel(x_ref, gate_ref, up_ref, down_ref, out_ref, rows_in, rows_out):
@@ -158,16 +164,9 @@
     width = gate_ref.shape[0]
     pieces = width // LANE
     used = wire_rows // pieces
-    group = TILE // SLOT_STRIDE
-    rows_in[...] = jnp.zeros(rows_in.shape, rows_in.dtype)
 
     def tile(i, carry):
-        for jl in range(group):
-            j = i * group + jl
-            for q in range(pieces):
-                rows_in[pl.ds(jl * SLOT_STRIDE, used), pl.ds(q * LANE, LANE)] = x_ref[
-                    j, pl.ds(q * used, used), :
-                ]
+        _gather_tile(i, used, x_ref, rows_in)
         rows = rows_in[...]
         gate_act = jnp.dot(rows, gate_ref[...], preferred_element_type=jnp.float32)
         up_act = jnp.dot(rows, up_ref[...], preferred_element_type=jnp.float32)
@@ -175,62 +174,66 @@
         rows_out[...] = jnp.dot(
             inner_act, down_ref[...], preferred_element_type=jnp.float32
         ).astype(rows_out.dtype)
-        for jl in range(group):
-            j = i * group + jl
+        for jl in range(GROUP):
+            j = i * GROUP + jl
             for q in range(pieces):
                 out_ref[j, pl.ds(q * used, used), :] = rows_out[
-                    pl.ds(jl * SLOT_STRIDE, used), pl.ds(q * LANE, LANE)
+                    pl.ds(jl * used, used), pl.ds(q * LANE, LANE)
                 ]
         return carry
 
-    lax.fori_loop(0, chunks // group, tile, 0)
+    lax.fori_loop(0, chunks // GROUP, tile, 0)
 
 
 def expert_block(arrived, gate_weights, up_weights, down_weights):
+    chunks, wire_rows, _ = arrived.shape
     width = gate_weights.shape[1]
+    used = wire_rows // (width // LANE)
     return pl.pallas_call(
         expert_kernel,
         out_shape=jax.ShapeDtypeStruct(arrived.shape, jnp.bfloat16),
         in_specs=[pl.BlockSpec(memory_space=pltpu.VMEM)] * 4,
         out_specs=pl.BlockSpec(memory_space=pltpu.VMEM),
         scratch_shapes=[
-            pltpu.VMEM((TILE, width), jnp.bfloat16),
-            pltpu.VMEM((TILE, width), jnp.bfloat16),
+            pltpu.VMEM((GROUP * used, width), jnp.bfloat16),
+            pltpu.VMEM((GROUP * used, width), jnp.bfloat16),
         ],
         compiler_params=pltpu.CompilerParams(vmem_limit_bytes=60 * 1024 * 1024),
     )(arrived, gate_weights[0], up_weights[0], down_weights[0])
 
 
-def combine_kernel(ret_ref, mix_ref, hidden_ref, out_ref, rows):
+def combine_kernel(ret_ref, mix_ref, hidden_ref, out_ref, rows, total):
     chunks, wire_rows, _ = ret_ref.shape
     width = rows.shape[1]
-    pieces = width // LANE
-    used = wire_rows // pieces
+    used = wire_rows // (width // LANE)
     tokens = hidden_ref.shape[0]
-    rows[...] = jnp.zeros(rows.shape, rows.dtype)
-
-    def fill(e, carry):
-        start = pl.multiple_of(e * SLOT_STRIDE, SLOT_STRIDE)
-        for q in range(pieces):
-            rows[pl.ds(start, used), pl.ds(q * LANE, LANE)] = ret_ref[e, pl.ds(q * used, used), :]
+    total[...] = jnp.zeros(total.shape, total.dtype)
+
+    def tile(i, carry):
+        _gather_tile(i, used, ret_ref, rows)
+        total[...] += jnp.dot(mix_ref[i], rows[...], preferred_element_type=jnp.float32)
         return carry
 
-    lax.fori_loop(0, chunks, fill, 0)
-    both = jnp.dot(mix_ref[...], rows[...], preferred_element_type=jnp.float32)
+    lax.fori_loop(0, chunks // GROUP, tile, 0)
+    both = total[...]
     out_ref[...] = (
         hidden_ref[...].astype(jnp.float32) + both[:tokens] + both[tokens:]
     ).astype(out_ref.dtype)
 
 
 def combine(returned, mix_both, hidden):
-    chunks = returned.shape[0]
+    chunks, wire_rows, _ = returned.shape
     width = hidden.shape[1]
+    used = wire_rows // (width // LANE)
     return pl.pallas_call(
         combine_kernel,
         out_shape=jax.ShapeDtypeStruct(hidden.shape, jnp.bfloat16),
         in_specs=[pl.BlockSpec(memory_space=pltpu.VMEM)] * 3,
         out_specs=pl.BlockSpec(memory_space=pltpu.VMEM),
-        scratch_shapes=[pltpu.VMEM((chunks * SLOT_STRIDE, width), jnp.bfloat16)],
+        scratch_shapes=[
+            pltpu.VMEM((GROUP * used, width), jnp.bfloat16),
+            pltpu.VMEM((mix_both.shape[1], width), jnp.float32),
+        ],
         compiler_params=pltpu.CompilerParams(vmem_limit_bytes=48 * 1024 * 1024),
     )(returned, mix_both, hidden)
 
@@ -278,7 +281,7 @@
     chosen_ids = routes[0]
     tokens, top_k = chosen_ids.shape
     model_width = hidden.shape[1]
-    capacity = 16
+    capacity = 14
     logits = jnp.dot(normed, router, preferred_element_type=jnp.float32)
     one_hot = chosen_ids[..., None] == jnp.arange(experts, dtype=jnp.int32)
     chosen = jnp.sum(jnp.where(one_hot, logits[:, None, :], 0.0), axis=2)
@@ -289,7 +292,10 @@
     rank_hot = slot_rank[..., None] == jnp.arange(capacity, dtype=jnp.int32)
     fills = one_hot[..., None] & rank_hot[:, :, None, :]
     place = jnp.any(fills, axis=1).reshape(tokens, experts * capacity).astype(jnp.bfloat16)
-    outgoing = dispatch(place.T, normed, 14)
+    tiles = experts // GROUP
+    tile_rows = GROUP * capacity
+    place_t = place.T.reshape(tiles, tile_rows, tokens)
+    outgoing = dispatch(place_t, normed, capacity)
     arrived = lax.all_to_all(outgoing, ("kv", "blk"), split_axis=0, concat_axis=0, tiled=True)
     processed = expert_block(arrived, expert_gate, expert_up, expert_down)
     returned = lax.all_to_all(processed, ("kv", "blk"), split_axis=0, concat_axis=0, tiled=True)
@@ -297,7 +303,9 @@
     mix = mix.reshape(tokens, experts * capacity)
     mix_hi = mix.astype(jnp.bfloat16)
     mix_lo = (mix - mix_hi.astype(jnp.float32)).astype(jnp.bfloat16)
-    layer_sum = combine(returned, jnp.concatenate([mix_hi, mix_lo], axis=0), hidden)
+    mix_both = jnp.concatenate([mix_hi, mix_lo], axis=0)
+    mix_tiles = mix_both.reshape(2 * tokens, tiles, tile_rows).transpose(1, 0, 2)
+    layer_sum = combine(returned, mix_tiles, hidden)
     return layer_sum[None]
 
 

time: 262 us -> 256 us (0.977)
  Pallas kernels: 57.9 us -> 54.3 us
    pallas_call x1, Pallas kernels: 30.8 us -> 28 us  [expert_block(): pl.pallas_call(expert_kernel, out_shape=jax.ShapeDtypeStruct(arrived.shap...]
where the time goes in v6:
time: 256 us
  blocking collectives  95 us (37%)
  waiting for transfers between devices  85.4 us (33%)
  Pallas kernels  54.3 us (21%)
  other arithmetic  9.71 us (4%)
  starting transfers between devices  6.01 us (2%)
  local copies, waits for them, and re-layouts  5.07 us (2%)
    all_to_all x1, blocking collectives, body(): lax.all_to_all(outgoing, ('kv', 'blk'), split_axis=0, concat_axis=0, tile...  95 us
    all_to_all x1, waiting for transfers between devices, body(): lax.all_to_all(processed, ('kv', 'blk'), split_axis=0, concat_axis=0, til...  85.4 us
    pallas_call x1, Pallas kernels, expert_block(): pl.pallas_call(expert_kernel, out_shape=jax.ShapeDtypeStruct(arrived.shap...  28 us
    pallas_call x1, Pallas kernels, attend_reduce(): pl.pallas_call(lambda *refs: attend_reduce_kernel(n_kv, *refs), out_shape...  12 us
    pallas_call x1, Pallas kernels, combine(): pl.pallas_call(combine_kernel, out_shape=jax.ShapeDtypeStruct(hidden.shap...  7.57 us
    pallas_call x1, Pallas kernels, dispatch(): pl.pallas_call(lambda *refs: dispatch_kernel(used, *refs), out_shape=jax....  6.77 us
    all_to_all x1, starting transfers between devices, body(): lax.all_to_all(processed, ('kv', 'blk'), split_axis=0, concat_axis=0, til...  6.01 us
  transfers between devices with their start and end apart: 1, of which 1 were waited for; matrix products, arithmetic and copies ran while one was open for 2% of the time, Pallas kernels for 0%

profile of v6, /device:TPU:2, one launch (start us, length us, event | category | flops | bytes accessed | tf_op | source)
XLA Modules:
  0.0 256.1 jit_solution(15569371507715519821)
XLA Ops:
  0.0 0.0 copy-start
  0.0 0.0 copy-start.5
  0.0 0.0 copy-start.7
  0.0 0.0 copy-start.6
  0.0 0.8 copy.34
  0.9 0.3 iota_compare_fusion.1
  1.1 0.2 reduce_window_sum.11
  1.3 2.1 select_reduce_fusion.1
  3.4 0.1 iota_compare_fusion
  3.5 2.6 %and_reduce_fusion = pred[112,128,14]{1,2,0:T(8,128)(4,1)S(1)} fusion(pred[112,8,14]{1,2,0:T(8,128)(4,1)S(1)} %iota_compare_fusion, pred[112,8,128]{2,1,0:T(8,128)(4,1)S(1)} %get-tuple-element.9), kind=kLoop, calls=%fused_computation.1 | loop fusion | flops 3010560 | bytes 327936 | tf_op jit(solution)/shard_map/reduce_or | solution.py:294
  6.2 0.1 copy_convert_fusion
  6.3 0.4 copy.36
  6.7 0.2 reshape.100
  6.9 0.0 copy-done.5
  6.9 0.0 copy-done.7
  6.9 0.1 subtract_bitcast_fusion
  7.0 0.1 copy.37.refs_3_
  7.1 0.0 copy-done.6
  7.1 0.1 copy.38.refs_4_
  7.2 0.0 copy-start.1
  7.2 2.2 copy-done.1
  9.4 0.0 copy-start.4
  9.4 0.0 copy-start.2
  9.4 0.0 copy-start.3
  9.4 12.0 %shard_map.136 = f32[1,2048]{1,0:T(1,128)S(1)} custom-call(bf16[4,8,128]{2,1,0:T(8,128)(2,1)S(1)} %bitcast.28, bf16[4,4096,128]{2,1,0:T(8,128)(2,1)S(1)} %bitcast.26, bf16[4,4096,128]{2,1,0:T(8,128)(2,1)} %bitcast.29, s32[4,1]{1,0:T(4,128)S(1)} %copy.37.refs_3_, f32[8,1]{1,0:T(8,128)S(1)} %copy.38.refs_4_, bf16[1024,2048]{1,0:T(8,128)(2,1)} %refs_5_.1), custom_call_target="tpu_custom_call" | custom-call | tf_op jit(solution)/shard_map/pallas_call | solution.py:87
  21.4 0.0 copy-done.4
  21.4 0.0 copy-done.2
  21.4 0.3 fusion.1
  21.7 0.0 copy-done.3
  21.7 0.2 fusion.3.refs_1_
  21.9 6.8 %shard_map.137 = bf16[128,112,256]{2,1,0:T(8,128)(2,1)} custom-call(bf16[8,224,112]{2,1,0:T(8,128)(2,1)S(1)} %bitcast.27, bf16[112,2048]{1,0:T(8,128)(2,1)S(1)} %fusion.3.refs_1_), custom_call_target="tpu_custom_call" | custom-call | tf_op jit(solution)/shard_map/pallas_call | solution.py:144
  28.6 95.0 %all_to_all.10.x_ref = bf16[128,112,256]{2,1,0:T(8,128)(2,1)} all-to-all(bf16[128,112,256]{2,1,0:T(8,128)(2,1)} %shard_map.137), channel_id=1, replica_groups=mesh['kv'=4,'blk'=32] {'kv','blk'}, dimensions={0} | all-to-all | bytes 14680064 | tf_op jit(solution)/shard_map/all_to_all | solution.py:299
  123.6 28.0 %shard_map.138 = bf16[128,112,256]{2,1,0:T(8,128)(2,1)} custom-call(bf16[128,112,256]{2,1,0:T(8,128)(2,1)} %all_to_all.10.x_ref, bf16[2048,768]{1,0:T(8,128)(2,1)} %bitcast.30, bf16[2048,768]{1,0:T(8,128)(2,1)} %bitcast.31, bf16[768,2048]{1,0:T(8,128)(2,1)} %bitcast.32), custom_call_target="tpu_custom_call" | custom-call | tf_op jit(solution)/shard_map/pallas_call | solution.py:192
  151.7 6.0 %all-to-all-start.1 = ((bf16[128,112,256]{2,1,0:T(8,128)(2,1)}), bf16[128,112,256]{2,1,0:T(8,128)(2,1)}, u32[]{:S(2)}, u32[]{:S(2)}) async-start(bf16[128,112,256]{2,1,0:T(8,128)(2,1)} %shard_map.138), calls=%async_computation.1 | async-start | bytes 14680064 | tf_op jit(solution)/shard_map/all_to_all | solution.py:301
  157.7 0.0 copy-done
  157.7 0.3 fusion.7
  158.0 0.3 select_reduce_fusion
  158.3 0.1 copy.40
  158.4 0.1 reduce_max.9
  158.5 0.1 copy.41
  158.6 3.1 %fusion = f32[112,128,14]{1,2,0:T(8,128)S(1)} fusion(f32[112,8]{1,0:T(8,128)S(1)} %copy.41, pred[112,8,14]{1,2,0:T(8,128)(4,1)S(1)} %iota_compare_fusion, pred[112,8,128]{2,1,0:T(8,128)(4,1)S(1)} %get-tuple-element.9), kind=kLoop, calls=%fused_computation.2 | loop fusion | flops 4616192 | bytes 933632 | tf_op jit(solution)/shard_map/reduce_sum | solution.py:302
  161.7 0.7 copy.42
  162.4 0.1 reshape.95
  162.5 0.3 copy.43
  162.8 0.1 subtract_convert_fusion
  162.9 0.2 maximum_bitcast_fusion.mix_ref
  163.1 85.4 %all-to-all-done.1.ret_ref = bf16[128,112,256]{2,1,0:T(8,128)(2,1)} async-done(((bf16[128,112,256]{2,1,0:T(8,128)(2,1)}), bf16[128,112,256]{2,1,0:T(8,128)(2,1)}, u32[]{:S(2)}, u32[]{:S(2)}) %all-to-all-start.1) | async-done | bytes 7340064 | tf_op jit(solution)/shard_map/all_to_all | solution.py:301
  248.5 7.6 %shard_map.139 = bf16[112,2048]{1,0:T(8,128)(2,1)} custom-call(bf16[128,112,256]{2,1,0:T(8,128)(2,1)} %all-to-all-done.1.ret_ref, bf16[8,224,224]{2,1,0:T(8,128)(2,1)S(1)} %maximum_bitcast_fusion.mix_ref, bf16[112,2048]{1,0:T(8,128)(2,1)S(1)} %get-tuple-element.8.hidden_ref), custom_call_target="tpu_custom_call" | custom-call | tf_op jit(solution)/shard_map/pallas_call | solution.py:228
  (7 shorter events, 0.1 us)
Async XLA Ops:
  0.0 157.7 %copy-start = (bf16[2048,128]{1,0:T(8,128)(2,1)S(1)}, bf16[2048,128]{1,0:T(8,128)(2,1)}, u32[]{:S(2)}) copy-start(bf16[2048,128]{1,0:T(8,128)(2,1)} %param.23) | copy-start | bytes 1572868
  0.0 6.9 %copy-start.5 = (bf16[4,1024]{1,0:T(4,128)(2,1)S(1)}, bf16[4,1024]{1,0:T(4,128)(2,1)}, u32[]{:S(2)}) copy-start(bf16[4,1024]{1,0:T(4,128)(2,1)} %param.14) | copy-start | bytes 24580
  0.0 6.9 %copy-start.7 = (s32[128]{0:T(128)S(1)}, s32[128]{0:T(128)}, u32[]{:S(2)}) copy-start(s32[128]{0:T(128)} %param.17) | copy-start | bytes 1540
  0.0 7.1 %copy-start.6 = (f32[8]{0:T(128)S(1)}, f32[8]{0:T(128)}, u32[]{:S(2)}) copy-start(f32[8]{0:T(128)} %param.18) | copy-start | bytes 100
  7.2 2.2 copy-start.1
  9.4 12.0 %copy-start.4 = (bf16[1,2048]{1,0:T(2,128)(2,1)S(1)}, bf16[1,2048]{1,0:T(2,128)(2,1)}, u32[]{:S(2)}) copy-start(bf16[1,2048]{1,0:T(2,128)(2,1)} %param.20) | copy-start | bytes 12292
  9.4 12.0 %copy-start.2 = (bf16[1,111,2048]{2,1,0:T(8,128)(2,1)S(1)}, bf16[1,111,2048]{2,1,0:T(8,128)(2,1)}, u32[]{:S(2)}) copy-start(bf16[1,111,2048]{2,1,0:T(8,128)(2,1)} %param.21) | copy-start | bytes 1363972
  9.4 12.3 %copy-start.3 = (f32[2048]{0:T(1024)S(1)}, f32[2048]{0:T(1024)}, u32[]{:S(2)}) copy-start(f32[2048]{0:T(1024)} %param.22) | copy-start | bytes 24580
  151.7 96.8 %all-to-all-start.1 = ((bf16[128,112,256]{2,1,0:T(8,128)(2,1)}), bf16[128,112,256]{2,1,0:T(8,128)(2,1)}, u32[]{:S(2)}, u32[]{:S(2)}) async-start(bf16[128,112,256]{2,1,0:T(8,128)(2,1)} %shard_map.138), calls=%async_computation.1 | async-start | bytes 14680064 | tf_op jit(solution)/shard_map/all_to_all | solution.py:301

commit v7 on v6

--- a/solution.py
+++ b/solution.py
@@ -117,14 +117,20 @@
     return ((width // LANE) * used, LANE)
 
 
-def dispatch_kernel(used, place_ref, rows_ref, out_ref, staged):
+def dispatch_kernel(used, ids_ref, rows_ref, out_ref, staged):
     chunks = out_ref.shape[0]
     pieces = rows_ref.shape[1] // LANE
     tile_rows = GROUP * used
+    top_k, tokens = ids_ref.shape
 
     def tile(i, carry):
+        slot = lax.broadcasted_iota(jnp.int32, (tile_rows, tokens), 0) + i * tile_rows
+        ids = ids_ref[...]
+        hit = slot == ids[0:1, :]
+        for k in range(1, top_k):
+            hit = jnp.logical_or(hit, slot == ids[k : k + 1, :])
         staged[...] = jnp.dot(
-            place_ref[i], rows_ref[...], preferred_element_type=jnp.float32
+            hit.astype(jnp.bfloat16), rows_ref[...], preferred_element_type=jnp.float32
         ).astype(staged.dtype)
         for jl in range(GROUP):
             j = i * GROUP + jl
@@ -137,18 +143,16 @@
     lax.fori_loop(0, chunks // GROUP, tile, 0)
 
 
-def dispatch(place_t, rows, used):
-    tiles, tile_rows, _ = place_t.shape
+def dispatch(slot_ids_t, rows, chunks, used):
     width = rows.shape[1]
-    chunks = tiles * GROUP
     return pl.pallas_call(
         lambda *refs: dispatch_kernel(used, *refs),
         out_shape=jax.ShapeDtypeStruct((chunks,) + _wire_shape(width, used), jnp.bfloat16),
         in_specs=[pl.BlockSpec(memory_space=pltpu.VMEM)] * 2,
         out_specs=pl.BlockSpec(memory_space=pltpu.VMEM),
-        scratch_shapes=[pltpu.VMEM((tile_rows, width), jnp.bfloat16)],
+        scratch_shapes=[pltpu.VMEM((GROUP * used, width), jnp.bfloat16)],
         compiler_params=pltpu.CompilerParams(vmem_limit_bytes=48 * 1024 * 1024),
-    )(place_t, rows)
+    )(slot_ids_t, rows)
 
 
 def _gather_tile(i, used, src_ref, dst):
@@ -291,11 +295,10 @@
     slot_rank = jnp.sum(jnp.where(one_hot, earlier[:, None, :], 0), axis=2)
     rank_hot = slot_rank[..., None] == jnp.arange(capacity, dtype=jnp.int32)
     fills = one_hot[..., None] & rank_hot[:, :, None, :]
-    place = jnp.any(fills, axis=1).reshape(tokens, experts * capacity).astype(jnp.bfloat16)
     tiles = experts // GROUP
     tile_rows = GROUP * capacity
-    place_t = place.T.reshape(tiles, tile_rows, tokens)
-    outgoing = dispatch(place_t, normed, capacity)
+    slot_ids = chosen_ids * capacity + slot_rank
+    outgoing = dispatch(slot_ids.T, normed, experts, capacity)
     arrived = lax.all_to_all(outgoing, ("kv", "blk"), split_axis=0, concat_axis=0, tiled=True)
     processed = expert_block(arrived, expert_gate, expert_up, expert_down)
     returned = lax.all_to_all(processed, ("kv", "blk"), split_axis=0, concat_axis=0, tiled=True)

time: 256 us -> 256 us (level)
    reduce_or x1 -> x0, other arithmetic: 2.6 us -> none  [body(): jnp.any(fills, axis=1).reshape(tokens, experts * capacity)]
where the time goes in v7:
time: 256 us
  blocking collectives  95 us (37%)
  waiting for transfers between devices  85.3 us (33%)
  Pallas kernels  54.7 us (21%)
  other arithmetic  8.37 us (3%)
  starting transfers between devices  6 us (2%)
  local copies, waits for them, and re-layouts  5.84 us (2%)
    all_to_all x1, blocking collectives, body(): lax.all_to_all(outgoing, ('kv', 'blk'), split_axis=0, concat_axis=0, tile...  95 us
    all_to_all x1, waiting for transfers between devices, body(): lax.all_to_all(processed, ('kv', 'blk'), split_axis=0, concat_axis=0, til...  85.3 us
    pallas_call x1, Pallas kernels, expert_block(): pl.pallas_call(expert_kernel, out_shape=jax.ShapeDtypeStruct(arrived.shap...  28 us
    pallas_call x1, Pallas kernels, attend_reduce(): pl.pallas_call(lambda *refs: attend_reduce_kernel(n_kv, *refs), out_shape...  12 us
    pallas_call x1, Pallas kernels, combine(): pl.pallas_call(combine_kernel, out_shape=jax.ShapeDtypeStruct(hidden.shap...  7.58 us
    pallas_call x1, Pallas kernels, dispatch(): pl.pallas_call(lambda *refs: dispatch_kernel(used, *refs), out_shape=jax....  7.15 us
    all_to_all x1, starting transfers between devices, body(): lax.all_to_all(processed, ('kv', 'blk'), split_axis=0, concat_axis=0, til...  6 us
  transfers between devices with their start and end apart: 1, of which 1 were waited for; matrix products, arithmetic and copies ran while one was open for 2% of the time, Pallas kernels for 0%

profile of v7, /device:TPU:2, one launch (start us, length us, event | category | flops | bytes accessed | tf_op | source)
XLA Modules:
  0.0 255.7 jit_solution(3406218340520356620)
XLA Ops:
  0.0 0.0 copy-start
  0.0 0.8 copy.36
  0.8 0.3 iota_compare_fusion.1
  1.1 0.2 reduce_window_sum.11
  1.3 2.1 select_reduce_fusion.2
  3.4 0.1 copy.37
  3.4 0.7 add_bitcast_fusion.refs_0_
  4.2 0.7 copy.49
  4.9 0.7 subtract_bitcast_fusion
  5.6 0.1 copy.38.refs_3_
  5.7 0.7 copy.39.refs_4_
  6.4 0.0 copy-start.1
  6.4 2.2 copy-done.1
  8.6 0.0 copy-start.4
  8.6 0.0 copy-start.2
  8.6 0.0 copy-start.3
  8.6 12.0 %shard_map.136 = f32[1,2048]{1,0:T(1,128)S(1)} custom-call(bf16[4,8,128]{2,1,0:T(8,128)(2,1)S(1)} %bitcast.25, bf16[4,4096,128]{2,1,0:T(8,128)(2,1)S(1)} %bitcast.24, bf16[4,4096,128]{2,1,0:T(8,128)(2,1)} %bitcast.26, s32[4,1]{1,0:T(4,128)S(1)} %copy.38.refs_3_, f32[8,1]{1,0:T(8,128)S(1)} %copy.39.refs_4_, bf16[1024,2048]{1,0:T(8,128)(2,1)} %refs_5_.1), custom_call_target="tpu_custom_call" | custom-call | tf_op jit(solution)/shard_map/pallas_call | solution.py:87
  20.6 0.0 copy-done.4
  20.6 0.0 copy-done.2
  20.6 0.3 fusion
  20.9 0.0 copy-done.3
  20.9 0.2 fusion.2.refs_1_
  21.1 7.2 %shard_map.137 = bf16[128,112,256]{2,1,0:T(8,128)(2,1)} custom-call(s32[8,112]{1,0:T(8,128)S(1)} %add_bitcast_fusion.refs_0_, bf16[112,2048]{1,0:T(8,128)(2,1)S(1)} %fusion.2.refs_1_), custom_call_target="tpu_custom_call" | custom-call | tf_op jit(solution)/shard_map/pallas_call | solution.py:148
  28.2 95.0 %all_to_all.10.x_ref = bf16[128,112,256]{2,1,0:T(8,128)(2,1)} all-to-all(bf16[128,112,256]{2,1,0:T(8,128)(2,1)} %shard_map.137), channel_id=1, replica_groups=mesh['kv'=4,'blk'=32] {'kv','blk'}, dimensions={0} | all-to-all | bytes 14680064 | tf_op jit(solution)/shard_map/all_to_all | solution.py:302
  123.2 28.0 %shard_map.138 = bf16[128,112,256]{2,1,0:T(8,128)(2,1)} custom-call(bf16[128,112,256]{2,1,0:T(8,128)(2,1)} %all_to_all.10.x_ref, bf16[2048,768]{1,0:T(8,128)(2,1)} %bitcast.27, bf16[2048,768]{1,0:T(8,128)(2,1)} %bitcast.28, bf16[768,2048]{1,0:T(8,128)(2,1)} %bitcast.29), custom_call_target="tpu_custom_call" | custom-call | tf_op jit(solution)/shard_map/pallas_call | solution.py:196
  151.3 6.0 %all-to-all-start.1 = ((bf16[128,112,256]{2,1,0:T(8,128)(2,1)}), bf16[128,112,256]{2,1,0:T(8,128)(2,1)}, u32[]{:S(2)}, u32[]{:S(2)}) async-start(bf16[128,112,256]{2,1,0:T(8,128)(2,1)} %shard_map.138), calls=%async_computation.1 | async-start | bytes 14680064 | tf_op jit(solution)/shard_map/all_to_all | solution.py:304
  157.3 0.0 copy-done
  157.3 0.3 fusion.6
  157.6 0.3 select_reduce_fusion.1
  157.9 0.1 copy.41
  158.0 0.1 reduce_max.9
  158.1 0.1 copy.42
  158.2 0.1 iota_compare_fusion
  158.4 3.1 %select_reduce_fusion = f32[112,128,14]{1,2,0:T(8,128)S(1)} fusion(f32[112,8]{1,0:T(8,128)S(1)} %copy.42, pred[112,8,14]{1,2,0:T(8,128)(4,1)S(1)} %iota_compare_fusion, pred[112,8,128]{2,1,0:T(8,128)(4,1)S(1)} %get-tuple-element.9), kind=kLoop, calls=%fused_computation | loop fusion | flops 4616192 | bytes 933632 | tf_op jit(solution)/shard_map/reduce_sum | solution.py:305
  161.4 0.7 copy.43
  162.1 0.1 reshape.85
  162.2 0.3 copy.44
  162.5 0.1 subtract_convert_fusion
  162.6 0.2 maximum_bitcast_fusion.mix_ref
  162.8 85.3 %all-to-all-done.1.ret_ref = bf16[128,112,256]{2,1,0:T(8,128)(2,1)} async-done(((bf16[128,112,256]{2,1,0:T(8,128)(2,1)}), bf16[128,112,256]{2,1,0:T(8,128)(2,1)}, u32[]{:S(2)}, u32[]{:S(2)}) %all-to-all-start.1) | async-done | bytes 7340064 | tf_op jit(solution)/shard_map/all_to_all | solution.py:304
  248.1 7.6 %shard_map.139 = bf16[112,2048]{1,0:T(8,128)(2,1)} custom-call(bf16[128,112,256]{2,1,0:T(8,128)(2,1)} %all-to-all-done.1.ret_ref, bf16[8,224,224]{2,1,0:T(8,128)(2,1)S(1)} %maximum_bitcast_fusion.mix_ref, bf16[112,2048]{1,0:T(8,128)(2,1)S(1)} %get-tuple-element.8.hidden_ref), custom_call_target="tpu_custom_call" | custom-call | tf_op jit(solution)/shard_map/pallas_call | solution.py:232
  (6 shorter events, 0.1 us)
Async XLA Ops:
  0.0 157.3 %copy-start = (bf16[2048,128]{1,0:T(8,128)(2,1)S(1)}, bf16[2048,128]{1,0:T(8,128)(2,1)}, u32[]{:S(2)}) copy-start(bf16[2048,128]{1,0:T(8,128)(2,1)} %param.23) | copy-start | bytes 1572868
  6.4 2.2 copy-start.1
  8.6 12.0 %copy-start.4 = (bf16[1,2048]{1,0:T(2,128)(2,1)S(1)}, bf16[1,2048]{1,0:T(2,128)(2,1)}, u32[]{:S(2)}) copy-start(bf16[1,2048]{1,0:T(2,128)(2,1)} %param.20) | copy-start | bytes 12292
  8.6 12.0 %copy-start.2 = (bf16[1,111,2048]{2,1,0:T(8,128)(2,1)S(1)}, bf16[1,111,2048]{2,1,0:T(8,128)(2,1)}, u32[]{:S(2)}) copy-start(bf16[1,111,2048]{2,1,0:T(8,128)(2,1)} %param.21) | copy-start | bytes 1363972
  8.6 12.3 %copy-start.3 = (f32[2048]{0:T(1024)S(1)}, f32[2048]{0:T(1024)}, u32[]{:S(2)}) copy-start(f32[2048]{0:T(1024)} %param.22) | copy-start | bytes 24580
  151.3 96.8 %all-to-all-start.1 = ((bf16[128,112,256]{2,1,0:T(8,128)(2,1)}), bf16[128,112,256]{2,1,0:T(8,128)(2,1)}, u32[]{:S(2)}, u32[]{:S(2)}) async-start(bf16[128,112,256]{2,1,0:T(8,128)(2,1)} %shard_map.138), calls=%async_computation.1 | async-start | bytes 14680064 | tf_op jit(solution)/shard_map/all_to_all | solution.py:304

commit v8 on v7

--- a/solution.py
+++ b/solution.py
@@ -163,7 +163,7 @@
             dst[pl.ds(jl * used, used), pl.ds(q * LANE, LANE)] = src_ref[j, pl.ds(q * used, used), :]
 
 
-def expert_kernel(x_ref, gate_ref, up_ref, down_ref, out_ref, rows_in, rows_out):
+def expert_kernel(x_ref, gate_ref, up_ref, down_ref, order_ref, out_ref, rows_in, rows_out):
     chunks, wire_rows, _ = x_ref.shape
     width = gate_ref.shape[0]
     pieces = width // LANE
@@ -189,21 +189,21 @@
     lax.fori_loop(0, chunks // GROUP, tile, 0)
 
 
-def expert_block(arrived, gate_weights, up_weights, down_weights):
+def expert_block(arrived, gate_weights, up_weights, down_weights, order):
     chunks, wire_rows, _ = arrived.shape
     width = gate_weights.shape[1]
     used = wire_rows // (width // LANE)
     return pl.pallas_call(
         expert_kernel,
         out_shape=jax.ShapeDtypeStruct(arrived.shape, jnp.bfloat16),
-        in_specs=[pl.BlockSpec(memory_space=pltpu.VMEM)] * 4,
+        in_specs=[pl.BlockSpec(memory_space=pltpu.VMEM)] * 4 + [pl.BlockSpec(memory_space=pl.ANY)],
         out_specs=pl.BlockSpec(memory_space=pltpu.VMEM),
         scratch_shapes=[
             pltpu.VMEM((GROUP * used, width), jnp.bfloat16),
             pltpu.VMEM((GROUP * used, width), jnp.bfloat16),
         ],
         compiler_params=pltpu.CompilerParams(vmem_limit_bytes=60 * 1024 * 1024),
-    )(arrived, gate_weights[0], up_weights[0], down_weights[0])
+    )(arrived, gate_weights[0], up_weights[0], down_weights[0], order)
 
 
 def combine_kernel(ret_ref, mix_ref, hidden_ref, out_ref, rows, total):
@@ -299,15 +299,15 @@
     tile_rows = GROUP * capacity
     slot_ids = chosen_ids * capacity + slot_rank
     outgoing = dispatch(slot_ids.T, normed, experts, capacity)
-    arrived = lax.all_to_all(outgoing, ("kv", "blk"), split_axis=0, concat_axis=0, tiled=True)
-    processed = expert_block(arrived, expert_gate, expert_up, expert_down)
-    returned = lax.all_to_all(processed, ("kv", "blk"), split_axis=0, concat_axis=0, tiled=True)
     mix = jnp.sum(jnp.where(fills, gate_probs[..., None, None], 0.0), axis=1)
     mix = mix.reshape(tokens, experts * capacity)
     mix_hi = mix.astype(jnp.bfloat16)
     mix_lo = (mix - mix_hi.astype(jnp.float32)).astype(jnp.bfloat16)
     mix_both = jnp.concatenate([mix_hi, mix_lo], axis=0)
     mix_tiles = mix_both.reshape(2 * tokens, tiles, tile_rows).transpose(1, 0, 2)
+    arrived = lax.all_to_all(outgoing, ("kv", "blk"), split_axis=0, concat_axis=0, tiled=True)
+    processed = expert_block(arrived, expert_gate, expert_up, expert_down, mix_tiles)
+    returned = lax.all_to_all(processed, ("kv", "blk"), split_axis=0, concat_axis=0, tiled=True)
     layer_sum = combine(returned, mix_tiles, hidden)
     return layer_sum[None]
 

time: 256 us -> 260 us (1.016)
  starting transfers between devices: 6 us -> 9.02 us
    all_to_all x1, starting transfers between devices: 6 us -> 9.02 us  [body(): lax.all_to_all(outgoing, ('kv', 'blk'), split_axis=0, concat_axis=0, tile...]
where the time goes in v8:
time: 260 us; the launch traced here: 258 us
  blocking collectives  94.6 us (36%)
  waiting for transfers between devices  84.3 us (32%)
  Pallas kernels  54.7 us (21%)
  other arithmetic  9.35 us (4%)
  starting transfers between devices  9.02 us (3%)
  local copies, waits for them, and re-layouts  5.78 us (2%)
    all_to_all x1, blocking collectives, body(): lax.all_to_all(processed, ('kv', 'blk'), split_axis=0, concat_axis=0, til...  94.6 us
    all_to_all x1, waiting for transfers between devices, body(): lax.all_to_all(outgoing, ('kv', 'blk'), split_axis=0, concat_axis=0, tile...  84.3 us
    pallas_call x1, Pallas kernels, expert_block(): pl.pallas_call(expert_kernel, out_shape=jax.ShapeDtypeStruct(arrived.shap...  28 us
    pallas_call x1, Pallas kernels, attend_reduce(): pl.pallas_call(lambda *refs: attend_reduce_kernel(n_kv, *refs), out_shape...  12 us
    all_to_all x1, starting transfers between devices, body(): lax.all_to_all(outgoing, ('kv', 'blk'), split_axis=0, concat_axis=0, tile...  9.02 us
    pallas_call x1, Pallas kernels, combine(): pl.pallas_call(combine_kernel, out_shape=jax.ShapeDtypeStruct(hidden.shap...  7.57 us
    pallas_call x1, Pallas kernels, dispatch(): pl.pallas_call(lambda *refs: dispatch_kernel(used, *refs), out_shape=jax....  7.15 us
  transfers between devices with their start and end apart: 1, of which 1 were waited for; matrix products, arithmetic and copies ran while one was open for 2% of the time, Pallas kernels for 0%

profile of v8, /device:TPU:2, one launch (start us, length us, event | category | flops | bytes accessed | tf_op | source)
XLA Modules:
  0.0 258.3 jit_solution(12071756744455249629)
XLA Ops:
  0.0 0.0 copy-start
  0.0 0.8 subtract_bitcast_fusion
  0.8 0.1 copy.38.refs_3_
  0.9 0.7 copy.39.refs_4_
  1.6 0.7 copy.49
  2.3 0.8 copy.36
  3.1 0.3 iota_compare_fusion.1
  3.4 0.2 reduce_window_sum.11
  3.5 2.1 select_reduce_fusion.2
  5.6 0.1 copy.37
  5.7 0.7 add_bitcast_fusion.refs_0_
  6.4 0.0 copy-start.2
  6.4 2.2 copy-done.2
  8.6 0.0 copy-start.5
  8.6 0.0 copy-start.3
  8.6 0.0 copy-start.4
  8.6 12.0 %shard_map.136 = f32[1,2048]{1,0:T(1,128)S(1)} custom-call(bf16[4,8,128]{2,1,0:T(8,128)(2,1)S(1)} %bitcast.25, bf16[4,4096,128]{2,1,0:T(8,128)(2,1)S(1)} %bitcast.24, bf16[4,4096,128]{2,1,0:T(8,128)(2,1)} %bitcast.26, s32[4,1]{1,0:T(4,128)S(1)} %copy.38.refs_3_, f32[8,1]{1,0:T(8,128)S(1)} %copy.39.refs_4_, bf16[1024,2048]{1,0:T(8,128)(2,1)} %refs_5_.1), custom_call_target="tpu_custom_call" | custom-call | tf_op jit(solution)/shard_map/pallas_call | solution.py:87
  20.6 0.0 copy-done.5
  20.6 0.0 copy-done.3
  20.6 0.3 fusion
  20.9 0.0 copy-done.4
  20.9 0.2 fusion.2.refs_1_
  21.1 7.2 %shard_map.137 = bf16[128,112,256]{2,1,0:T(8,128)(2,1)} custom-call(s32[8,112]{1,0:T(8,128)S(1)} %add_bitcast_fusion.refs_0_, bf16[112,2048]{1,0:T(8,128)(2,1)S(1)} %fusion.2.refs_1_), custom_call_target="tpu_custom_call" | custom-call | tf_op jit(solution)/shard_map/pallas_call | solution.py:148
  28.2 9.0 %all-to-all-start = ((bf16[128,112,256]{2,1,0:T(8,128)(2,1)}), bf16[128,112,256]{2,1,0:T(8,128)(2,1)}, u32[]{:S(2)}, u32[]{:S(2)}) async-start(bf16[128,112,256]{2,1,0:T(8,128)(2,1)} %shard_map.137), calls=%async_computation | async-start | bytes 14680064 | tf_op jit(solution)/shard_map/all_to_all | solution.py:308
  37.3 0.0 copy-done
  37.3 0.3 fusion.6
  37.5 0.3 select_reduce_fusion.1
  37.9 0.1 copy.41
  37.9 0.1 reduce_max.9
  38.1 0.1 copy.42
  38.2 0.1 iota_compare_fusion
  38.3 3.1 %select_reduce_fusion = f32[112,128,14]{1,2,0:T(8,128)S(1)} fusion(f32[112,8]{1,0:T(8,128)S(1)} %copy.42, pred[112,8,14]{1,2,0:T(8,128)(4,1)S(1)} %iota_compare_fusion, pred[112,8,128]{2,1,0:T(8,128)(4,1)S(1)} %get-tuple-element.9), kind=kLoop, calls=%fused_computation | loop fusion | flops 4616192 | bytes 933632 | tf_op jit(solution)/shard_map/reduce_sum | solution.py:302
  41.4 0.7 copy.43
  42.1 0.1 reshape.85
  42.2 0.3 copy.44
  42.5 0.1 subtract_convert_fusion
  42.6 1.1 maximum_bitcast_fusion.order_ref.mix_ref
  43.7 84.3 %all-to-all-done.x_ref = bf16[128,112,256]{2,1,0:T(8,128)(2,1)} async-done(((bf16[128,112,256]{2,1,0:T(8,128)(2,1)}), bf16[128,112,256]{2,1,0:T(8,128)(2,1)}, u32[]{:S(2)}, u32[]{:S(2)}) %all-to-all-start) | async-done | bytes 7340064 | tf_op jit(solution)/shard_map/all_to_all | solution.py:308
  128.0 28.0 %shard_map.138 = bf16[128,112,256]{2,1,0:T(8,128)(2,1)} custom-call(bf16[128,112,256]{2,1,0:T(8,128)(2,1)} %all-to-all-done.x_ref, bf16[2048,768]{1,0:T(8,128)(2,1)} %bitcast.27, bf16[2048,768]{1,0:T(8,128)(2,1)} %bitcast.28, bf16[768,2048]{1,0:T(8,128)(2,1)} %bitcast.29, bf16[8,224,224]{2,1,0:T(8,128)(2,1)} %maximum_bitcast_fusion.order_ref.mix_ref), custom_call_target="tpu_custom_call" | custom-call | tf_op jit(solution)/shard_map/pallas_call | solution.py:196
  156.0 0.0 copy-start.1
  156.0 94.6 %all_to_all.10.ret_ref = bf16[128,112,256]{2,1,0:T(8,128)(2,1)} all-to-all(bf16[128,112,256]{2,1,0:T(8,128)(2,1)} %shard_map.138), channel_id=1, replica_groups=mesh['kv'=4,'blk'=32] {'kv','blk'}, dimensions={0} | all-to-all | bytes 14680064 | tf_op jit(solution)/shard_map/all_to_all | solution.py:310
  250.7 0.0 copy-done.1
  250.7 7.6 %shard_map.139 = bf16[112,2048]{1,0:T(8,128)(2,1)} custom-call(bf16[128,112,256]{2,1,0:T(8,128)(2,1)} %all_to_all.10.ret_ref, bf16[8,224,224]{2,1,0:T(8,128)(2,1)S(1)} %copy-done.1, bf16[112,2048]{1,0:T(8,128)(2,1)S(1)} %get-tuple-element.8.hidden_ref), custom_call_target="tpu_custom_call" | custom-call | tf_op jit(solution)/shard_map/pallas_call | solution.py:232
  (6 shorter events, 0.1 us)
Async XLA Ops:
  0.0 37.3 %copy-start = (bf16[2048,128]{1,0:T(8,128)(2,1)S(1)}, bf16[2048,128]{1,0:T(8,128)(2,1)}, u32[]{:S(2)}) copy-start(bf16[2048,128]{1,0:T(8,128)(2,1)} %param.23) | copy-start | bytes 1572868
  6.4 2.2 copy-start.2
  8.6 12.0 %copy-start.5 = (bf16[1,2048]{1,0:T(2,128)(2,1)S(1)}, bf16[1,2048]{1,0:T(2,128)(2,1)}, u32[]{:S(2)}) copy-start(bf16[1,2048]{1,0:T(2,128)(2,1)} %param.20) | copy-start | bytes 12292
  8.6 12.0 %copy-start.3 = (bf16[1,111,2048]{2,1,0:T(8,128)(2,1)S(1)}, bf16[1,111,2048]{2,1,0:T(8,128)(2,1)}, u32[]{:S(2)}) copy-start(bf16[1,111,2048]{2,1,0:T(8,128)(2,1)} %param.21) | copy-start | bytes 1363972
  8.6 12.3 %copy-start.4 = (f32[2048]{0:T(1024)S(1)}, f32[2048]{0:T(1024)}, u32[]{:S(2)}) copy-start(f32[2048]{0:T(1024)} %param.22) | copy-start | bytes 24580
  28.2 99.8 %all-to-all-start = ((bf16[128,112,256]{2,1,0:T(8,128)(2,1)}), bf16[128,112,256]{2,1,0:T(8,128)(2,1)}, u32[]{:S(2)}, u32[]{:S(2)}) async-start(bf16[128,112,256]{2,1,0:T(8,128)(2,1)} %shard_map.137), calls=%async_computation | async-start | bytes 14680064 | tf_op jit(solution)/shard_map/all_to_all | solution.py:308
  156.0 94.7 %copy-start.1 = (bf16[8,224,224]{2,1,0:T(8,128)(2,1)S(1)}, bf16[8,224,224]{2,1,0:T(8,128)(2,1)}, u32[]{:S(2)}) copy-start(bf16[8,224,224]{2,1,0:T(8,128)(2,1)} %maximum_bitcast_fusion.order_ref.mix_ref) | copy-start | bytes 2408452

commit v9 on v8

--- a/solution.py
+++ b/solution.py
@@ -299,15 +299,15 @@
     tile_rows = GROUP * capacity
     slot_ids = chosen_ids * capacity + slot_rank
     outgoing = dispatch(slot_ids.T, normed, experts, capacity)
+    arrived = lax.all_to_all(outgoing, ("kv", "blk"), split_axis=0, concat_axis=0, tiled=True)
+    processed = expert_block(arrived, expert_gate, expert_up, expert_down, gate_probs)
+    returned = lax.all_to_all(processed, ("kv", "blk"), split_axis=0, concat_axis=0, tiled=True)
     mix = jnp.sum(jnp.where(fills, gate_probs[..., None, None], 0.0), axis=1)
     mix = mix.reshape(tokens, experts * capacity)
     mix_hi = mix.astype(jnp.bfloat16)
     mix_lo = (mix - mix_hi.astype(jnp.float32)).astype(jnp.bfloat16)
     mix_both = jnp.concatenate([mix_hi, mix_lo], axis=0)
     mix_tiles = mix_both.reshape(2 * tokens, tiles, tile_rows).transpose(1, 0, 2)
-    arrived = lax.all_to_all(outgoing, ("kv", "blk"), split_axis=0, concat_axis=0, tiled=True)
-    processed = expert_block(arrived, expert_gate, expert_up, expert_down, mix_tiles)
-    returned = lax.all_to_all(processed, ("kv", "blk"), split_axis=0, concat_axis=0, tiled=True)
     layer_sum = combine(returned, mix_tiles, hidden)
     return layer_sum[None]
 

time: 260 us -> 263 us (1.012)
  blocking collectives: 94.6 us -> 0 us
  waiting for transfers between devices: 84.3 us -> 175 us
  starting transfers between devices: 9.02 us -> 17.7 us
    all_to_all x1 -> x0, blocking collectives: 94.6 us -> none  [body(): lax.all_to_all(processed, ('kv', 'blk'), split_axis=0, concat_axis=0, til...]
    all_to_all x0 -> x1, waiting for transfers between devices: none -> 86.2 us  [body(): lax.all_to_all(processed, ('kv', 'blk'), split_axis=0, concat_axis=0, til...]
    all_to_all x0 -> x1, starting transfers between devices: none -> 8.67 us  [body(): lax.all_to_all(processed, ('kv', 'blk'), split_axis=0, concat_axis=0, til...]
    all_to_all x1, waiting for transfers between devices: 84.3 us -> 89.1 us  [body(): lax.all_to_all(outgoing, ('kv', 'blk'), split_axis=0, concat_axis=0, tile...]
  transfers between devices with their start and end apart: 1 -> 2, of which waited for: 1 -> 2; matrix products, arithmetic and copies ran while one was open for 2% -> 2% of each run, Pallas kernels for 0% -> 0%
where the time goes in v9:
time: 263 us
  waiting for transfers between devices  175 us (67%)
  Pallas kernels  54.7 us (21%)
  starting transfers between devices  17.7 us (7%)
  other arithmetic  9.24 us (4%)
  local copies, waits for them, and re-layouts  5.69 us (2%)
    all_to_all x1, waiting for transfers between devices, body(): lax.all_to_all(outgoing, ('kv', 'blk'), split_axis=0, concat_axis=0, tile...  89.1 us
    all_to_all x1, waiting for transfers between devices, body(): lax.all_to_all(processed, ('kv', 'blk'), split_axis=0, concat_axis=0, til...  86.2 us
    pallas_call x1, Pallas kernels, expert_block(): pl.pallas_call(expert_kernel, out_shape=jax.ShapeDtypeStruct(arrived.shap...  28 us
    pallas_call x1, Pallas kernels, attend_reduce(): pl.pallas_call(lambda *refs: attend_reduce_kernel(n_kv, *refs), out_shape...  12 us
    all_to_all x1, starting transfers between devices, body(): lax.all_to_all(outgoing, ('kv', 'blk'), split_axis=0, concat_axis=0, tile...  9.02 us
    all_to_all x1, starting transfers between devices, body(): lax.all_to_all(processed, ('kv', 'blk'), split_axis=0, concat_axis=0, til...  8.67 us
    pallas_call x1, Pallas kernels, combine(): pl.pallas_call(combine_kernel, out_shape=jax.ShapeDtypeStruct(hidden.shap...  7.58 us
    pallas_call x1, Pallas kernels, dispatch(): pl.pallas_call(lambda *refs: dispatch_kernel(used, *refs), out_shape=jax....  7.15 us
  transfers between devices with their start and end apart: 2, of which 2 were waited for; matrix products, arithmetic and copies ran while one was open for 2% of the time, Pallas kernels for 0%

profile of v9, /device:TPU:2, one launch (start us, length us, event | category | flops | bytes accessed | tf_op | source)
XLA Modules:
  0.0 263.0 jit_solution(1254403701990356294)
XLA Ops:
  0.0 0.0 copy-start
  0.0 0.8 copy.25
  0.8 0.3 iota_compare_fusion.1
  1.1 0.2 reduce_window_sum.11
  1.3 2.1 select_reduce_fusion.2
  3.4 0.1 copy.26
  3.4 0.7 add_bitcast_fusion.refs_0_
  4.2 0.7 copy.34
  4.9 0.7 subtract_bitcast_fusion
  5.6 0.1 copy.27.refs_3_
  5.7 0.7 copy.28.refs_4_
  6.4 0.0 copy-start.1
  6.4 2.2 copy-done.1
  8.6 0.0 copy-start.5
  8.6 0.0 copy-start.3
  8.6 0.0 copy-start.4
  8.6 12.0 %shard_map.136 = f32[1,2048]{1,0:T(1,128)S(1)} custom-call(bf16[4,8,128]{2,1,0:T(8,128)(2,1)S(1)} %bitcast.25, bf16[4,4096,128]{2,1,0:T(8,128)(2,1)S(1)} %bitcast.24, bf16[4,4096,128]{2,1,0:T(8,128)(2,1)} %bitcast.26, s32[4,1]{1,0:T(4,128)S(1)} %copy.27.refs_3_, f32[8,1]{1,0:T(8,128)S(1)} %copy.28.refs_4_, bf16[1024,2048]{1,0:T(8,128)(2,1)} %refs_5_.1), custom_call_target="tpu_custom_call" | custom-call | tf_op jit(solution)/shard_map/pallas_call | solution.py:87
  20.6 0.0 copy-done.5
  20.6 0.0 copy-done.3
  20.6 0.3 fusion
  20.9 0.0 copy-done.4
  20.9 0.2 fusion.2.refs_1_
  21.1 7.2 %shard_map.137 = bf16[128,112,256]{2,1,0:T(8,128)(2,1)} custom-call(s32[8,112]{1,0:T(8,128)S(1)} %add_bitcast_fusion.refs_0_, bf16[112,2048]{1,0:T(8,128)(2,1)S(1)} %fusion.2.refs_1_), custom_call_target="tpu_custom_call" | custom-call | tf_op jit(solution)/shard_map/pallas_call | solution.py:148
  28.2 9.0 %all-to-all-start = ((bf16[128,112,256]{2,1,0:T(8,128)(2,1)}), bf16[128,112,256]{2,1,0:T(8,128)(2,1)}, u32[]{:S(2)}, u32[]{:S(2)}) async-start(bf16[128,112,256]{2,1,0:T(8,128)(2,1)} %shard_map.137), calls=%async_computation | async-start | bytes 14680064 | tf_op jit(solution)/shard_map/all_to_all | solution.py:302
  37.3 0.0 copy-done
  37.3 0.3 fusion.6
  37.6 0.3 select_reduce_fusion.1
  37.9 0.1 reduce_max.9
  38.0 0.2 fusion.5
  38.2 0.7 fusion.4.order_ref
  38.9 89.1 %all-to-all-done.x_ref = bf16[128,112,256]{2,1,0:T(8,128)(2,1)} async-done(((bf16[128,112,256]{2,1,0:T(8,128)(2,1)}), bf16[128,112,256]{2,1,0:T(8,128)(2,1)}, u32[]{:S(2)}, u32[]{:S(2)}) %all-to-all-start) | async-done | bytes 7340064 | tf_op jit(solution)/shard_map/all_to_all | solution.py:302
  128.0 28.0 %shard_map.138 = bf16[128,112,256]{2,1,0:T(8,128)(2,1)} custom-call(bf16[128,112,256]{2,1,0:T(8,128)(2,1)} %all-to-all-done.x_ref, bf16[2048,768]{1,0:T(8,128)(2,1)} %bitcast.27, bf16[2048,768]{1,0:T(8,128)(2,1)} %bitcast.28, bf16[768,2048]{1,0:T(8,128)(2,1)} %bitcast.29, f32[112,8]{1,0:T(8,128)} %fusion.4.order_ref), custom_call_target="tpu_custom_call" | custom-call | tf_op jit(solution)/shard_map/pallas_call | solution.py:196
  156.0 0.0 copy-start.2
  156.0 8.7 %all-to-all-start.1 = ((bf16[128,112,256]{2,1,0:T(8,128)(2,1)}), bf16[128,112,256]{2,1,0:T(8,128)(2,1)}, u32[]{:S(2)}, u32[]{:S(2)}) async-start(bf16[128,112,256]{2,1,0:T(8,128)(2,1)} %shard_map.138), calls=%async_computation.1 | async-start | bytes 14680064 | tf_op jit(solution)/shard_map/all_to_all | solution.py:304
  164.7 0.1 iota_compare_fusion
  164.8 0.0 copy-done.2
  164.9 3.1 %select_reduce_fusion = f32[112,128,14]{1,2,0:T(8,128)S(1)} fusion(f32[112,8]{1,0:T(8,128)S(1)} %copy-done.2, pred[112,8,14]{1,2,0:T(8,128)(4,1)S(1)} %iota_compare_fusion, pred[112,8,128]{2,1,0:T(8,128)(4,1)S(1)} %get-tuple-element.9), kind=kLoop, calls=%fused_computation | loop fusion | flops 4616192 | bytes 933632 | tf_op jit(solution)/shard_map/reduce_sum | solution.py:305
  167.9 0.7 copy.29
  168.6 0.1 reshape.83
  168.7 0.3 copy.30
  169.0 0.1 subtract_convert_fusion
  169.1 0.2 maximum_bitcast_fusion.mix_ref
  169.3 86.2 %all-to-all-done.1.ret_ref = bf16[128,112,256]{2,1,0:T(8,128)(2,1)} async-done(((bf16[128,112,256]{2,1,0:T(8,128)(2,1)}), bf16[128,112,256]{2,1,0:T(8,128)(2,1)}, u32[]{:S(2)}, u32[]{:S(2)}) %all-to-all-start.1) | async-done | bytes 7340064 | tf_op jit(solution)/shard_map/all_to_all | solution.py:304
  255.4 7.6 %shard_map.139 = bf16[112,2048]{1,0:T(8,128)(2,1)} custom-call(bf16[128,112,256]{2,1,0:T(8,128)(2,1)} %all-to-all-done.1.ret_ref, bf16[8,224,224]{2,1,0:T(8,128)(2,1)S(1)} %maximum_bitcast_fusion.mix_ref, bf16[112,2048]{1,0:T(8,128)(2,1)S(1)} %get-tuple-element.8.hidden_ref), custom_call_target="tpu_custom_call" | custom-call | tf_op jit(solution)/shard_map/pallas_call | solution.py:232
  (4 shorter events, 0.0 us)
Async XLA Ops:
  0.0 37.3 %copy-start = (bf16[2048,128]{1,0:T(8,128)(2,1)S(1)}, bf16[2048,128]{1,0:T(8,128)(2,1)}, u32[]{:S(2)}) copy-start(bf16[2048,128]{1,0:T(8,128)(2,1)} %param.23) | copy-start | bytes 1572868
  6.4 2.2 copy-start.1
  8.6 12.0 %copy-start.5 = (bf16[1,2048]{1,0:T(2,128)(2,1)S(1)}, bf16[1,2048]{1,0:T(2,128)(2,1)}, u32[]{:S(2)}) copy-start(bf16[1,2048]{1,0:T(2,128)(2,1)} %param.20) | copy-start | bytes 12292
  8.6 12.0 %copy-start.3 = (bf16[1,111,2048]{2,1,0:T(8,128)(2,1)S(1)}, bf16[1,111,2048]{2,1,0:T(8,128)(2,1)}, u32[]{:S(2)}) copy-start(bf16[1,111,2048]{2,1,0:T(8,128)(2,1)} %param.21) | copy-start | bytes 1363972
  8.6 12.3 %copy-start.4 = (f32[2048]{0:T(1024)S(1)}, f32[2048]{0:T(1024)}, u32[]{:S(2)}) copy-start(f32[2048]{0:T(1024)} %param.22) | copy-start | bytes 24580
  28.2 99.8 %all-to-all-start = ((bf16[128,112,256]{2,1,0:T(8,128)(2,1)}), bf16[128,112,256]{2,1,0:T(8,128)(2,1)}, u32[]{:S(2)}, u32[]{:S(2)}) async-start(bf16[128,112,256]{2,1,0:T(8,128)(2,1)} %shard_map.137), calls=%async_computation | async-start | bytes 14680064 | tf_op jit(solution)/shard_map/all_to_all | solution.py:302
  156.0 8.8 %copy-start.2 = (f32[112,8]{1,0:T(8,128)S(1)}, f32[112,8]{1,0:T(8,128)}, u32[]{:S(2)}) copy-start(f32[112,8]{1,0:T(8,128)} %fusion.4.order_ref) | copy-start | bytes 10756
  156.0 99.4 %all-to-all-start.1 = ((bf16[128,112,256]{2,1,0:T(8,128)(2,1)}), bf16[128,112,256]{2,1,0:T(8,128)(2,1)}, u32[]{:S(2)}, u32[]{:S(2)}) async-start(bf16[128,112,256]{2,1,0:T(8,128)(2,1)} %shard_map.138), calls=%async_computation.1 | async-start | bytes 14680064 | tf_op jit(solution)/shard_map/all_to_all | solution.py:304

commit v10 on v7

--- a/solution.py
+++ b/solution.py
@@ -38,16 +38,10 @@
         numerator = jnp.dot(
             weights.astype(jnp.bfloat16), v_ref[r], preferred_element_type=jnp.float32
         )
-        att[:, pl.ds(r, 1), :] = (numerator / denominator).astype(jnp.bfloat16).astype(
-            jnp.float32
-        )[:, None, :]
-    total = jnp.zeros((requests, proj_ref.shape[1]), jnp.float32)
-    for h in range(heads):
-        total = total + jnp.dot(
-            att[h].astype(jnp.bfloat16),
-            proj_ref[pl.ds(h * head_dim, head_dim), :],
-            preferred_element_type=jnp.float32,
-        )
+        attended = (numerator / denominator).astype(jnp.bfloat16)
+        for h in range(heads):
+            att[pl.ds(r, 1), pl.ds(h * head_dim, head_dim)] = attended[h : h + 1, :]
+    total = jnp.dot(att[...], proj_ref[...], preferred_element_type=jnp.float32)
     part[...] = total[:, None, :]
     pl.semaphore_wait(barrier, n_kv - 1)
     for step in range(1, n_kv):
@@ -90,7 +84,7 @@
         in_specs=[pl.BlockSpec(memory_space=pltpu.VMEM)] * 6,
         out_specs=pl.BlockSpec(memory_space=pltpu.VMEM),
         scratch_shapes=[
-            pltpu.VMEM((heads, requests, head_dim), jnp.float32),
+            pltpu.VMEM((requests, heads * head_dim), jnp.bfloat16),
             pltpu.VMEM((requests, 1, width), jnp.float32),
             pltpu.VMEM((n_kv, 1, width), jnp.float32),
             pltpu.SemaphoreType.DMA((n_kv,)),

time: 256 us -> 256 us (level)
  no operation moved by 1% of the time
where the time goes in v10:
time: 256 us
  blocking collectives  95 us (37%)
  waiting for transfers between devices  85.3 us (33%)
  Pallas kernels  54.7 us (21%)
  other arithmetic  8.37 us (3%)
  starting transfers between devices  6 us (2%)
  local copies, waits for them, and re-layouts  5.84 us (2%)
    all_to_all x1, blocking collectives, body(): lax.all_to_all(outgoing, ('kv', 'blk'), split_axis=0, concat_axis=0, tile...  95 us
    all_to_all x1, waiting for transfers between devices, body(): lax.all_to_all(processed, ('kv', 'blk'), split_axis=0, concat_axis=0, til...  85.3 us
    pallas_call x1, Pallas kernels, expert_block(): pl.pallas_call(expert_kernel, out_shape=jax.ShapeDtypeStruct(arrived.shap...  28 us
    pallas_call x1, Pallas kernels, attend_reduce(): pl.pallas_call(lambda *refs: attend_reduce_kernel(n_kv, *refs), out_shape...  11.9 us
    pallas_call x1, Pallas kernels, combine(): pl.pallas_call(combine_kernel, out_shape=jax.ShapeDtypeStruct(hidden.shap...  7.57 us
    pallas_call x1, Pallas kernels, dispatch(): pl.pallas_call(lambda *refs: dispatch_kernel(used, *refs), out_shape=jax....  7.15 us
    all_to_all x1, starting transfers between devices, body(): lax.all_to_all(processed, ('kv', 'blk'), split_axis=0, concat_axis=0, til...  6 us
  transfers between devices with their start and end apart: 1, of which 1 were waited for; matrix products, arithmetic and copies ran while one was open for 2% of the time, Pallas kernels for 0%

profile of v10, /device:TPU:2, one launch (start us, length us, event | category | flops | bytes accessed | tf_op | source)
XLA Modules:
  0.0 255.6 jit_solution(17017603057440059659)
XLA Ops:
  0.0 0.0 copy-start
  0.0 0.8 copy.36
  0.8 0.3 iota_compare_fusion.1
  1.1 0.2 reduce_window_sum.11
  1.3 2.1 select_reduce_fusion.2
  3.4 0.1 copy.37
  3.4 0.7 add_bitcast_fusion.refs_0_
  4.2 0.7 copy.49
  4.9 0.7 subtract_bitcast_fusion
  5.6 0.1 copy.38.refs_3_
  5.7 0.7 copy.39.refs_4_
  6.4 0.0 copy-start.1
  6.4 2.2 copy-done.1
  8.6 0.0 copy-start.4
  8.6 0.0 copy-start.2
  8.6 0.0 copy-start.3
  8.6 11.9 %shard_map.136 = f32[1,2048]{1,0:T(1,128)S(1)} custom-call(bf16[4,8,128]{2,1,0:T(8,128)(2,1)S(1)} %bitcast.25, bf16[4,4096,128]{2,1,0:T(8,128)(2,1)S(1)} %bitcast.24, bf16[4,4096,128]{2,1,0:T(8,128)(2,1)} %bitcast.26, s32[4,1]{1,0:T(4,128)S(1)} %copy.38.refs_3_, f32[8,1]{1,0:T(8,128)S(1)} %copy.39.refs_4_, bf16[1024,2048]{1,0:T(8,128)(2,1)} %refs_5_.1), custom_call_target="tpu_custom_call" | custom-call | tf_op jit(solution)/shard_map/pallas_call | solution.py:81
  20.6 0.0 copy-done.4
  20.6 0.0 copy-done.2
  20.6 0.3 fusion
  20.9 0.0 copy-done.3
  20.9 0.2 fusion.2.refs_1_
  21.1 7.2 %shard_map.137 = bf16[128,112,256]{2,1,0:T(8,128)(2,1)} custom-call(s32[8,112]{1,0:T(8,128)S(1)} %add_bitcast_fusion.refs_0_, bf16[112,2048]{1,0:T(8,128)(2,1)S(1)} %fusion.2.refs_1_), custom_call_target="tpu_custom_call" | custom-call | tf_op jit(solution)/shard_map/pallas_call | solution.py:142
  28.2 95.0 %all_to_all.10.x_ref = bf16[128,112,256]{2,1,0:T(8,128)(2,1)} all-to-all(bf16[128,112,256]{2,1,0:T(8,128)(2,1)} %shard_map.137), channel_id=1, replica_groups=mesh['kv'=4,'blk'=32] {'kv','blk'}, dimensions={0} | all-to-all | bytes 14680064 | tf_op jit(solution)/shard_map/all_to_all | solution.py:296
  123.2 28.0 %shard_map.138 = bf16[128,112,256]{2,1,0:T(8,128)(2,1)} custom-call(bf16[128,112,256]{2,1,0:T(8,128)(2,1)} %all_to_all.10.x_ref, bf16[2048,768]{1,0:T(8,128)(2,1)} %bitcast.27, bf16[2048,768]{1,0:T(8,128)(2,1)} %bitcast.28, bf16[768,2048]{1,0:T(8,128)(2,1)} %bitcast.29), custom_call_target="tpu_custom_call" | custom-call | tf_op jit(solution)/shard_map/pallas_call | solution.py:190
  151.3 6.0 %all-to-all-start.1 = ((bf16[128,112,256]{2,1,0:T(8,128)(2,1)}), bf16[128,112,256]{2,1,0:T(8,128)(2,1)}, u32[]{:S(2)}, u32[]{:S(2)}) async-start(bf16[128,112,256]{2,1,0:T(8,128)(2,1)} %shard_map.138), calls=%async_computation.1 | async-start | bytes 14680064 | tf_op jit(solution)/shard_map/all_to_all | solution.py:298
  157.3 0.0 copy-done
  157.3 0.3 fusion.6
  157.6 0.3 select_reduce_fusion.1
  157.9 0.1 copy.41
  157.9 0.1 reduce_max.9
  158.1 0.1 copy.42
  158.2 0.1 iota_compare_fusion
  158.4 3.1 %select_reduce_fusion = f32[112,128,14]{1,2,0:T(8,128)S(1)} fusion(f32[112,8]{1,0:T(8,128)S(1)} %copy.42, pred[112,8,14]{1,2,0:T(8,128)(4,1)S(1)} %iota_compare_fusion, pred[112,8,128]{2,1,0:T(8,128)(4,1)S(1)} %get-tuple-element.9), kind=kLoop, calls=%fused_computation | loop fusion | flops 4616192 | bytes 933632 | tf_op jit(solution)/shard_map/reduce_sum | solution.py:299
  161.4 0.7 copy.43
  162.1 0.1 reshape.85
  162.2 0.3 copy.44
  162.5 0.1 subtract_convert_fusion
  162.6 0.2 maximum_bitcast_fusion.mix_ref
  162.8 85.3 %all-to-all-done.1.ret_ref = bf16[128,112,256]{2,1,0:T(8,128)(2,1)} async-done(((bf16[128,112,256]{2,1,0:T(8,128)(2,1)}), bf16[128,112,256]{2,1,0:T(8,128)(2,1)}, u32[]{:S(2)}, u32[]{:S(2)}) %all-to-all-start.1) | async-done | bytes 7340064 | tf_op jit(solution)/shard_map/all_to_all | solution.py:298
  248.1 7.6 %shard_map.139 = bf16[112,2048]{1,0:T(8,128)(2,1)} custom-call(bf16[128,112,256]{2,1,0:T(8,128)(2,1)} %all-to-all-done.1.ret_ref, bf16[8,224,224]{2,1,0:T(8,128)(2,1)S(1)} %maximum_bitcast_fusion.mix_ref, bf16[112,2048]{1,0:T(8,128)(2,1)S(1)} %get-tuple-element.8.hidden_ref), custom_call_target="tpu_custom_call" | custom-call | tf_op jit(solution)/shard_map/pallas_call | solution.py:226
  (6 shorter events, 0.1 us)
Async XLA Ops:
  0.0 157.3 %copy-start = (bf16[2048,128]{1,0:T(8,128)(2,1)S(1)}, bf16[2048,128]{1,0:T(8,128)(2,1)}, u32[]{:S(2)}) copy-start(bf16[2048,128]{1,0:T(8,128)(2,1)} %param.23) | copy-start | bytes 1572868
  6.4 2.2 copy-start.1
  8.6 12.0 %copy-start.4 = (bf16[1,2048]{1,0:T(2,128)(2,1)S(1)}, bf16[1,2048]{1,0:T(2,128)(2,1)}, u32[]{:S(2)}) copy-start(bf16[1,2048]{1,0:T(2,128)(2,1)} %param.20) | copy-start | bytes 12292
  8.6 12.0 %copy-start.2 = (bf16[1,111,2048]{2,1,0:T(8,128)(2,1)S(1)}, bf16[1,111,2048]{2,1,0:T(8,128)(2,1)}, u32[]{:S(2)}) copy-start(bf16[1,111,2048]{2,1,0:T(8,128)(2,1)} %param.21) | copy-start | bytes 1363972
  8.6 12.3 %copy-start.3 = (f32[2048]{0:T(1024)S(1)}, f32[2048]{0:T(1024)}, u32[]{:S(2)}) copy-start(f32[2048]{0:T(1024)} %param.22) | copy-start | bytes 24580
  151.3 96.8 %all-to-all-start.1 = ((bf16[128,112,256]{2,1,0:T(8,128)(2,1)}), bf16[128,112,256]{2,1,0:T(8,128)(2,1)}, u32[]{:S(2)}, u32[]{:S(2)}) async-start(bf16[128,112,256]{2,1,0:T(8,128)(2,1)} %shard_map.138), calls=%async_computation.1 | async-start | bytes 14680064 | tf_op jit(solution)/shard_map/all_to_all | solution.py:298

commit v11 on v10

--- a/solution.py
+++ b/solution.py
@@ -105,6 +105,7 @@
 
 LANE = 256
 GROUP = 16
+FFN_GROUP = 64
 
 
 def _wire_shape(width, used):
@@ -149,10 +150,10 @@
     )(slot_ids_t, rows)
 
 
-def _gather_tile(i, used, src_ref, dst):
+def _gather_tile(i, used, src_ref, dst, group=GROUP):
     pieces = dst.shape[1] // LANE
-    for jl in range(GROUP):
-        j = i * GROUP + jl
+    for jl in range(group):
+        j = i * group + jl
         for q in range(pieces):
             dst[pl.ds(jl * used, used), pl.ds(q * LANE, LANE)] = src_ref[j, pl.ds(q * used, used), :]
 
@@ -164,7 +165,7 @@
     used = wire_rows // pieces
 
     def tile(i, carry):
-        _gather_tile(i, used, x_ref, rows_in)
+        _gather_tile(i, used, x_ref, rows_in, FFN_GROUP)
         rows = rows_in[...]
         gate_act = jnp.dot(rows, gate_ref[...], preferred_element_type=jnp.float32)
         up_act = jnp.dot(rows, up_ref[...], preferred_element_type=jnp.float32)
@@ -172,15 +173,15 @@
         rows_out[...] = jnp.dot(
             inner_act, down_ref[...], preferred_element_type=jnp.float32
         ).astype(rows_out.dtype)
-        for jl in range(GROUP):
-            j = i * GROUP + jl
+        for jl in range(FFN_GROUP):
+            j = i * FFN_GROUP + jl
             for q in range(pieces):
                 out_ref[j, pl.ds(q * used, used), :] = rows_out[
                     pl.ds(jl * used, used), pl.ds(q * LANE, LANE)
                 ]
         return carry
 
-    lax.fori_loop(0, chunks // GROUP, tile, 0)
+    lax.fori_loop(0, chunks // FFN_GROUP, tile, 0)
 
 
 def expert_block(arrived, gate_weights, up_weights, down_weights):
@@ -193,8 +194,8 @@
         in_specs=[pl.BlockSpec(memory_space=pltpu.VMEM)] * 4,
         out_specs=pl.BlockSpec(memory_space=pltpu.VMEM),
         scratch_shapes=[
-            pltpu.VMEM((GROUP * used, width), jnp.bfloat16),
-            pltpu.VMEM((GROUP * used, width), jnp.bfloat16),
+            pltpu.VMEM((FFN_GROUP * used, width), jnp.bfloat16),
+            pltpu.VMEM((FFN_GROUP * used, width), jnp.bfloat16),
         ],
         compiler_params=pltpu.CompilerParams(vmem_limit_bytes=60 * 1024 * 1024),
     )(arrived, gate_weights[0], up_weights[0], down_weights[0])

time: 256 us -> 255 us (level)
  no operation moved by 1% of the time
where the time goes in v11:
time: 255 us
  blocking collectives  95 us (37%)
  waiting for transfers between devices  85.3 us (33%)
  Pallas kernels  53.6 us (21%)
  other arithmetic  8.37 us (3%)
  starting transfers between devices  6.11 us (2%)
  local copies, waits for them, and re-layouts  5.84 us (2%)
    all_to_all x1, blocking collectives, body(): lax.all_to_all(outgoing, ('kv', 'blk'), split_axis=0, concat_axis=0, tile...  95 us
    all_to_all x1, waiting for transfers between devices, body(): lax.all_to_all(processed, ('kv', 'blk'), split_axis=0, concat_axis=0, til...  85.3 us
    pallas_call x1, Pallas kernels, expert_block(): pl.pallas_call(expert_kernel, out_shape=jax.ShapeDtypeStruct(arrived.shap...  27 us
    pallas_call x1, Pallas kernels, attend_reduce(): pl.pallas_call(lambda *refs: attend_reduce_kernel(n_kv, *refs), out_shape...  11.9 us
    pallas_call x1, Pallas kernels, combine(): pl.pallas_call(combine_kernel, out_shape=jax.ShapeDtypeStruct(hidden.shap...  7.57 us
    pallas_call x1, Pallas kernels, dispatch(): pl.pallas_call(lambda *refs: dispatch_kernel(used, *refs), out_shape=jax....  7.15 us
    all_to_all x1, starting transfers between devices, body(): lax.all_to_all(processed, ('kv', 'blk'), split_axis=0, concat_axis=0, til...  6.11 us
  transfers between devices with their start and end apart: 1, of which 1 were waited for; matrix products, arithmetic and copies ran while one was open for 2% of the time, Pallas kernels for 0%

profile of v11, /device:TPU:2, one launch (start us, length us, event | category | flops | bytes accessed | tf_op | source)
XLA Modules:
  0.0 254.7 jit_solution(3546313976501490009)
XLA Ops:
  0.0 0.0 copy-start
  0.0 0.8 copy.36
  0.8 0.3 iota_compare_fusion.1
  1.1 0.2 reduce_window_sum.11
  1.3 2.1 select_reduce_fusion.2
  3.4 0.1 copy.37
  3.4 0.7 add_bitcast_fusion.refs_0_
  4.2 0.7 copy.49
  4.9 0.7 subtract_bitcast_fusion
  5.6 0.1 copy.38.refs_3_
  5.7 0.7 copy.39.refs_4_
  6.4 0.0 copy-start.1
  6.4 2.2 copy-done.1
  8.6 0.0 copy-start.4
  8.6 0.0 copy-start.2
  8.6 0.0 copy-start.3
  8.6 11.9 %shard_map.136 = f32[1,2048]{1,0:T(1,128)S(1)} custom-call(bf16[4,8,128]{2,1,0:T(8,128)(2,1)S(1)} %bitcast.25, bf16[4,4096,128]{2,1,0:T(8,128)(2,1)S(1)} %bitcast.24, bf16[4,4096,128]{2,1,0:T(8,128)(2,1)} %bitcast.26, s32[4,1]{1,0:T(4,128)S(1)} %copy.38.refs_3_, f32[8,1]{1,0:T(8,128)S(1)} %copy.39.refs_4_, bf16[1024,2048]{1,0:T(8,128)(2,1)} %refs_5_.1), custom_call_target="tpu_custom_call" | custom-call | tf_op jit(solution)/shard_map/pallas_call | solution.py:81
  20.6 0.0 copy-done.4
  20.6 0.0 copy-done.2
  20.6 0.3 fusion
  20.9 0.0 copy-done.3
  20.9 0.2 fusion.2.refs_1_
  21.1 7.2 %shard_map.137 = bf16[128,112,256]{2,1,0:T(8,128)(2,1)} custom-call(s32[8,112]{1,0:T(8,128)S(1)} %add_bitcast_fusion.refs_0_, bf16[112,2048]{1,0:T(8,128)(2,1)S(1)} %fusion.2.refs_1_), custom_call_target="tpu_custom_call" | custom-call | tf_op jit(solution)/shard_map/pallas_call | solution.py:143
  28.2 95.0 %all_to_all.10.x_ref = bf16[128,112,256]{2,1,0:T(8,128)(2,1)} all-to-all(bf16[128,112,256]{2,1,0:T(8,128)(2,1)} %shard_map.137), channel_id=1, replica_groups=mesh['kv'=4,'blk'=32] {'kv','blk'}, dimensions={0} | all-to-all | bytes 14680064 | tf_op jit(solution)/shard_map/all_to_all | solution.py:297
  123.2 27.0 %shard_map.138 = bf16[128,112,256]{2,1,0:T(8,128)(2,1)} custom-call(bf16[128,112,256]{2,1,0:T(8,128)(2,1)} %all_to_all.10.x_ref, bf16[2048,768]{1,0:T(8,128)(2,1)} %bitcast.27, bf16[2048,768]{1,0:T(8,128)(2,1)} %bitcast.28, bf16[768,2048]{1,0:T(8,128)(2,1)} %bitcast.29), custom_call_target="tpu_custom_call" | custom-call | tf_op jit(solution)/shard_map/pallas_call | solution.py:191
  150.2 6.1 %all-to-all-start.1 = ((bf16[128,112,256]{2,1,0:T(8,128)(2,1)}), bf16[128,112,256]{2,1,0:T(8,128)(2,1)}, u32[]{:S(2)}, u32[]{:S(2)}) async-start(bf16[128,112,256]{2,1,0:T(8,128)(2,1)} %shard_map.138), calls=%async_computation.1 | async-start | bytes 14680064 | tf_op jit(solution)/shard_map/all_to_all | solution.py:299
  156.3 0.0 copy-done
  156.3 0.3 fusion.6
  156.6 0.3 select_reduce_fusion.1
  156.9 0.1 copy.41
  157.0 0.1 reduce_max.9
  157.2 0.1 copy.42
  157.3 0.1 iota_compare_fusion
  157.4 3.1 %select_reduce_fusion = f32[112,128,14]{1,2,0:T(8,128)S(1)} fusion(f32[112,8]{1,0:T(8,128)S(1)} %copy.42, pred[112,8,14]{1,2,0:T(8,128)(4,1)S(1)} %iota_compare_fusion, pred[112,8,128]{2,1,0:T(8,128)(4,1)S(1)} %get-tuple-element.9), kind=kLoop, calls=%fused_computation | loop fusion | flops 4616192 | bytes 933632 | tf_op jit(solution)/shard_map/reduce_sum | solution.py:300
  160.5 0.7 copy.43
  161.1 0.1 reshape.85
  161.2 0.3 copy.44
  161.6 0.1 subtract_convert_fusion
  161.7 0.2 maximum_bitcast_fusion.mix_ref
  161.8 85.3 %all-to-all-done.1.ret_ref = bf16[128,112,256]{2,1,0:T(8,128)(2,1)} async-done(((bf16[128,112,256]{2,1,0:T(8,128)(2,1)}), bf16[128,112,256]{2,1,0:T(8,128)(2,1)}, u32[]{:S(2)}, u32[]{:S(2)}) %all-to-all-start.1) | async-done | bytes 7340064 | tf_op jit(solution)/shard_map/all_to_all | solution.py:299
  247.2 7.6 %shard_map.139 = bf16[112,2048]{1,0:T(8,128)(2,1)} custom-call(bf16[128,112,256]{2,1,0:T(8,128)(2,1)} %all-to-all-done.1.ret_ref, bf16[8,224,224]{2,1,0:T(8,128)(2,1)S(1)} %maximum_bitcast_fusion.mix_ref, bf16[112,2048]{1,0:T(8,128)(2,1)S(1)} %get-tuple-element.8.hidden_ref), custom_call_target="tpu_custom_call" | custom-call | tf_op jit(solution)/shard_map/pallas_call | solution.py:227
  (6 shorter events, 0.1 us)
Async XLA Ops:
  0.0 156.3 %copy-start = (bf16[2048,128]{1,0:T(8,128)(2,1)S(1)}, bf16[2048,128]{1,0:T(8,128)(2,1)}, u32[]{:S(2)}) copy-start(bf16[2048,128]{1,0:T(8,128)(2,1)} %param.23) | copy-start | bytes 1572868
  6.4 2.2 copy-start.1
  8.6 12.0 %copy-start.4 = (bf16[1,2048]{1,0:T(2,128)(2,1)S(1)}, bf16[1,2048]{1,0:T(2,128)(2,1)}, u32[]{:S(2)}) copy-start(bf16[1,2048]{1,0:T(2,128)(2,1)} %param.20) | copy-start | bytes 12292
  8.6 12.0 %copy-start.2 = (bf16[1,111,2048]{2,1,0:T(8,128)(2,1)S(1)}, bf16[1,111,2048]{2,1,0:T(8,128)(2,1)}, u32[]{:S(2)}) copy-start(bf16[1,111,2048]{2,1,0:T(8,128)(2,1)} %param.21) | copy-start | bytes 1363972
  8.6 12.3 %copy-start.3 = (f32[2048]{0:T(1024)S(1)}, f32[2048]{0:T(1024)}, u32[]{:S(2)}) copy-start(f32[2048]{0:T(1024)} %param.22) | copy-start | bytes 24580
  150.2 97.0 %all-to-all-start.1 = ((bf16[128,112,256]{2,1,0:T(8,128)(2,1)}), bf16[128,112,256]{2,1,0:T(8,128)(2,1)}, u32[]{:S(2)}, u32[]{:S(2)}) async-start(bf16[128,112,256]{2,1,0:T(8,128)(2,1)} %shard_map.138), calls=%async_computation.1 | async-start | bytes 14680064 | tf_op jit(solution)/shard_map/all_to_all | solution.py:299

commit v12 on v11

--- a/solution.py
+++ b/solution.py
@@ -104,7 +104,7 @@
 
 
 LANE = 256
-GROUP = 16
+GROUP = 32
 FFN_GROUP = 64
 
 

time: 255 us -> 254 us (level)
  no operation moved by 1% of the time
where the time goes in v12:
time: 254 us; the launch traced here: 253 us
  blocking collectives  95 us (37%)
  waiting for transfers between devices  85.3 us (34%)
  Pallas kernels  52.3 us (21%)
  other arithmetic  8.35 us (3%)
  starting transfers between devices  6 us (2%)
  local copies, waits for them, and re-layouts  5.84 us (2%)
    all_to_all x1, blocking collectives, body(): lax.all_to_all(outgoing, ('kv', 'blk'), split_axis=0, concat_axis=0, tile...  95 us
    all_to_all x1, waiting for transfers between devices, body(): lax.all_to_all(processed, ('kv', 'blk'), split_axis=0, concat_axis=0, til...  85.3 us
    pallas_call x1, Pallas kernels, expert_block(): pl.pallas_call(expert_kernel, out_shape=jax.ShapeDtypeStruct(arrived.shap...  27 us
    pallas_call x1, Pallas kernels, attend_reduce(): pl.pallas_call(lambda *refs: attend_reduce_kernel(n_kv, *refs), out_shape...  11.9 us
    pallas_call x1, Pallas kernels, combine(): pl.pallas_call(combine_kernel, out_shape=jax.ShapeDtypeStruct(hidden.shap...  6.82 us
    pallas_call x1, Pallas kernels, dispatch(): pl.pallas_call(lambda *refs: dispatch_kernel(used, *refs), out_shape=jax....  6.53 us
    all_to_all x1, starting transfers between devices, body(): lax.all_to_all(processed, ('kv', 'blk'), split_axis=0, concat_axis=0, til...  6 us
  transfers between devices with their start and end apart: 1, of which 1 were waited for; matrix products, arithmetic and copies ran while one was open for 2% of the time, Pallas kernels for 0%

profile of v12, /device:TPU:2, one launch (start us, length us, event | category | flops | bytes accessed | tf_op | source)
XLA Modules:
  0.0 253.2 jit_solution(13547429632850238182)
XLA Ops:
  0.0 0.0 copy-start
  0.0 0.8 copy.36
  0.8 0.3 iota_compare_fusion.1
  1.1 0.2 reduce_window_sum.11
  1.3 2.1 select_reduce_fusion.2
  3.4 0.1 copy.37
  3.4 0.7 add_bitcast_fusion.refs_0_
  4.2 0.7 copy.49
  4.9 0.7 subtract_bitcast_fusion
  5.6 0.1 copy.38.refs_3_
  5.7 0.7 copy.39.refs_4_
  6.4 0.0 copy-start.1
  6.4 2.2 copy-done.1
  8.6 0.0 copy-start.4
  8.6 0.0 copy-start.2
  8.6 0.0 copy-start.3
  8.6 11.9 %shard_map.136 = f32[1,2048]{1,0:T(1,128)S(1)} custom-call(bf16[4,8,128]{2,1,0:T(8,128)(2,1)S(1)} %bitcast.25, bf16[4,4096,128]{2,1,0:T(8,128)(2,1)S(1)} %bitcast.24, bf16[4,4096,128]{2,1,0:T(8,128)(2,1)} %bitcast.26, s32[4,1]{1,0:T(4,128)S(1)} %copy.38.refs_3_, f32[8,1]{1,0:T(8,128)S(1)} %copy.39.refs_4_, bf16[1024,2048]{1,0:T(8,128)(2,1)} %refs_5_.1), custom_call_target="tpu_custom_call" | custom-call | tf_op jit(solution)/shard_map/pallas_call | solution.py:81
  20.6 0.0 copy-done.4
  20.6 0.0 copy-done.2
  20.6 0.3 fusion
  20.9 0.0 copy-done.3
  20.9 0.2 fusion.2.refs_1_
  21.1 6.5 %shard_map.137 = bf16[128,112,256]{2,1,0:T(8,128)(2,1)} custom-call(s32[8,112]{1,0:T(8,128)S(1)} %add_bitcast_fusion.refs_0_, bf16[112,2048]{1,0:T(8,128)(2,1)S(1)} %fusion.2.refs_1_), custom_call_target="tpu_custom_call" | custom-call | tf_op jit(solution)/shard_map/pallas_call | solution.py:143
  27.6 95.0 %all_to_all.10.x_ref = bf16[128,112,256]{2,1,0:T(8,128)(2,1)} all-to-all(bf16[128,112,256]{2,1,0:T(8,128)(2,1)} %shard_map.137), channel_id=1, replica_groups=mesh['kv'=4,'blk'=32] {'kv','blk'}, dimensions={0} | all-to-all | bytes 14680064 | tf_op jit(solution)/shard_map/all_to_all | solution.py:297
  122.6 27.0 %shard_map.138 = bf16[128,112,256]{2,1,0:T(8,128)(2,1)} custom-call(bf16[128,112,256]{2,1,0:T(8,128)(2,1)} %all_to_all.10.x_ref, bf16[2048,768]{1,0:T(8,128)(2,1)} %bitcast.27, bf16[2048,768]{1,0:T(8,128)(2,1)} %bitcast.28, bf16[768,2048]{1,0:T(8,128)(2,1)} %bitcast.29), custom_call_target="tpu_custom_call" | custom-call | tf_op jit(solution)/shard_map/pallas_call | solution.py:191
  149.6 6.0 %all-to-all-start.1 = ((bf16[128,112,256]{2,1,0:T(8,128)(2,1)}), bf16[128,112,256]{2,1,0:T(8,128)(2,1)}, u32[]{:S(2)}, u32[]{:S(2)}) async-start(bf16[128,112,256]{2,1,0:T(8,128)(2,1)} %shard_map.138), calls=%async_computation.1 | async-start | bytes 14680064 | tf_op jit(solution)/shard_map/all_to_all | solution.py:299
  155.6 0.0 copy-done
  155.6 0.3 fusion.6
  155.9 0.3 select_reduce_fusion.1
  156.2 0.1 copy.41
  156.2 0.1 reduce_max.9
  156.4 0.1 copy.42
  156.5 0.1 iota_compare_fusion
  156.7 3.1 %select_reduce_fusion = f32[112,128,14]{1,2,0:T(8,128)S(1)} fusion(f32[112,8]{1,0:T(8,128)S(1)} %copy.42, pred[112,8,14]{1,2,0:T(8,128)(4,1)S(1)} %iota_compare_fusion, pred[112,8,128]{2,1,0:T(8,128)(4,1)S(1)} %get-tuple-element.9), kind=kLoop, calls=%fused_computation | loop fusion | flops 4616192 | bytes 933632 | tf_op jit(solution)/shard_map/reduce_sum | solution.py:300
  159.7 0.7 copy.43
  160.4 0.1 reshape.85
  160.5 0.3 copy.44
  160.8 0.1 subtract_convert_fusion
  161.0 0.1 maximum_bitcast_fusion.mix_ref
  161.1 85.3 %all-to-all-done.1.ret_ref = bf16[128,112,256]{2,1,0:T(8,128)(2,1)} async-done(((bf16[128,112,256]{2,1,0:T(8,128)(2,1)}), bf16[128,112,256]{2,1,0:T(8,128)(2,1)}, u32[]{:S(2)}, u32[]{:S(2)}) %all-to-all-start.1) | async-done | bytes 7340064 | tf_op jit(solution)/shard_map/all_to_all | solution.py:299
  246.4 6.8 %shard_map.139 = bf16[112,2048]{1,0:T(8,128)(2,1)} custom-call(bf16[128,112,256]{2,1,0:T(8,128)(2,1)} %all-to-all-done.1.ret_ref, bf16[4,224,448]{2,1,0:T(8,128)(2,1)S(1)} %maximum_bitcast_fusion.mix_ref, bf16[112,2048]{1,0:T(8,128)(2,1)S(1)} %get-tuple-element.8.hidden_ref), custom_call_target="tpu_custom_call" | custom-call | tf_op jit(solution)/shard_map/pallas_call | solution.py:227
  (6 shorter events, 0.1 us)
Async XLA Ops:
  0.0 155.6 %copy-start = (bf16[2048,128]{1,0:T(8,128)(2,1)S(1)}, bf16[2048,128]{1,0:T(8,128)(2,1)}, u32[]{:S(2)}) copy-start(bf16[2048,128]{1,0:T(8,128)(2,1)} %param.23) | copy-start | bytes 1572868
  6.4 2.2 copy-start.1
  8.6 12.0 %copy-start.4 = (bf16[1,2048]{1,0:T(2,128)(2,1)S(1)}, bf16[1,2048]{1,0:T(2,128)(2,1)}, u32[]{:S(2)}) copy-start(bf16[1,2048]{1,0:T(2,128)(2,1)} %param.20) | copy-start | bytes 12292
  8.6 12.0 %copy-start.2 = (bf16[1,111,2048]{2,1,0:T(8,128)(2,1)S(1)}, bf16[1,111,2048]{2,1,0:T(8,128)(2,1)}, u32[]{:S(2)}) copy-start(bf16[1,111,2048]{2,1,0:T(8,128)(2,1)} %param.21) | copy-start | bytes 1363972
  8.6 12.3 %copy-start.3 = (f32[2048]{0:T(1024)S(1)}, f32[2048]{0:T(1024)}, u32[]{:S(2)}) copy-start(f32[2048]{0:T(1024)} %param.22) | copy-start | bytes 24580
  149.6 96.8 %all-to-all-start.1 = ((bf16[128,112,256]{2,1,0:T(8,128)(2,1)}), bf16[128,112,256]{2,1,0:T(8,128)(2,1)}, u32[]{:S(2)}, u32[]{:S(2)}) async-start(bf16[128,112,256]{2,1,0:T(8,128)(2,1)} %shard_map.138), calls=%async_computation.1 | async-start | bytes 14680064 | tf_op jit(solution)/shard_map/all_to_all | solution.py:299

commit v13 on v12

--- a/solution.py
+++ b/solution.py
@@ -104,7 +104,7 @@
 
 
 LANE = 256
-GROUP = 32
+GROUP = 64
 FFN_GROUP = 64
 
 

time: 254 us -> 253 us (level)
  no operation moved by 1% of the time
where the time goes in v13:
time: 253 us
  blocking collectives  95 us (38%)
  waiting for transfers between devices  85.4 us (34%)
  Pallas kernels  51.6 us (20%)
  other arithmetic  8.25 us (3%)
  starting transfers between devices  6 us (2%)
  local copies, waits for them, and re-layouts  5.8 us (2%)
    all_to_all x1, blocking collectives, body(): lax.all_to_all(outgoing, ('kv', 'blk'), split_axis=0, concat_axis=0, tile...  95 us
    all_to_all x1, waiting for transfers between devices, body(): lax.all_to_all(processed, ('kv', 'blk'), split_axis=0, concat_axis=0, til...  85.4 us
    pallas_call x1, Pallas kernels, expert_block(): pl.pallas_call(expert_kernel, out_shape=jax.ShapeDtypeStruct(arrived.shap...  27 us
    pallas_call x1, Pallas kernels, attend_reduce(): pl.pallas_call(lambda *refs: attend_reduce_kernel(n_kv, *refs), out_shape...  11.9 us
    pallas_call x1, Pallas kernels, combine(): pl.pallas_call(combine_kernel, out_shape=jax.ShapeDtypeStruct(hidden.shap...  6.46 us
    pallas_call x1, Pallas kernels, dispatch(): pl.pallas_call(lambda *refs: dispatch_kernel(used, *refs), out_shape=jax....  6.26 us
    all_to_all x1, starting transfers between devices, body(): lax.all_to_all(processed, ('kv', 'blk'), split_axis=0, concat_axis=0, til...  6 us
  transfers between devices with their start and end apart: 1, of which 1 were waited for; matrix products, arithmetic and copies ran while one was open for 2% of the time, Pallas kernels for 0%

profile of v13, /device:TPU:2, one launch (start us, length us, event | category | flops | bytes accessed | tf_op | source)
XLA Modules:
  0.0 252.6 jit_solution(14447184194785222721)
XLA Ops:
  0.0 0.0 copy-start
  0.0 0.8 copy.36
  0.8 0.3 iota_compare_fusion.1
  1.1 0.2 reduce_window_sum.11
  1.3 2.1 select_reduce_fusion.2
  3.4 0.1 copy.37
  3.4 0.7 add_bitcast_fusion.refs_0_
  4.2 0.7 copy.49
  4.9 0.7 subtract_bitcast_fusion
  5.6 0.1 copy.38.refs_3_
  5.7 0.7 copy.39.refs_4_
  6.4 0.0 copy-start.1
  6.4 2.2 copy-done.1
  8.6 0.0 copy-start.4
  8.6 0.0 copy-start.2
  8.6 0.0 copy-start.3
  8.6 11.9 %shard_map.136 = f32[1,2048]{1,0:T(1,128)S(1)} custom-call(bf16[4,8,128]{2,1,0:T(8,128)(2,1)S(1)} %bitcast.25, bf16[4,4096,128]{2,1,0:T(8,128)(2,1)S(1)} %bitcast.24, bf16[4,4096,128]{2,1,0:T(8,128)(2,1)} %bitcast.26, s32[4,1]{1,0:T(4,128)S(1)} %copy.38.refs_3_, f32[8,1]{1,0:T(8,128)S(1)} %copy.39.refs_4_, bf16[1024,2048]{1,0:T(8,128)(2,1)} %refs_5_.1), custom_call_target="tpu_custom_call" | custom-call | tf_op jit(solution)/shard_map/pallas_call | solution.py:81
  20.6 0.0 copy-done.4
  20.6 0.0 copy-done.2
  20.6 0.3 fusion
  20.9 0.0 copy-done.3
  20.9 0.2 fusion.2.refs_1_
  21.1 6.3 %shard_map.137 = bf16[128,112,256]{2,1,0:T(8,128)(2,1)} custom-call(s32[8,112]{1,0:T(8,128)S(1)} %add_bitcast_fusion.refs_0_, bf16[112,2048]{1,0:T(8,128)(2,1)S(1)} %fusion.2.refs_1_), custom_call_target="tpu_custom_call" | custom-call | tf_op jit(solution)/shard_map/pallas_call | solution.py:143
  27.3 95.0 %all_to_all.10.x_ref = bf16[128,112,256]{2,1,0:T(8,128)(2,1)} all-to-all(bf16[128,112,256]{2,1,0:T(8,128)(2,1)} %shard_map.137), channel_id=1, replica_groups=mesh['kv'=4,'blk'=32] {'kv','blk'}, dimensions={0} | all-to-all | bytes 14680064 | tf_op jit(solution)/shard_map/all_to_all | solution.py:297
  122.3 27.0 %shard_map.138 = bf16[128,112,256]{2,1,0:T(8,128)(2,1)} custom-call(bf16[128,112,256]{2,1,0:T(8,128)(2,1)} %all_to_all.10.x_ref, bf16[2048,768]{1,0:T(8,128)(2,1)} %bitcast.27, bf16[2048,768]{1,0:T(8,128)(2,1)} %bitcast.28, bf16[768,2048]{1,0:T(8,128)(2,1)} %bitcast.29), custom_call_target="tpu_custom_call" | custom-call | tf_op jit(solution)/shard_map/pallas_call | solution.py:191
  149.3 6.0 %all-to-all-start.1 = ((bf16[128,112,256]{2,1,0:T(8,128)(2,1)}), bf16[128,112,256]{2,1,0:T(8,128)(2,1)}, u32[]{:S(2)}, u32[]{:S(2)}) async-start(bf16[128,112,256]{2,1,0:T(8,128)(2,1)} %shard_map.138), calls=%async_computation.1 | async-start | bytes 14680064 | tf_op jit(solution)/shard_map/all_to_all | solution.py:299
  155.3 0.0 copy-done
  155.3 0.3 fusion.6
  155.6 0.3 select_reduce_fusion.1
  155.9 0.1 copy.41
  156.0 0.1 reduce_max.9
  156.1 0.1 copy.42
  156.2 0.1 iota_compare_fusion
  156.4 3.1 %select_reduce_fusion = f32[112,128,14]{1,2,0:T(8,128)S(1)} fusion(f32[112,8]{1,0:T(8,128)S(1)} %copy.42, pred[112,8,14]{1,2,0:T(8,128)(4,1)S(1)} %iota_compare_fusion, pred[112,8,128]{2,1,0:T(8,128)(4,1)S(1)} %get-tuple-element.9), kind=kLoop, calls=%fused_computation | loop fusion | flops 4616192 | bytes 933632 | tf_op jit(solution)/shard_map/reduce_sum | solution.py:300
  159.5 0.7 copy.43
  160.1 0.1 reshape.85
  160.2 0.3 copy.44
  160.5 0.1 subtract_convert_fusion
  160.6 0.1 maximum_bitcast_fusion.mix_ref
  160.7 85.4 %all-to-all-done.1.ret_ref = bf16[128,112,256]{2,1,0:T(8,128)(2,1)} async-done(((bf16[128,112,256]{2,1,0:T(8,128)(2,1)}), bf16[128,112,256]{2,1,0:T(8,128)(2,1)}, u32[]{:S(2)}, u32[]{:S(2)}) %all-to-all-start.1) | async-done | bytes 7340064 | tf_op jit(solution)/shard_map/all_to_all | solution.py:299
  246.1 6.5 %shard_map.139 = bf16[112,2048]{1,0:T(8,128)(2,1)} custom-call(bf16[128,112,256]{2,1,0:T(8,128)(2,1)} %all-to-all-done.1.ret_ref, bf16[2,224,896]{2,1,0:T(8,128)(2,1)S(1)} %maximum_bitcast_fusion.mix_ref, bf16[112,2048]{1,0:T(8,128)(2,1)S(1)} %get-tuple-element.8.hidden_ref), custom_call_target="tpu_custom_call" | custom-call | tf_op jit(solution)/shard_map/pallas_call | solution.py:227
  (6 shorter events, 0.1 us)
Async XLA Ops:
  0.0 155.3 %copy-start = (bf16[2048,128]{1,0:T(8,128)(2,1)S(1)}, bf16[2048,128]{1,0:T(8,128)(2,1)}, u32[]{:S(2)}) copy-start(bf16[2048,128]{1,0:T(8,128)(2,1)} %param.23) | copy-start | bytes 1572868
  6.4 2.2 copy-start.1
  8.6 12.0 %copy-start.4 = (bf16[1,2048]{1,0:T(2,128)(2,1)S(1)}, bf16[1,2048]{1,0:T(2,128)(2,1)}, u32[]{:S(2)}) copy-start(bf16[1,2048]{1,0:T(2,128)(2,1)} %param.20) | copy-start | bytes 12292
  8.6 12.0 %copy-start.2 = (bf16[1,111,2048]{2,1,0:T(8,128)(2,1)S(1)}, bf16[1,111,2048]{2,1,0:T(8,128)(2,1)}, u32[]{:S(2)}) copy-start(bf16[1,111,2048]{2,1,0:T(8,128)(2,1)} %param.21) | copy-start | bytes 1363972
  8.6 12.3 %copy-start.3 = (f32[2048]{0:T(1024)S(1)}, f32[2048]{0:T(1024)}, u32[]{:S(2)}) copy-start(f32[2048]{0:T(1024)} %param.22) | copy-start | bytes 24580
  149.3 96.8 %all-to-all-start.1 = ((bf16[128,112,256]{2,1,0:T(8,128)(2,1)}), bf16[128,112,256]{2,1,0:T(8,128)(2,1)}, u32[]{:S(2)}, u32[]{:S(2)}) async-start(bf16[128,112,256]{2,1,0:T(8,128)(2,1)} %shard_map.138), calls=%async_computation.1 | async-start | bytes 14680064 | tf_op jit(solution)/shard_map/all_to_all | solution.py:299

commit v14 on v13

--- a/solution.py
+++ b/solution.py
@@ -13,7 +13,8 @@
 
 
 def attend_reduce_kernel(
-    n_kv, q_ref, k_ref, v_ref, first_ref, sink_ref, proj_ref, out_ref, att, part, held, send_sem, recv_sem
+    n_kv, q_ref, k_hbm, v_hbm, first_ref, sink_ref, proj_ref, out_ref, att, part, held, send_sem, recv_sem,
+    k_ref, v_ref, load_sem
 ):
     me = lax.axis_index("kv")
     blk = lax.axis_index("blk")
@@ -23,10 +24,21 @@
         pl.semaphore_signal(barrier, inc=1, device_id=(peer, blk), device_id_type=MESH)
     requests, heads, head_dim = q_ref.shape
     window = k_ref.shape[1]
+    loads = []
+    for r in range(requests):
+        pair = (
+            pltpu.make_async_copy(k_hbm.at[r], k_ref.at[r], load_sem.at[0, r]),
+            pltpu.make_async_copy(v_hbm.at[r], v_ref.at[r], load_sem.at[1, r]),
+        )
+        pair[0].start()
+        pair[1].start()
+        loads.append(pair)
     scale = 1.0 / math.sqrt(head_dim)
     sink = sink_ref[...]
     positions = lax.broadcasted_iota(jnp.int32, (heads, window), 1)
     for r in range(requests):
+        loads[r][0].wait()
+        loads[r][1].wait()
         scores = lax.dot_general(
             q_ref[r], k_ref[r], (((1,), (1,)), ((), ())), preferred_element_type=jnp.float32
         ) * scale
@@ -81,7 +93,9 @@
     return pl.pallas_call(
         lambda *refs: attend_reduce_kernel(n_kv, *refs),
         out_shape=jax.ShapeDtypeStruct((1, width), jnp.float32),
-        in_specs=[pl.BlockSpec(memory_space=pltpu.VMEM)] * 6,
+        in_specs=[pl.BlockSpec(memory_space=pltpu.VMEM)]
+        + [pl.BlockSpec(memory_space=pl.ANY)] * 2
+        + [pl.BlockSpec(memory_space=pltpu.VMEM)] * 3,
         out_specs=pl.BlockSpec(memory_space=pltpu.VMEM),
         scratch_shapes=[
             pltpu.VMEM((requests, heads * head_dim), jnp.bfloat16),
@@ -89,6 +103,9 @@
             pltpu.VMEM((n_kv, 1, width), jnp.float32),
             pltpu.SemaphoreType.DMA((n_kv,)),
             pltpu.SemaphoreType.DMA((n_kv,)),
+            pltpu.VMEM(keys.shape, keys.dtype),
+            pltpu.VMEM(values.shape, values.dtype),
+            pltpu.SemaphoreType.DMA((2, requests)),
         ],
         compiler_params=pltpu.CompilerParams(
             collective_id=0, has_side_effects=True, vmem_limit_bytes=48 * 1024 * 1024

time: 253 us -> 253 us (level)
  no operation moved by 1% of the time
where the time goes in v14:
time: 253 us
  blocking collectives  95 us (38%)
  waiting for transfers between devices  85.4 us (34%)
  Pallas kernels  52.1 us (21%)
  other arithmetic  8.25 us (3%)
  starting transfers between devices  6 us (2%)
  local copies, waits for them, and re-layouts  5.8 us (2%)
    all_to_all x1, blocking collectives, body(): lax.all_to_all(outgoing, ('kv', 'blk'), split_axis=0, concat_axis=0, tile...  95 us
    all_to_all x1, waiting for transfers between devices, body(): lax.all_to_all(processed, ('kv', 'blk'), split_axis=0, concat_axis=0, til...  85.4 us
    pallas_call x1, Pallas kernels, expert_block(): pl.pallas_call(expert_kernel, out_shape=jax.ShapeDtypeStruct(arrived.shap...  27 us
    pallas_call x1, Pallas kernels, attend_reduce(): pl.pallas_call(lambda *refs: attend_reduce_kernel(n_kv, *refs), out_shape...  12.4 us
    pallas_call x1, Pallas kernels, combine(): pl.pallas_call(combine_kernel, out_shape=jax.ShapeDtypeStruct(hidden.shap...  6.46 us
    pallas_call x1, Pallas kernels, dispatch(): pl.pallas_call(lambda *refs: dispatch_kernel(used, *refs), out_shape=jax....  6.26 us
    all_to_all x1, starting transfers between devices, body(): lax.all_to_all(processed, ('kv', 'blk'), split_axis=0, concat_axis=0, til...  6 us
  transfers between devices with their start and end apart: 1, of which 1 were waited for; matrix products, arithmetic and copies ran while one was open for 2% of the time, Pallas kernels for 0%

profile of v14, /device:TPU:2, one launch (start us, length us, event | category | flops | bytes accessed | tf_op | source)
XLA Modules:
  0.0 253.0 jit_solution(8458290731993928978)
XLA Ops:
  0.0 0.0 copy-start
  0.0 0.8 copy.36
  0.8 0.3 iota_compare_fusion.1
  1.1 0.2 reduce_window_sum.11
  1.3 2.1 select_reduce_fusion.2
  3.4 0.1 copy.37
  3.4 0.7 add_bitcast_fusion.refs_0_
  4.2 0.7 copy.49
  4.9 0.7 subtract_bitcast_fusion
  5.6 0.1 copy.38.refs_3_
  5.7 0.7 copy.39.refs_4_
  6.4 0.0 copy-start.1
  6.4 2.2 copy-done.1
  8.6 0.0 copy-start.4
  8.6 0.0 copy-start.2
  8.6 0.0 copy-start.3
  8.6 12.4 %shard_map.136 = f32[1,2048]{1,0:T(1,128)S(1)} custom-call(bf16[4,8,128]{2,1,0:T(8,128)(2,1)S(1)} %bitcast.25, bf16[4,4096,128]{2,1,0:T(8,128)(2,1)S(1)} %bitcast.24, bf16[4,4096,128]{2,1,0:T(8,128)(2,1)} %bitcast.26, s32[4,1]{1,0:T(4,128)S(1)} %copy.38.refs_3_, f32[8,1]{1,0:T(8,128)S(1)} %copy.39.refs_4_, bf16[1024,2048]{1,0:T(8,128)(2,1)} %refs_5_.1), custom_call_target="tpu_custom_call" | custom-call | tf_op jit(solution)/shard_map/pallas_call | solution.py:93
  21.0 0.0 copy-done.4
  21.1 0.0 copy-done.2
  21.1 0.3 fusion
  21.3 0.0 copy-done.3
  21.3 0.2 fusion.2.refs_1_
  21.5 6.3 %shard_map.137 = bf16[128,112,256]{2,1,0:T(8,128)(2,1)} custom-call(s32[8,112]{1,0:T(8,128)S(1)} %add_bitcast_fusion.refs_0_, bf16[112,2048]{1,0:T(8,128)(2,1)S(1)} %fusion.2.refs_1_), custom_call_target="tpu_custom_call" | custom-call | tf_op jit(solution)/shard_map/pallas_call | solution.py:160
  27.8 95.0 %all_to_all.10.x_ref = bf16[128,112,256]{2,1,0:T(8,128)(2,1)} all-to-all(bf16[128,112,256]{2,1,0:T(8,128)(2,1)} %shard_map.137), channel_id=1, replica_groups=mesh['kv'=4,'blk'=32] {'kv','blk'}, dimensions={0} | all-to-all | bytes 14680064 | tf_op jit(solution)/shard_map/all_to_all | solution.py:314
  122.8 27.0 %shard_map.138 = bf16[128,112,256]{2,1,0:T(8,128)(2,1)} custom-call(bf16[128,112,256]{2,1,0:T(8,128)(2,1)} %all_to_all.10.x_ref, bf16[2048,768]{1,0:T(8,128)(2,1)} %bitcast.27, bf16[2048,768]{1,0:T(8,128)(2,1)} %bitcast.28, bf16[768,2048]{1,0:T(8,128)(2,1)} %bitcast.29), custom_call_target="tpu_custom_call" | custom-call | tf_op jit(solution)/shard_map/pallas_call | solution.py:208
  149.7 6.0 %all-to-all-start.1 = ((bf16[128,112,256]{2,1,0:T(8,128)(2,1)}), bf16[128,112,256]{2,1,0:T(8,128)(2,1)}, u32[]{:S(2)}, u32[]{:S(2)}) async-start(bf16[128,112,256]{2,1,0:T(8,128)(2,1)} %shard_map.138), calls=%async_computation.1 | async-start | bytes 14680064 | tf_op jit(solution)/shard_map/all_to_all | solution.py:316
  155.8 0.0 copy-done
  155.8 0.3 fusion.6
  156.1 0.3 select_reduce_fusion.1
  156.4 0.1 copy.41
  156.4 0.1 reduce_max.9
  156.6 0.1 copy.42
  156.7 0.1 iota_compare_fusion
  156.8 3.1 %select_reduce_fusion = f32[112,128,14]{1,2,0:T(8,128)S(1)} fusion(f32[112,8]{1,0:T(8,128)S(1)} %copy.42, pred[112,8,14]{1,2,0:T(8,128)(4,1)S(1)} %iota_compare_fusion, pred[112,8,128]{2,1,0:T(8,128)(4,1)S(1)} %get-tuple-element.9), kind=kLoop, calls=%fused_computation | loop fusion | flops 4616192 | bytes 933632 | tf_op jit(solution)/shard_map/reduce_sum | solution.py:317
  159.9 0.7 copy.43
  160.6 0.1 reshape.85
  160.7 0.3 copy.44
  161.0 0.1 subtract_convert_fusion
  161.1 0.1 maximum_bitcast_fusion.mix_ref
  161.1 85.4 %all-to-all-done.1.ret_ref = bf16[128,112,256]{2,1,0:T(8,128)(2,1)} async-done(((bf16[128,112,256]{2,1,0:T(8,128)(2,1)}), bf16[128,112,256]{2,1,0:T(8,128)(2,1)}, u32[]{:S(2)}, u32[]{:S(2)}) %all-to-all-start.1) | async-done | bytes 7340064 | tf_op jit(solution)/shard_map/all_to_all | solution.py:316
  246.6 6.5 %shard_map.139 = bf16[112,2048]{1,0:T(8,128)(2,1)} custom-call(bf16[128,112,256]{2,1,0:T(8,128)(2,1)} %all-to-all-done.1.ret_ref, bf16[2,224,896]{2,1,0:T(8,128)(2,1)S(1)} %maximum_bitcast_fusion.mix_ref, bf16[112,2048]{1,0:T(8,128)(2,1)S(1)} %get-tuple-element.8.hidden_ref), custom_call_target="tpu_custom_call" | custom-call | tf_op jit(solution)/shard_map/pallas_call | solution.py:244
  (6 shorter events, 0.1 us)
Async XLA Ops:
  0.0 155.8 %copy-start = (bf16[2048,128]{1,0:T(8,128)(2,1)S(1)}, bf16[2048,128]{1,0:T(8,128)(2,1)}, u32[]{:S(2)}) copy-start(bf16[2048,128]{1,0:T(8,128)(2,1)} %param.23) | copy-start | bytes 1572868
  6.4 2.2 copy-start.1
  8.6 12.4 %copy-start.4 = (bf16[1,2048]{1,0:T(2,128)(2,1)S(1)}, bf16[1,2048]{1,0:T(2,128)(2,1)}, u32[]{:S(2)}) copy-start(bf16[1,2048]{1,0:T(2,128)(2,1)} %param.20) | copy-start | bytes 12292
  8.6 12.5 %copy-start.2 = (bf16[1,111,2048]{2,1,0:T(8,128)(2,1)S(1)}, bf16[1,111,2048]{2,1,0:T(8,128)(2,1)}, u32[]{:S(2)}) copy-start(bf16[1,111,2048]{2,1,0:T(8,128)(2,1)} %param.21) | copy-start | bytes 1363972
  8.6 12.7 %copy-start.3 = (f32[2048]{0:T(1024)S(1)}, f32[2048]{0:T(1024)}, u32[]{:S(2)}) copy-start(f32[2048]{0:T(1024)} %param.22) | copy-start | bytes 24580
  149.7 96.8 %all-to-all-start.1 = ((bf16[128,112,256]{2,1,0:T(8,128)(2,1)}), bf16[128,112,256]{2,1,0:T(8,128)(2,1)}, u32[]{:S(2)}, u32[]{:S(2)}) async-start(bf16[128,112,256]{2,1,0:T(8,128)(2,1)} %shard_map.138), calls=%async_computation.1 | async-start | bytes 14680064 | tf_op jit(solution)/shard_map/all_to_all | solution.py:316

commit v15 on v13

--- a/solution.py
+++ b/solution.py
@@ -105,7 +105,7 @@
 
 LANE = 256
 GROUP = 64
-FFN_GROUP = 64
+FFN_GROUP = 128
 
 
 def _wire_shape(width, used):

time: 253 us -> 254 us (level)
  no operation moved by 1% of the time
where the time goes in v15:
time: 254 us; the launch traced here: 253 us
  blocking collectives  95 us (37%)
  waiting for transfers between devices  85.4 us (34%)
  Pallas kernels  52.2 us (21%)
  other arithmetic  8.25 us (3%)
  starting transfers between devices  6 us (2%)
  local copies, waits for them, and re-layouts  5.8 us (2%)
    all_to_all x1, blocking collectives, body(): lax.all_to_all(outgoing, ('kv', 'blk'), split_axis=0, concat_axis=0, tile...  95 us
    all_to_all x1, waiting for transfers between devices, body(): lax.all_to_all(processed, ('kv', 'blk'), split_axis=0, concat_axis=0, til...  85.4 us
    pallas_call x1, Pallas kernels, expert_block(): pl.pallas_call(expert_kernel, out_shape=jax.ShapeDtypeStruct(arrived.shap...  27.5 us
    pallas_call x1, Pallas kernels, attend_reduce(): pl.pallas_call(lambda *refs: attend_reduce_kernel(n_kv, *refs), out_shape...  11.9 us
    pallas_call x1, Pallas kernels, combine(): pl.pallas_call(combine_kernel, out_shape=jax.ShapeDtypeStruct(hidden.shap...  6.46 us
    pallas_call x1, Pallas kernels, dispatch(): pl.pallas_call(lambda *refs: dispatch_kernel(used, *refs), out_shape=jax....  6.26 us
    all_to_all x1, starting transfers between devices, body(): lax.all_to_all(processed, ('kv', 'blk'), split_axis=0, concat_axis=0, til...  6 us
  transfers between devices with their start and end apart: 1, of which 1 were waited for; matrix products, arithmetic and copies ran while one was open for 2% of the time, Pallas kernels for 0%

profile of v15, /device:TPU:2, one launch (start us, length us, event | category | flops | bytes accessed | tf_op | source)
XLA Modules:
  0.0 253.1 jit_solution(200173679730405198)
XLA Ops:
  0.0 0.0 copy-start
  0.0 0.8 copy.36
  0.8 0.3 iota_compare_fusion.1
  1.1 0.2 reduce_window_sum.11
  1.3 2.1 select_reduce_fusion.2
  3.4 0.1 copy.37
  3.4 0.7 add_bitcast_fusion.refs_0_
  4.2 0.7 copy.49
  4.9 0.7 subtract_bitcast_fusion
  5.6 0.1 copy.38.refs_3_
  5.7 0.7 copy.39.refs_4_
  6.4 0.0 copy-start.1
  6.4 2.2 copy-done.1
  8.6 0.0 copy-start.4
  8.6 0.0 copy-start.2
  8.6 0.0 copy-start.3
  8.6 11.9 %shard_map.136 = f32[1,2048]{1,0:T(1,128)S(1)} custom-call(bf16[4,8,128]{2,1,0:T(8,128)(2,1)S(1)} %bitcast.25, bf16[4,4096,128]{2,1,0:T(8,128)(2,1)S(1)} %bitcast.24, bf16[4,4096,128]{2,1,0:T(8,128)(2,1)} %bitcast.26, s32[4,1]{1,0:T(4,128)S(1)} %copy.38.refs_3_, f32[8,1]{1,0:T(8,128)S(1)} %copy.39.refs_4_, bf16[1024,2048]{1,0:T(8,128)(2,1)} %refs_5_.1), custom_call_target="tpu_custom_call" | custom-call | tf_op jit(solution)/shard_map/pallas_call | solution.py:81
  20.6 0.0 copy-done.4
  20.6 0.0 copy-done.2
  20.6 0.3 fusion
  20.9 0.0 copy-done.3
  20.9 0.2 fusion.2.refs_1_
  21.1 6.3 %shard_map.137 = bf16[128,112,256]{2,1,0:T(8,128)(2,1)} custom-call(s32[8,112]{1,0:T(8,128)S(1)} %add_bitcast_fusion.refs_0_, bf16[112,2048]{1,0:T(8,128)(2,1)S(1)} %fusion.2.refs_1_), custom_call_target="tpu_custom_call" | custom-call | tf_op jit(solution)/shard_map/pallas_call | solution.py:143
  27.3 95.0 %all_to_all.10.x_ref = bf16[128,112,256]{2,1,0:T(8,128)(2,1)} all-to-all(bf16[128,112,256]{2,1,0:T(8,128)(2,1)} %shard_map.137), channel_id=1, replica_groups=mesh['kv'=4,'blk'=32] {'kv','blk'}, dimensions={0} | all-to-all | bytes 14680064 | tf_op jit(solution)/shard_map/all_to_all | solution.py:297
  122.3 27.5 %shard_map.138 = bf16[128,112,256]{2,1,0:T(8,128)(2,1)} custom-call(bf16[128,112,256]{2,1,0:T(8,128)(2,1)} %all_to_all.10.x_ref, bf16[2048,768]{1,0:T(8,128)(2,1)} %bitcast.27, bf16[2048,768]{1,0:T(8,128)(2,1)} %bitcast.28, bf16[768,2048]{1,0:T(8,128)(2,1)} %bitcast.29), custom_call_target="tpu_custom_call" | custom-call | tf_op jit(solution)/shard_map/pallas_call | solution.py:191
  149.8 6.0 %all-to-all-start.1 = ((bf16[128,112,256]{2,1,0:T(8,128)(2,1)}), bf16[128,112,256]{2,1,0:T(8,128)(2,1)}, u32[]{:S(2)}, u32[]{:S(2)}) async-start(bf16[128,112,256]{2,1,0:T(8,128)(2,1)} %shard_map.138), calls=%async_computation.1 | async-start | bytes 14680064 | tf_op jit(solution)/shard_map/all_to_all | solution.py:299
  155.8 0.0 copy-done
  155.8 0.3 fusion.6
  156.1 0.3 select_reduce_fusion.1
  156.5 0.1 copy.41
  156.5 0.1 reduce_max.9
  156.7 0.1 copy.42
  156.8 0.1 iota_compare_fusion
  156.9 3.1 %select_reduce_fusion = f32[112,128,14]{1,2,0:T(8,128)S(1)} fusion(f32[112,8]{1,0:T(8,128)S(1)} %copy.42, pred[112,8,14]{1,2,0:T(8,128)(4,1)S(1)} %iota_compare_fusion, pred[112,8,128]{2,1,0:T(8,128)(4,1)S(1)} %get-tuple-element.9), kind=kLoop, calls=%fused_computation | loop fusion | flops 4616192 | bytes 933632 | tf_op jit(solution)/shard_map/reduce_sum | solution.py:300
  160.0 0.7 copy.43
  160.7 0.1 reshape.85
  160.8 0.3 copy.44
  161.1 0.1 subtract_convert_fusion
  161.1 0.1 maximum_bitcast_fusion.mix_ref
  161.2 85.4 %all-to-all-done.1.ret_ref = bf16[128,112,256]{2,1,0:T(8,128)(2,1)} async-done(((bf16[128,112,256]{2,1,0:T(8,128)(2,1)}), bf16[128,112,256]{2,1,0:T(8,128)(2,1)}, u32[]{:S(2)}, u32[]{:S(2)}) %all-to-all-start.1) | async-done | bytes 7340064 | tf_op jit(solution)/shard_map/all_to_all | solution.py:299
  246.6 6.5 %shard_map.139 = bf16[112,2048]{1,0:T(8,128)(2,1)} custom-call(bf16[128,112,256]{2,1,0:T(8,128)(2,1)} %all-to-all-done.1.ret_ref, bf16[2,224,896]{2,1,0:T(8,128)(2,1)S(1)} %maximum_bitcast_fusion.mix_ref, bf16[112,2048]{1,0:T(8,128)(2,1)S(1)} %get-tuple-element.8.hidden_ref), custom_call_target="tpu_custom_call" | custom-call | tf_op jit(solution)/shard_map/pallas_call | solution.py:227
  (6 shorter events, 0.1 us)
Async XLA Ops:
  0.0 155.8 %copy-start = (bf16[2048,128]{1,0:T(8,128)(2,1)S(1)}, bf16[2048,128]{1,0:T(8,128)(2,1)}, u32[]{:S(2)}) copy-start(bf16[2048,128]{1,0:T(8,128)(2,1)} %param.23) | copy-start | bytes 1572868
  6.4 2.2 copy-start.1
  8.6 12.0 %copy-start.4 = (bf16[1,2048]{1,0:T(2,128)(2,1)S(1)}, bf16[1,2048]{1,0:T(2,128)(2,1)}, u32[]{:S(2)}) copy-start(bf16[1,2048]{1,0:T(2,128)(2,1)} %param.20) | copy-start | bytes 12292
  8.6 12.0 %copy-start.2 = (bf16[1,111,2048]{2,1,0:T(8,128)(2,1)S(1)}, bf16[1,111,2048]{2,1,0:T(8,128)(2,1)}, u32[]{:S(2)}) copy-start(bf16[1,111,2048]{2,1,0:T(8,128)(2,1)} %param.21) | copy-start | bytes 1363972
  8.6 12.3 %copy-start.3 = (f32[2048]{0:T(1024)S(1)}, f32[2048]{0:T(1024)}, u32[]{:S(2)}) copy-start(f32[2048]{0:T(1024)} %param.22) | copy-start | bytes 24580
  149.8 96.8 %all-to-all-start.1 = ((bf16[128,112,256]{2,1,0:T(8,128)(2,1)}), bf16[128,112,256]{2,1,0:T(8,128)(2,1)}, u32[]{:S(2)}, u32[]{:S(2)}) async-start(bf16[128,112,256]{2,1,0:T(8,128)(2,1)} %shard_map.138), calls=%async_computation.1 | async-start | bytes 14680064 | tf_op jit(solution)/shard_map/all_to_all | solution.py:299
